TPU v7x, 32 devices: a whole 2x2x4 slice. The times are simulated.
32 devices in a mesh: elem: 8 (over z, x), crm: 4 (over y, core).
Axes of the slice: x: 2, y: 2, z: 4, core: 2. Of those that a mesh axis runs over, the one named last changes fastest.
Arguments:
- state: float32 [128, 64, 320], P('elem', 'crm'), may hold values from -6 to 6
- wind: float32 [128, 64, 128], P('elem', 'crm'), may hold values from -0.15 to 0.15
- dyn_mix: bfloat16 [320, 320], replicated, may hold values from -0.15625 to 0.15625
- owner: int32 [512, 1], P(('elem', 'crm')), may hold values from 0 to 3; in each aligned block of 16 rows (0 to 15, 16 to 31, ...) at most 4 rows name the same one
- crm_state: bfloat16 [512, 32, 320], P(('elem', 'crm')), may hold values from -6 to 6
- crm_mix: bfloat16 [320, 320], replicated, may hold values from -0.3125 to 0.3125
Outputs:
- dyn_state: float32 [128, 64, 320], P('elem', 'crm')
- crm_next: bfloat16 [512, 32, 320], P(('elem', 'crm'))
Inputs may be any that keep to these rules, and one draw needn't show every extreme that they name: Within the 16 columns of one device (an aligned block) no owner is named more than 4 times, a bound that some block reaches.
All inputs are finite; a program needn't handle non-finite values.
Results may differ from a plain program's by a relative error of at most 0.0021.
Values sent between devices are 32-bit elements; how exact they have to be, the bound alone decides.
No kernel may reach another device: no remote copies, remote signals or barrier semaphores. Data moves between devices by JAX's collectives and lax.ppermute only.
A program may use at most 64 MiB of HBM per device.

v0:
```python
import functools

import jax
import jax.numpy as jnp
import numpy as np
from jax import lax
from jax.experimental import pallas as pl
from jax.experimental.pallas import tpu as pltpu
from jax.sharding import PartitionSpec as P


SUB = 4
HIGHEST = lax.Precision.HIGHEST
CRM_STEP = 0.5
DIFFUSION = 0.2
COUPLING = 0.5
NODES = 4


def gll_derivative():
    points = np.array([-1.0, -1.0 / np.sqrt(5.0), 1.0 / np.sqrt(5.0), 1.0])
    barycentric = np.array(
        [
            1.0 / np.prod([points[i] - points[j] for j in range(NODES) if j != i])
            for i in range(NODES)
        ]
    )
    derivative = np.zeros((NODES, NODES))
    for i in range(NODES):
        for j in range(NODES):
            if j != i:
                derivative[i, j] = barycentric[j] / barycentric[i] / (points[i] - points[j])
        derivative[i, i] = -np.sum(derivative[i])
    return derivative


DERIV = [[float(value) for value in row] for row in gll_derivative().astype(np.float32)]
FIRST, LAST = DERIV[0][0], DERIV[3][3]
QUADRATURE = np.array([1.0, 5.0, 5.0, 1.0]) / 6.0


def lane_tiles(channels, width):
    return [(at, min(at + width, channels)) for at in range(0, channels, width)]


def winds(pair, levels):
    along_x, along_y = pair[:, :levels], pair[:, levels:]
    return (
        jnp.concatenate([along_x, along_x], axis=1),
        jnp.concatenate([along_y, along_y], axis=1),
    )


def full_winds(pair, levels, channels):
    along_x, along_y = winds(pair, levels)
    count = -(-channels // (2 * levels))
    return (
        jnp.concatenate([along_x] * count, axis=1)[:, :channels],
        jnp.concatenate([along_y] * count, axis=1)[:, :channels],
    )


def dx_rows(rows):
    out = []
    for i in range(NODES):
        total = None
        for j in range(NODES):
            if DERIV[i][j] != 0.0 and not (i == j and abs(DERIV[i][j]) < 1e-6):
                term = DERIV[i][j] * rows[j]
                total = term if total is None else total + term
        out.append(total)
    return out


def sublane_coefficients(rows, width):
    position = lax.broadcasted_iota(jnp.int32, (rows, width), 0) & 3
    table = []
    for shift in range(-3, 4):
        value = jnp.zeros((rows, width), jnp.float32)
        for at in range(NODES):
            if 0 <= at + shift < NODES:
                value = jnp.where(position == at, DERIV[at][at + shift], value)
        table.append(value)
    return table


def dsub(field, table):
    width = field.shape[1]
    blocks = []
    for at in range(0, field.shape[0], 8):
        part = field[at : at + 8]
        total = None
        for index, shift in enumerate(range(-3, 4)):
            moved = part if shift == 0 else pltpu.roll(part, (-shift) % 8, 0)
            term = table[index][:, :width] * moved
            total = term if total is None else total + term
        blocks.append(total)
    return blocks[0] if len(blocks) == 1 else jnp.concatenate(blocks, axis=0)


def sub_average(field):
    rows = field.shape[0]
    position = lax.broadcasted_iota(jnp.int32, field.shape, 0)
    phase = position & 3
    upper = (phase == 3) & (position < rows - 1)
    lower = (phase == 0) & (position > 0)
    ahead = pltpu.roll(field, rows - 1, 0)
    behind = pltpu.roll(field, 1, 0)
    partner = jnp.where(upper, ahead, jnp.where(lower, behind, field))
    return 0.5 * (field + partner)


def average_rows(ref, size_x, size_y):
    for at in range(NODES - 1, size_x - 1, NODES):
        low, high = pl.ds(at * size_y, size_y), pl.ds((at + 1) * size_y, size_y)
        mean = 0.5 * (ref[low, :] + ref[high, :])
        ref[low, :] = mean
        ref[high, :] = mean


def end_rows(rows, first, last):
    shape = (rows, first.shape[1])
    position = lax.broadcasted_iota(jnp.int32, shape, 0)
    return jnp.where(position == 0, first, jnp.where(position == rows - 1, last, 0.0))


def edge_rows(rows, first, last):
    position = lax.broadcasted_iota(jnp.int32, rows.shape, 0)
    count = rows.shape[0]
    return rows + jnp.where(
        position == 0, first, jnp.where(position == count - 1, last, 0.0)
    )


def local_update(base_ref, field_ref, mixed_ref, wind_ref, out_ref, size_x, size_y, levels, average):
    channels = field_ref.shape[1]
    table = sublane_coefficients(8, 2 * levels)
    for element in range(size_x // NODES):
        rows = [pl.ds((NODES * element + i) * size_y, size_y) for i in range(NODES)]
        wind = [winds(wind_ref[row, :], levels) for row in rows]
        for begin, end in lane_tiles(channels, 2 * levels):
            width = end - begin
            values = [field_ref[row, begin:end] for row in rows]
            slopes = dx_rows(values)
            for i in range(NODES):
                along_x, along_y = wind[i][0][:, :width], wind[i][1][:, :width]
                result = (
                    base_ref[rows[i], begin:end]
                    + mixed_ref[rows[i], begin:end]
                    - (along_x * slopes[i] + along_y * dsub(values[i], table))
                )
                out_ref[rows[i], begin:end] = sub_average(result) if average else result


def to_bf16(value):
    return value.astype(jnp.bfloat16)


def mix_all(field, mix):
    return jnp.dot(to_bf16(field), mix, preferred_element_type=jnp.float32)


def column_of(ref, y, size_x, size_y):
    return jnp.concatenate(
        [ref[x * size_y + y : x * size_y + y + 1, :] for x in range(size_x)], axis=0
    )


def column_parts(message, channels, levels):
    return (
        message[:, 0:channels],
        message[:, channels : 2 * channels],
        message[:, 2 * channels : 3 * channels],
        message[:, 3 * channels : 3 * channels + 2 * levels],
    )


def is_even(rank):
    return (rank[0] & 1) == 0


def begin_kernel(size_x, size_y, levels, rank, state_in, wind_in, mix_in, partial, to_a, to_b,
                 state, wind, mix, mixed, message, arrivals):
    channels = state.shape[1]
    copies = [
        pltpu.make_async_copy(source, target, arrivals.at[index])
        for index, (source, target) in enumerate(
            ((state_in, state), (mix_in, mix), (wind_in, wind))
        )
    ]
    for copy in copies:
        copy.start()
    copies[0].wait()
    copies[1].wait()
    mixed[...] = mix_all(state[...], mix[...])
    copies[2].wait()
    local_update(state, state, mixed, wind, partial, size_x, size_y, levels, True)
    average_rows(partial, size_x, size_y)
    to_left, to_right = message.at[0], message.at[1]
    for out, column, near, row in ((to_left, 0, 0, 0), (to_right, size_y - 1, size_y - NODES, 3)):
        values = [column_of(partial, near + j, size_x, size_y) for j in range(NODES)]
        slope = None
        for j in range(NODES):
            term = DERIV[row][j] * values[j]
            slope = term if slope is None else slope + term
        out[:, 0:channels] = values[row]
        out[:, channels : 2 * channels] = slope
        out[:, 2 * channels : 3 * channels] = column_of(state, column, size_x, size_y)
        out[:, 3 * channels : 3 * channels + 2 * levels] = column_of(wind, column, size_x, size_y)
    even = is_even(rank)
    to_a[...] = jnp.where(even, message[1], message[0])
    to_b[...] = jnp.where(even, message[0], message[1])


def in_order(rank, from_a, from_b):
    even = is_even(rank)
    first, second = from_a[...], from_b[...]
    return jnp.where(even, second, first), jnp.where(even, first, second)


def side_changes(size_x, size_y, partial, from_left, from_right):
    channels = partial.shape[1]
    return (
        0.5 * (from_left[0:size_x, 0:channels] - column_of(partial, 0, size_x, size_y)),
        0.5 * (from_right[0:size_x, 0:channels] - column_of(partial, size_y - 1, size_x, size_y)),
    )


def turn_kernel(size_x, size_y, levels, rank, place, partial, state, wind, from_a, from_b,
                to_a, to_b, line, message):
    channels = state.shape[1]
    from_left, from_right = in_order(rank, from_a, from_b)
    to_up, to_down = message.at[0], message.at[1]
    left_value, left_slope, left_state, left_wind = column_parts(from_left, channels, levels)
    right_value, right_slope, right_state, right_wind = column_parts(from_right, channels, levels)
    span = 2 * channels + 2 * levels
    pieces = span // (2 * levels)
    for out, x, near, kind in ((to_up, 0, 0, 0), (to_down, size_x - 1, size_x - NODES, 3)):
        slope = None
        for j in range(NODES):
            value = partial[pl.ds((near + j) * size_y, size_y), :]
            at = near + j
            left = 0.5 * (left_value[at : at + 1] - value[0:1])
            right = 0.5 * (right_value[at : at + 1] - value[size_y - 1 : size_y])
            value = edge_rows(value, left, right)
            if at == x:
                out[:, 0:channels] = value
                changes = (left, right)
            term = DERIV[kind][j] * value
            slope = term if slope is None else slope + term
        row = pl.ds(x * size_y, size_y)
        along_x, _ = full_winds(wind[row, :], levels, channels)
        out[:, channels : 2 * channels] = state[row, :] - along_x * slope
        out[:, 2 * channels : span] = wind[row, :]
        corners = (
            (left_slope[x : x + 1] - LAST * changes[0], left_state, left_wind, slope[0:1]),
            (
                right_slope[x : x + 1] - FIRST * changes[1],
                right_state,
                right_wind,
                slope[size_y - 1 : size_y],
            ),
        )
        for side, (side_slope, side_state, side_wind, corner_slope) in enumerate(corners):
            pair = side_wind[x : x + 1]
            corner_x, _ = full_winds(pair, levels, channels)
            line[side : side + 1, 0:channels] = side_slope
            line[side : side + 1, channels : 2 * channels] = (
                side_state[x : x + 1] - corner_x * corner_slope
            )
            line[side : side + 1, 2 * channels : span] = pair
            for piece in range(pieces):
                at = side * pieces + piece
                out[at : at + 1, span : span + 2 * levels] = line[
                    side : side + 1, piece * 2 * levels : (piece + 1) * 2 * levels
                ]
        used = 2 * pieces
        if used < size_y:
            out[used:size_y, span : span + 2 * levels] = jnp.zeros(
                (size_y - used, 2 * levels), jnp.float32
            )
    even = is_even(place)
    to_a[...] = jnp.where(even, message[1], message[0])
    to_b[...] = jnp.where(even, message[0], message[1])


def ready_kernel(size_x, size_y, levels, capacity, rank, owner, partial, state, wind, mix,
                 from_a, from_b, field, mixed, total, sides, onehot):
    channels = state.shape[1]
    from_left, from_right = in_order(rank, from_a, from_b)
    shape = onehot.shape
    parts = 8 // capacity
    lanes = lax.broadcasted_iota(jnp.int32, shape, 1) >> 2
    named = jnp.zeros(shape, jnp.int32)
    for c in range(owner.shape[0]):
        named = jnp.where(lanes == c, owner[c], named)
    position = jnp.zeros(shape, jnp.int32)
    for c in range(owner.shape[0]):
        position = position + jnp.where((lanes > c) & (named == owner[c]), 1, 0)
    offset = rank[0] ^ named
    slot = (offset * capacity + position) * parts
    rows = lax.broadcasted_iota(jnp.int32, shape, 0)
    onehot[...] = jnp.where((rows >= slot) & (rows < slot + parts), 1.0, 0.0)
    left, right = side_changes(size_x, size_y, partial, from_left, from_right)
    for x in range(size_x):
        row = pl.ds(x * size_y, size_y)
        field[row, :] = edge_rows(partial[row, :], left[x : x + 1], right[x : x + 1])
    mixed[...] = mix_all(field[...], mix[...])
    local_update(state, field, mixed, wind, total, size_x, size_y, levels, True)
    table = sublane_coefficients(8, channels)
    for side, (message, y, change, factor) in enumerate(
        ((from_left, 0, left, LAST), (from_right, size_y - 1, right, FIRST))
    ):
        _, slope, side_state, side_wind = column_parts(message, channels, levels)
        slope = slope - factor * change
        along_x, along_y = full_winds(side_wind, levels, channels)
        beyond = (
            side_state
            + column_of(mixed, y, size_x, size_y)
            - (
                along_x * dsub(column_of(field, y, size_x, size_y), table)
                + along_y * slope
            )
        )
        sides[side, 0] = beyond
        sides[side, 1] = slope
        sides[side, 2] = along_x
        sides[side, 3] = along_y


def part_roll(value, parts, by):
    by = by % parts
    if by == 0:
        return value
    part = lax.broadcasted_iota(jnp.int32, value.shape, 0) & (parts - 1)
    return jnp.where(
        part < parts - by, pltpu.roll(value, 8 - by, 0), pltpu.roll(value, parts - by, 0)
    )


def part_sum(value, parts):
    total = value
    for by in range(1, parts):
        total = total + part_roll(value, parts, by)
    return total


def packing(rows, channels):
    full, rest = channels // 128, channels % 128
    assert rest in (0, 64)
    return full, rest, full * rows + (rows // 2 if rest else 0)


def pack(tile, channels, out, rows):
    full, rest, _ = packing(rows, channels)
    count = rows // 8
    for t in range(count):
        for lane in range(full):
            out[lane * rows + 8 * t : lane * rows + 8 * t + 8, :] = tile(t, lane)
    if rest:
        for t in range(count // 2):
            out[full * rows + 8 * t : full * rows + 8 * t + 8, :] = jnp.concatenate(
                [tile(t, full)[:, :rest], tile(t + count // 2, full)[:, :rest]], axis=1
            )


def unpack(message, channels, out, start, rows):
    full, rest, _ = packing(rows, channels)
    for lane in range(full):
        out[start : start + rows, lane * 128 : lane * 128 + 128] = message[
            lane * rows : (lane + 1) * rows, :
        ]
    if rest:
        half = rows // 2
        tail = message[full * rows : full * rows + half, :]
        out[start : start + half, full * 128 : channels] = tail[:, :rest]
        out[start + half : start + rows, full * 128 : channels] = tail[:, rest:]


def interleave(states, start, channels, turned, rows):
    for lane, (begin, end) in enumerate(lane_tiles(channels, 128)):
        turned[lane, 0:rows, 0 : end - begin] = states[pl.ds(start, rows), begin:end].astype(
            jnp.float32
        )

    def tile(t, lane):
        return turned[lane, pl.ds(t, 8, stride=rows // 8), :]

    return tile


def widen_kernel(groups, rank, states, *refs):
    own, near = refs[:2]
    pairs = refs[2 : 1 + groups // 2]
    turned = refs[-1]
    rows, channels = own.shape
    length = near.shape[0]
    for k in range(groups):
        start = pl.multiple_of((rank[0] ^ k) * rows, rows)
        tile = interleave(states, start, channels, turned.at[k], rows)
        if k == 0:
            for t in range(rows // 8):
                for lane, (begin, end) in enumerate(lane_tiles(channels, 128)):
                    own[8 * t : 8 * t + 8, begin:end] = tile(t, lane)[:, : end - begin]
        elif k == 1:
            pack(tile, channels, near, rows)
        else:
            at = (k & 1) * length
            pack(tile, channels, pairs[k // 2 - 1].at[at : at + length], rows)


def cloud_run(states, forcing, mix, rows, parts, tendency, finals):
    blocks = states.shape[0] // rows
    count = rows // 8
    columns = count * parts
    means, totals = {}, {}
    for step in range(SUB):
        last = step == SUB - 1
        for begin in range(0, blocks, 2):
            group = range(begin, min(begin + 2, blocks))
            mixed = mix_all(states[begin * rows : (group[-1] + 1) * rows, :], mix[...])
            for block in group:
                push = forcing[8 * block : 8 * block + 8, :]

                def read(t):
                    at = block * rows + 8 * t
                    return states[at : at + 8, :]

                if step == 0:
                    total = read(0)
                    for t in range(1, count):
                        total = total + read(t)
                    means[block] = part_sum(total, parts) * (1.0 / columns)
                gain = CRM_STEP * (push - means[block])
                keep = not last or block in finals
                total = None
                if keep:
                    start = read(0)
                    behind, here = part_roll(read(count - 1), parts, -1), start
                for t in range(count):
                    at = (block - begin) * rows + 8 * t
                    turn = jnp.tanh(mixed[at : at + 8])
                    total = turn if total is None else total + turn
                    if keep:
                        ahead = read(t + 1) if t + 1 < count else part_roll(start, parts, 1)
                        states[block * rows + 8 * t : block * rows + 8 * t + 8, :] = (
                            (1.0 - 2.0 * CRM_STEP * DIFFUSION) * here
                            + CRM_STEP * DIFFUSION * (behind + ahead)
                            + CRM_STEP * turn
                            + gain
                        )
                        behind, here = here, ahead
                if tendency is not None:
                    mean = means[block] + part_sum(total, parts) * (CRM_STEP / columns) + gain
                    totals[block] = mean - push if step == 0 else totals[block] + (mean - push)
                    means[block] = mean
                elif not last:
                    means[block] = (
                        means[block] + part_sum(total, parts) * (CRM_STEP / columns) + gain
                    )
    if tendency is not None:
        for block in range(blocks):
            tendency[8 * block : 8 * block + 8, :] = totals[block] * (1.0 / SUB)


def settle(states, start, used, parts, turned, old, old_start, out, out_start, rows):
    channels = states.shape[1]
    count = rows // 8
    for lane, (begin, end) in enumerate(lane_tiles(channels, 128)):
        width = end - begin
        for t in range(count):
            value = states[start + 8 * t : start + 8 * t + 8, begin:end]
            if width < 128:
                value = jnp.concatenate([value, jnp.zeros((8, 128 - width), jnp.float32)], axis=1)
            turned[lane, pl.ds(t, 8, stride=count), :] = value
        for slot in range(8 // parts):
            at = slot * count * parts
            span = count * parts
            flag = used[slot * parts : slot * parts + 1, :] > 0.5
            before = old[pl.ds(old_start + at, span), begin:end].astype(jnp.float32)
            after = turned[lane, at : at + span, 0:width]
            out[pl.ds(out_start + at, span), begin:end] = jnp.where(flag, after, before).astype(
                jnp.bfloat16
            )


def second_kernel(size_x, size_y, levels, place, field, second, known, sides, onehot, wind, mix,
                  from_a, from_b, work, forcing, mixed, total, reduced):
    from_up, from_down = in_order(place, from_a, from_b)
    channels = field.shape[1]
    span = 2 * channels + 2 * levels
    pieces = span // (2 * levels)
    last_row = pl.ds((size_x - 1) * size_y, size_y)
    first_row = pl.ds(0, size_y)
    small = sublane_coefficients(8, channels)
    ups = 0.5 * (from_up[:, 0:channels] - field[first_row, :])
    downs = 0.5 * (from_down[:, 0:channels] - field[last_row, :])
    remixed = mix_all(
        jnp.concatenate([field[first_row, :] + ups, field[last_row, :] + downs], axis=0), mix[...]
    )
    new_mixed = (remixed[0:size_y], remixed[size_y : 2 * size_y])
    total[...] = second[...]
    edge_mixed = []
    for index, (x, near, end, change) in enumerate(
        ((0, 0, 0, ups), (size_x - 1, size_x - NODES, 3, downs))
    ):
        edge = pl.ds(x * size_y, size_y)
        edge_mixed.append(new_mixed[index] - known[edge, :])
        for i in range(NODES):
            row = pl.ds((near + i) * size_y, size_y)
            along_x, along_y = full_winds(wind[row, :], levels, channels)
            value = -DERIV[i][end] * (along_x * change)
            if near + i == x:
                value = value + edge_mixed[index] - along_y * dsub(change, small)
            total[row, :] = total[row, :] + sub_average(value)
    corner = {}
    for name, message in enumerate((from_up, from_down)):
        for side in range(2):
            line = jnp.concatenate(
                [
                    message[side * pieces + p : side * pieces + p + 1, span : span + 2 * levels]
                    for p in range(pieces)
                ],
                axis=1,
            )
            corner[name, side] = (
                line[:, 0:channels],
                line[:, channels : 2 * channels],
                line[:, 2 * channels : span],
            )
    edge_slopes = {}
    for side, y in ((0, 0), (1, size_y - 1)):
        slope = sides[side, 1]
        pick = slice(y, y + 1)
        new_first = 0.5 * (corner[0, side][0] + slope[0:1])
        new_last = 0.5 * (corner[1, side][0] + slope[size_x - 1 : size_x])
        edge_slopes[0, side], edge_slopes[1, side] = new_first, new_last
        slope_change = end_rows(
            size_x, new_first - slope[0:1], new_last - slope[size_x - 1 : size_x]
        )
        column_change = end_rows(size_x, ups[pick], downs[pick])
        mixed_change = end_rows(size_x, edge_mixed[0][pick], edge_mixed[1][pick])
        beyond = (
            sides[side, 0]
            + mixed_change
            - (sides[side, 2] * dsub(column_change, small) + sides[side, 3] * slope_change)
        )
        for x in range(size_x):
            at = slice(x * size_y + y, x * size_y + y + 1)
            total[at, :] = 0.5 * (total[at, :] + beyond[x : x + 1])
    for name, message, row, change, factor in (
        (0, from_up, first_row, ups, LAST),
        (1, from_down, last_row, downs, FIRST),
    ):
        along_x, along_y = full_winds(message[:, 2 * channels : span], levels, channels)
        beyond = (
            message[:, channels : 2 * channels]
            + new_mixed[name]
            + factor * along_x * change
            - along_y * dsub(field[row, :] + change, small)
        )
        beyond = sub_average(beyond)
        ends = []
        for side, y in ((0, 0), (1, size_y - 1)):
            _, part, pair = corner[name, side]
            corner_x, corner_y = full_winds(pair, levels, channels)
            value = (
                part
                + new_mixed[name][y : y + 1]
                + factor * corner_x * change[y : y + 1]
                - corner_y * edge_slopes[name, side]
            )
            ends.append(0.5 * (value - beyond[y : y + 1]))
        beyond = edge_rows(beyond, ends[0], ends[1])
        total[row, :] = 0.5 * (total[row, :] + beyond)
    average_rows(total, size_x, size_y)
    for element in range(size_x // NODES):
        value = None
        for i in range(NODES):
            term = float(QUADRATURE[i]) * total[pl.ds((NODES * element + i) * size_y, size_y), :]
            value = term if value is None else value + term
        reduced[pl.ds(element * size_y, size_y), :] = value
    phase = lax.broadcasted_iota(jnp.int32, onehot.shape, 1) & 3
    weight = jnp.where(
        (phase == 0) | (phase == 3), float(QUADRATURE[0] / 4.0), float(QUADRATURE[1] / 4.0)
    )
    forcing[...] = jnp.dot(
        onehot[...] * weight, reduced[...], precision=HIGHEST, preferred_element_type=jnp.float32
    )
    mixed[...] = mix_all(total[...], mix[...])
    local_update(total, total, mixed, wind, work, size_x, size_y, levels, False)


def home_kernel(size_x, size_y, groups, capacity, *refs):
    rank, work, forcing, onehot, mix, cloud_mix, own, near, far = refs[:9]
    pairs = refs[9 : 8 + groups // 2]
    out, to_a, to_b, sends, own_final = refs[8 + groups // 2 : 13 + groups // 2]
    reduced, tendency, cloud, message = refs[13 + groups // 2 :]
    channels = work.shape[1]
    parts = 8 // capacity
    rows = own.shape[0]
    length = near.shape[0]
    cloud[0:rows, :] = own[...]
    unpack(near, channels, cloud, rows, rows)
    for m in range(1, groups // 2):
        unpack(pairs[m - 1].at[0:length], channels, cloud, 2 * m * rows, rows)
        unpack(
            far.at[(m - 1) * length : m * length], channels, cloud, (2 * m + 1) * rows, rows
        )
    cloud_run(cloud, forcing, cloud_mix, rows, parts, tendency, (0,))
    own_final[...] = cloud[0:rows, :]
    tend = tendency[...]
    change = COUPLING * (tend + mix_all(tend, mix[...]))
    part = lax.broadcasted_iota(jnp.int32, onehot.shape, 0) & (parts - 1)
    reduced[...] = lax.dot_general(
        jnp.where(part == 0, onehot[...], 0.0),
        change,
        (((0,), (0,)), ((), ())),
        precision=HIGHEST,
        preferred_element_type=jnp.float32,
    )
    for x in range(size_x):
        row = pl.ds(x * size_y, size_y)
        element = pl.ds((x // NODES) * size_y, size_y)
        out[row, :] = sub_average(work[row, :] + reduced[element, :])
    average_rows(out, size_x, size_y)
    occupied = jnp.max(onehot[...], axis=1, keepdims=True)
    sends[:, 0:channels] = forcing[...]
    sends[:, channels : channels + 1] = occupied
    message[0] = column_of(out, 0, size_x, size_y)
    message[1] = column_of(out, size_y - 1, size_x, size_y)
    even = is_even(rank)
    to_a[0:size_x, 0:channels] = jnp.where(even, message[1], message[0])
    to_b[0:size_x, 0:channels] = jnp.where(even, message[0], message[1])
    to_a[size_x : size_x + 8, :] = sends[8:16, :]
    to_b[size_x : size_x + 8, :] = sends[8 * groups - 8 : 8 * groups, :]


def last_turn_kernel(size_x, size_y, rank, place, partial, from_a, from_b, to_a, to_b, ends):
    channels = partial.shape[1]
    from_left, from_right = in_order(rank, from_a, from_b)
    for index, x in enumerate((0, size_x - 1)):
        value = partial[x * size_y : (x + 1) * size_y, :]
        ends[index] = edge_rows(
            value,
            0.5 * (from_left[x : x + 1, 0:channels] - value[0:1]),
            0.5 * (from_right[x : x + 1, 0:channels] - value[size_y - 1 : size_y]),
        )
    even = is_even(place)
    to_a[...] = jnp.where(even, ends[1], ends[0])
    to_b[...] = jnp.where(even, ends[0], ends[1])


def owner_kernel(size_x, size_y, groups, capacity, *refs):
    rank, partial, from_a, from_b, states, mix, own_final, sends, near = refs[:9]
    pairs = refs[9 : 8 + groups // 2]
    forcings = refs[8 + groups // 2 : 7 + groups // 2 + groups]
    fields, out, field, cloud, forcing, turned, ready, done = refs[7 + groups // 2 + groups :]
    channels = partial.shape[1]
    parts = 8 // capacity
    rows = own_final.shape[0]
    length = near.shape[0]
    from_left, from_right = in_order(rank, from_a, from_b)
    left, right = side_changes(size_x, size_y, partial, from_left, from_right)
    for x in range(size_x):
        row = pl.ds(x * size_y, size_y)
        field[row, :] = edge_rows(partial[row, :], left[x : x + 1], right[x : x + 1])
    copies = [pltpu.make_async_copy(field, fields, done.at[groups])]
    copies[0].start()
    unpack(near, channels, cloud, 0, rows)
    forcing[0:8, :] = forcings[0][:, 0:channels]
    for k in range(2, groups):
        at = (k & 1) * length
        unpack(pairs[k // 2 - 1].at[at : at + length], channels, cloud, (k - 1) * rows, rows)
        forcing[8 * (k - 1) : 8 * k, :] = forcings[k - 1][:, 0:channels]
    cloud_run(cloud, forcing, mix, rows, parts, None, tuple(range(groups - 1)))
    for k in range(groups):
        start = pl.multiple_of((rank[0] ^ k) * rows, rows)
        source, at = (cloud, (k - 1) * rows) if k else (own_final, 0)
        flags = (forcings[k - 1] if k else sends)[0:8, channels : channels + 1]
        settle(source, at, flags, parts, turned.at[k], states, start, ready.at[k], 0, rows)
        copy = pltpu.make_async_copy(ready.at[k], out.at[pl.ds(start, rows), :], done.at[k])
        copy.start()
        copies.append(copy)
    for copy in copies:
        copy.wait()


def finish_kernel(size_x, size_y, place, fields_in, mine_a, mine_b, from_a, from_b,
                  fields, rows, done):
    even = is_even(place)
    last = size_x - 1
    copies = []
    for index, (mine, other, x) in enumerate(
        (
            (mine_a, from_a, jnp.where(even, last, 0)),
            (mine_b, from_b, jnp.where(even, 0, last)),
        )
    ):
        rows[index] = 0.5 * (mine[...] + other[...])
        start = pl.multiple_of(x * size_y, size_y)
        copy = pltpu.make_async_copy(
            rows.at[index], fields.at[pl.ds(start, size_y), :], done.at[index]
        )
        copy.start()
        copies.append(copy)
    for copy in copies:
        copy.wait()


VMEM_GRANT = 12 * 2**20
VMEM = pltpu.MemorySpace.VMEM
SMEM = pltpu.MemorySpace.SMEM
DMA = pltpu.SemaphoreType.DMA


def call(kernel, outs, scratch, *args, smem=(), far=(), far_out=(), aliases=None):
    def space(index, remote):
        if index in smem and not remote:
            return pl.BlockSpec(memory_space=SMEM)
        if index in (far_out if remote else far):
            return pl.BlockSpec(memory_space=pltpu.MemorySpace.HBM)
        return pl.BlockSpec(memory_space=VMEM)

    args = [
        pltpu.with_memory_space_constraint(arg, pltpu.MemorySpace.HBM) if index in far else arg
        for index, arg in enumerate(args)
    ]
    return pl.pallas_call(
        kernel,
        out_shape=[jax.ShapeDtypeStruct(shape, dtype) for shape, dtype in outs],
        in_specs=[space(index, False) for index in range(len(args))],
        out_specs=[space(index, True) for index in range(len(outs))],
        scratch_shapes=[
            item if not isinstance(item, tuple) else pltpu.VMEM(*item) for item in scratch
        ],
        input_output_aliases=aliases or {},
        compiler_params=pltpu.CompilerParams(vmem_limit_bytes=VMEM_GRANT),
    )(*args)


def lower_pairs(count):
    return [(i, i ^ 1) for i in range(count)]


def upper_pairs(count):
    return [(i, (i + 1) % count if i & 1 else (i - 1) % count) for i in range(count)]


def ring(to_a, to_b, axis):
    count = lax.axis_size(axis)
    from_b = lax.ppermute(to_b, axis, upper_pairs(count))
    from_a = lax.ppermute(to_a, axis, lower_pairs(count))
    return from_a, from_b


def on_device(state, wind, dyn_mix, owner, crm_state, crm_mix):
    f32 = jnp.float32
    size_x, size_y, channels = state.shape
    levels = wind.shape[2] // 2
    nodes = size_x * size_y
    groups = lax.axis_size("crm")
    slots, columns = crm_state.shape[:2]
    capacity = slots // groups
    rows = capacity * columns
    elements = size_x // NODES
    lane_count = len(lane_tiles(channels, 128))
    rank = lax.axis_index("crm").astype(jnp.int32).reshape(1)
    place = lax.axis_index("elem").astype(jnp.int32).reshape(1)
    state = state.reshape(nodes, channels)
    wind = wind.reshape(nodes, 2 * levels)
    clouds = crm_state.reshape(slots * columns, channels)
    owners = owner.reshape(owner.shape[0])
    grid = ((nodes, channels), f32)
    xor = [[(i, i ^ k) for i in range(groups)] for k in range(groups)]

    column_message = ((size_x, 3 * channels + 2 * levels), f32)
    partial, to_a, to_b = call(
        functools.partial(begin_kernel, size_x, size_y, levels),
        [grid, column_message, column_message],
        [
            grid, ((nodes, 2 * levels), f32), (dyn_mix.shape, dyn_mix.dtype), grid,
            ((2,) + column_message[0], f32), DMA((3,)),
        ],
        rank, state, wind, dyn_mix,
        smem=(0,), far=(1, 2, 3),
    )
    column_a, column_b = ring(to_a, to_b, "crm")

    length = packing(rows, channels)[2]
    own, near, *pairs = call(
        functools.partial(widen_kernel, groups),
        [((rows, channels), f32), ((length, 128), f32)]
        + [((2 * length, 128), f32)] * (groups // 2 - 1),
        [((groups, lane_count, rows, 128), f32)],
        rank, clouds,
        smem=(0,),
    )
    pairs_in = [lax.ppermute(pairs[m - 1], "crm", xor[2 * m]) for m in range(1, groups // 2)]
    near_in = lax.ppermute(near, "crm", xor[1])

    span = 2 * channels + 2 * levels
    row_message = ((size_y, span + 2 * levels), f32)
    to_a, to_b = call(
        functools.partial(turn_kernel, size_x, size_y, levels),
        [row_message, row_message],
        [((8, span), f32), ((2,) + row_message[0], f32)],
        rank, place, partial, state, wind, column_a, column_b,
        smem=(0, 1),
    )
    row_a, row_b = ring(to_a, to_b, "elem")
    field, known, total, sides, onehot = call(
        functools.partial(ready_kernel, size_x, size_y, levels, capacity),
        [
            grid, grid, grid, ((2, 4, size_x, channels), f32),
            ((8 * groups, elements * size_y), f32),
        ],
        [],
        rank, owners, partial, state, wind, dyn_mix, column_a, column_b,
        smem=(0, 1),
    )
    far_in = lax.ppermute(
        jnp.concatenate([value[length:] for value in pairs_in], axis=0), "crm", xor[1]
    )
    work, forcing = call(
        functools.partial(second_kernel, size_x, size_y, levels),
        [grid, ((8 * groups, channels), f32)],
        [grid, grid, ((elements * size_y, channels), f32)],
        place, field, total, known, sides, onehot, wind, dyn_mix, row_a, row_b,
        smem=(0,),
    )
    edge = ((size_x + 8, channels + 1), f32)
    partial, to_a, to_b, sends, own_final = call(
        functools.partial(home_kernel, size_x, size_y, groups, capacity),
        [grid, edge, edge, ((8 * groups, channels + 1), f32), ((rows, channels), f32)],
        [
            ((elements * size_y, channels), f32),
            ((8 * groups, channels), f32),
            ((groups * rows, channels), f32),
            ((2, size_x, channels), f32),
        ],
        rank, work, forcing, onehot, dyn_mix, crm_mix, own, near_in, far_in, *pairs_in,
        smem=(0,),
    )

    column_a, column_b = ring(to_a, to_b, "crm")
    rides = groups - 1 if all(i ^ j == groups - 1 for i, j in upper_pairs(groups)) else 0
    forcings = []
    for k in range(1, groups):
        if k == 1:
            forcings.append(column_a[size_x:])
        elif k == rides:
            forcings.append(column_b[size_x:])
        else:
            forcings.append(lax.ppermute(sends[8 * k : 8 * k + 8], "crm", xor[k]))
    mine_a, mine_b = call(
        functools.partial(last_turn_kernel, size_x, size_y),
        [((size_y, channels), f32)] * 2,
        [((2, size_y, channels), f32)],
        rank, place, partial, column_a, column_b,
        smem=(0, 1),
    )
    row_a, row_b = ring(mine_a, mine_b, "elem")
    fields, crm_next = call(
        functools.partial(owner_kernel, size_x, size_y, groups, capacity),
        [grid, ((slots * columns, channels), clouds.dtype)],
        [
            grid,
            (((groups - 1) * rows, channels), f32),
            ((8 * (groups - 1), channels), f32),
            ((groups, lane_count, rows, 128), f32),
            ((groups, rows, channels), clouds.dtype),
            DMA((groups + 1,)),
        ],
        rank, partial, column_a, column_b, clouds, crm_mix, own_final, sends, near,
        *pairs, *forcings,
        smem=(0,),
        far_out=(0, 1),
    )
    (third,) = call(
        functools.partial(finish_kernel, size_x, size_y),
        [grid],
        [((2, size_y, channels), f32), DMA((2,))],
        place, fields, mine_a, mine_b, row_a, row_b,
        smem=(0,), far=(1,), far_out=(0,), aliases={1: 0},
    )
    return (
        third.reshape(size_x, size_y, channels),
        crm_next.reshape(slots, columns, channels),
    )


def solution(mesh):
    return jax.shard_map(
        on_device,
        mesh=mesh,
        in_specs=(
            P("elem", "crm", None),
            P("elem", "crm", None),
            P(),
            P(("elem", "crm"), None),
            P(("elem", "crm"), None, None),
            P(),
        ),
        out_specs=(P("elem", "crm", None), P(("elem", "crm"), None, None)),
        check_vma=False,
    )
```

profile of v0, /device:TPU:0, one launch (start us, length us, event | category | flops | bytes accessed | tf_op | source)
XLA Modules:
  0.0 45.7 jit_solution(3191938019286402140)
XLA Ops:
  0.6 0.0 copy-start.3
  0.6 1.0 %copy-done.3 = bf16[16,32,320]{2,1,0:T(8,128)(2,1)S(1)} copy-done((bf16[16,32,320]{2,1,0:T(8,128)(2,1)S(1)}, bf16[16,32,320]{2,1,0:T(8,128)(2,1)}, u32[]{:S(2)}) %copy-start.3) | copy-done | bytes 327704
  1.6 0.3 shard_map.81
  1.9 3.1 %collective-permute-start.5 = (f32[640,128]{1,0:T(8,128)S(1)}, f32[640,128]{1,0:T(8,128)S(1)}, u32[]{:S(2)}, u32[]{:S(2)}) collective-permute-start(f32[640,128]{1,0:T(8,128)S(1)} %get-tuple-element.40.refs_9_), channel_id=1, source_target_pairs={{0,2},{1,3},{2,0},{3,1},{4,6},{5,7},{6,4},{7,5},{8,10},{9,11},{10,... | collective-permute-start | bytes 983048 | tf_op jit(solution)/shard_map/ppermute | solution.py:799
  5.0 0.0 collective-permute-start.4
  5.0 7.7 %collective-permute-done.5.refs_9_ = f32[640,128]{1,0:T(8,128)S(1)} collective-permute-done((f32[640,128]{1,0:T(8,128)S(1)}, f32[640,128]{1,0:T(8,128)S(1)}, u32[]{:S(2)}, u32[]{:S(2)}) %collective-permute-start.5) | collective-permute-done | bytes 327712 | tf_op jit(solution)/shard_map/ppermute | solution.py:799
  12.7 0.1 collective-permute-start.6
  12.8 0.0 copy-start.1
  12.8 0.0 copy-start.2
  12.8 2.1 %shard_map.77 = (f32[256,320]{1,0:T(8,128)S(1)}, f32[16,1088]{1,0:T(8,128)S(1)}, f32[16,1088]{1,0:T(8,128)S(1)}) custom-call(s32[1]{0:T(128)} %bitcast.1.rank.refs_0_, f32[256,320]{1,0:T(8,128)} %bitcast.8, f32[256,128]{1,0:T(8,128)} %bitcast.11, bf16[320,320]{1,0:T(8,128)(2,1)} %refs_4_.1), custom_call_target="tpu_custom_call" | custom-call | tf_op jit(solution)/shard_map/pallas_call | solution.py:729
  14.9 0.5 %collective-permute-start = (f32[16,1088]{1,0:T(8,128)S(1)}, f32[16,1088]{1,0:T(8,128)S(1)}, u32[]{:S(2)}, u32[]{:S(2)}) collective-permute-start(f32[16,1088]{1,0:T(8,128)S(1)} %get-tuple-element.27), channel_id=1, source_target_pairs={{0,1},{1,0},{2,3},{3,2},{4,5},{5,4},{6,7},{7,6},{8,9},{9,8},{10,11... | collective-permute-start | bytes 208904 | tf_op jit(solution)/shard_map/ppermute | solution.py:753
  15.4 1.4 %collective-permute-start.1 = (f32[16,1088]{1,0:T(8,128)S(1)}, f32[16,1088]{1,0:T(8,128)S(1)}, u32[]{:S(2)}, u32[]{:S(2)}) collective-permute-start(f32[16,1088]{1,0:T(8,128)S(1)} %get-tuple-element.28), channel_id=1, source_target_pairs={{0,3},{1,2},{2,1},{3,0},{4,7},{5,6},{6,5},{7,4},{8,11},{9,10},{10,... | collective-permute-start | bytes 208904 | tf_op jit(solution)/shard_map/ppermute | solution.py:752
  16.9 0.0 collective-permute-done.from_a
  16.9 2.8 %collective-permute-done.1.from_b = f32[16,1088]{1,0:T(8,128)S(1)} collective-permute-done((f32[16,1088]{1,0:T(8,128)S(1)}, f32[16,1088]{1,0:T(8,128)S(1)}, u32[]{:S(2)}, u32[]{:S(2)}) %collective-permute-start.1) | collective-permute-done | bytes 69664 | tf_op jit(solution)/shard_map/ppermute | solution.py:752
  19.7 0.2 shard_map.79
  19.9 1.8 %collective-permute-start.2 = (f32[16,896]{1,0:T(8,128)S(1)}, f32[16,896]{1,0:T(8,128)S(1)}, u32[]{:S(2)}, u32[]{:S(2)}) collective-permute-start(f32[16,896]{1,0:T(8,128)S(1)} %get-tuple-element.34), channel_id=1, source_target_pairs={{0,4},{4,0},{8,12},{12,8},{16,20},{20,16},{24,28},{28,24},{1,5},{5... | collective-permute-start | bytes 172040 | tf_op jit(solution)/shard_map/ppermute | solution.py:753
  21.7 3.6 %collective-permute-start.3 = (f32[16,896]{1,0:T(8,128)S(1)}, f32[16,896]{1,0:T(8,128)S(1)}, u32[]{:S(2)}, u32[]{:S(2)}) collective-permute-start(f32[16,896]{1,0:T(8,128)S(1)} %get-tuple-element.35), channel_id=1, source_target_pairs={{0,28},{4,8},{8,4},{12,16},{16,12},{20,24},{24,20},{28,0},{1,29},{... | collective-permute-start | bytes 172040 | tf_op jit(solution)/shard_map/ppermute | solution.py:752
  25.3 1.3 %shard_map.78 = (f32[256,320]{1,0:T(8,128)S(1)}, f32[256,320]{1,0:T(8,128)S(1)}, f32[256,320]{1,0:T(8,128)S(1)}, f32[2,4,16,320]{3,2,1,0:T(8,128)S(1)}, f32[32,64]{1,0:T(8,128)S(1)}) custom-call(s32[1]{0:T(128)} %bitcast.1.rank.refs_0_, s32[16]{0:T(128)S(1)} %bitcast.17, f32[256,320]{1,0:T(8,128)S(1)} %get-tuple-element.26.partial, f32[256,320]{1,0:T(8,128)S(1)} %bitcast.10, ...), custom_call_target="tpu_custom_call" | custom-call | tf_op jit(solution)/shard_map/pallas_call | solution.py:729
  26.6 0.0 collective-permute-done.2.from_a
  26.6 2.0 %collective-permute-done.3.from_b = f32[16,896]{1,0:T(8,128)S(1)} collective-permute-done((f32[16,896]{1,0:T(8,128)S(1)}, f32[16,896]{1,0:T(8,128)S(1)}, u32[]{:S(2)}, u32[]{:S(2)}) %collective-permute-start.3) | collective-permute-done | bytes 57376 | tf_op jit(solution)/shard_map/ppermute | solution.py:752
  28.6 1.1 %shard_map.80 = (f32[256,320]{1,0:T(8,128)S(1)}, f32[32,320]{1,0:T(8,128)S(1)}) custom-call(s32[1]{0:T(128)} %bitcast.place, f32[256,320]{1,0:T(8,128)S(1)} %get-tuple-element.29.field, f32[256,320]{1,0:T(8,128)S(1)} %get-tuple-element.30.second, f32[256,320]{1,0:T(8,128)S(1)} %get-tuple-element.31.known, f32[2,4,16,320]{3,2,1,0:T(8,128)S(1)} %get-tuple-element.32.sides, ...), custom_call_target="tpu_custom_call" | custom-call | tf_op jit(solution)/shard_map/pallas_call | solution.py:729
  29.7 1.9 %shard_map.82 = (f32[256,320]{1,0:T(8,128)S(1)}, f32[24,321]{1,0:T(8,128)S(1)}, f32[24,321]{1,0:T(8,128)S(1)}, f32[32,321]{1,0:T(8,128)S(1)}, f32[128,320]{1,0:T(8,128)S(1)}) custom-call(s32[1]{0:T(128)} %bitcast.1.rank.refs_0_, f32[256,320]{1,0:T(8,128)S(1)} %get-tuple-element.36.refs_1_, f32[32,320]{1,0:T(8,128)S(1)} %get-tuple-element.37.refs_2_, ...), custom_call_target="tpu_custom_call" | custom-call | tf_op jit(solution)/shard_map/pallas_call | solution.py:729
  31.6 0.0 copy-start.4
  31.7 0.1 collective-permute-start.7
  31.7 1.6 %collective-permute-start.8 = (f32[24,321]{1,0:T(8,128)S(1)}, f32[24,321]{1,0:T(8,128)S(1)}, u32[]{:S(2)}, u32[]{:S(2)}) collective-permute-start(f32[24,321]{1,0:T(8,128)S(1)} %get-tuple-element.43), channel_id=1, source_target_pairs={{0,3},{1,2},{2,1},{3,0},{4,7},{5,6},{6,5},{7,4},{8,11},{9,10},{10,... | collective-permute-start | bytes 92456 | tf_op jit(solution)/shard_map/ppermute | solution.py:752
  33.4 1.8 %collective-permute-done.8.refs_3_.from_b = f32[24,321]{1,0:T(8,128)S(1)} collective-permute-done((f32[24,321]{1,0:T(8,128)S(1)}, f32[24,321]{1,0:T(8,128)S(1)}, u32[]{:S(2)}, u32[]{:S(2)}) %collective-permute-start.8) | collective-permute-done | bytes 30848 | tf_op jit(solution)/shard_map/ppermute | solution.py:752
  35.2 0.1 collective-permute-start.10
  35.3 3.6 %collective-permute-start.11 = (f32[16,320]{1,0:T(8,128)S(1)}, f32[16,320]{1,0:T(8,128)S(1)}, u32[]{:S(2)}, u32[]{:S(2)}) collective-permute-start(f32[16,320]{1,0:T(8,128)S(1)} %get-tuple-element.48.mine_b), channel_id=1, source_target_pairs={{0,28},{4,8},{8,4},{12,16},{16,12},{20,24},{24,20},{28,0},{1,29},{... | collective-permute-start | bytes 61448 | tf_op jit(solution)/shard_map/ppermute | solution.py:752
  38.9 1.5 %collective-permute-start.9 = (f32[8,321]{1,0:T(8,128)S(1)}, f32[8,321]{1,0:T(8,128)S(1)}, u32[]{:S(2)}, u32[]{:S(2)}) collective-permute-start(f32[8,321]{1,0:T(8,128)S(1)} %slice.14), channel_id=1, source_target_pairs={{0,2},{1,3},{2,0},{3,1},{4,6},{5,7},{6,4},{7,5},{8,10},{9,11},{10,... | collective-permute-start | bytes 30824 | tf_op jit(solution)/shard_map/ppermute | solution.py:855
  40.5 2.2 %collective-permute-done.9.refs_11_ = f32[8,321]{1,0:T(8,128)S(1)} collective-permute-done((f32[8,321]{1,0:T(8,128)S(1)}, f32[8,321]{1,0:T(8,128)S(1)}, u32[]{:S(2)}, u32[]{:S(2)}) %collective-permute-start.9) | collective-permute-done | bytes 10304 | tf_op jit(solution)/shard_map/ppermute | solution.py:855
  42.6 2.4 %shard_map.83 = (f32[256,320]{1,0:T(8,128)}, bf16[512,320]{1,0:T(8,128)(2,1)}) custom-call(s32[1]{0:T(128)} %bitcast.1.rank.refs_0_, f32[256,320]{1,0:T(8,128)S(1)} %get-tuple-element.41.refs_1_.partial, f32[24,321]{1,0:T(8,128)S(1)} %collective-permute-done.7.refs_2_.from_a, f32[24,321]{1,0:T(8,128)S(1)} %collective-permute-done.8.refs_3_.from_b, ...), custom_call_target="tpu_custom_call" | custom-call | tf_op jit(solution)/shard_map/pallas_call | solution.py:729
  45.1 0.6 %shard_map.85 = f32[256,320]{1,0:T(8,128)} custom-call(s32[1]{0:T(128)} %bitcast.place, f32[256,320]{1,0:T(8,128)} %get-tuple-element.46.fields_in, f32[16,320]{1,0:T(8,128)S(1)} %get-tuple-element.47.mine_a, f32[16,320]{1,0:T(8,128)S(1)} %get-tuple-element.48.mine_b, f32[16,320]{1,0:T(8,128)S(1)} %collective-permute-done.10.from_a, ...), custom_call_target="tpu_custom_call", output_to_operand_aliasing={{}: (1, {})} | custom-call | tf_op jit(solution)/shard_map/pallas_call | solution.py:729
  (19 shorter events, 0.1 us)
Async XLA Ops:
  0.6 1.0 %copy-start.3 = (bf16[16,32,320]{2,1,0:T(8,128)(2,1)S(1)}, bf16[16,32,320]{2,1,0:T(8,128)(2,1)}, u32[]{:S(2)}) copy-start(bf16[16,32,320]{2,1,0:T(8,128)(2,1)} %param.10) | copy-start | bytes 983044
  1.9 10.8 %collective-permute-start.5 = (f32[640,128]{1,0:T(8,128)S(1)}, f32[640,128]{1,0:T(8,128)S(1)}, u32[]{:S(2)}, u32[]{:S(2)}) collective-permute-start(f32[640,128]{1,0:T(8,128)S(1)} %get-tuple-element.40.refs_9_), channel_id=1, source_target_pairs={{0,2},{1,3},{2,0},{3,1},{4,6},{5,7},{6,4},{7,5},{8,10},{9,11},{10,... | collective-permute-start | bytes 983048 | tf_op jit(solution)/shard_map/ppermute | solution.py:799
  5.0 24.7 %collective-permute-start.4 = (f32[320,128]{1,0:T(8,128)S(1)}, f32[320,128]{1,0:T(8,128)S(1)}, u32[]{:S(2)}, u32[]{:S(2)}) collective-permute-start(f32[320,128]{1,0:T(8,128)S(1)} %get-tuple-element.39.refs_8_), channel_id=1, source_target_pairs={{0,1},{1,0},{2,3},{3,2},{4,5},{5,4},{6,7},{7,6},{8,9},{9,8},{10,11... | collective-permute-start | bytes 491528 | tf_op jit(solution)/shard_map/ppermute | solution.py:800
  12.7 17.0 %collective-permute-start.6 = (f32[320,128]{1,0:T(8,128)S(1)}, f32[320,128]{1,0:T(8,128)S(1)}, u32[]{:S(2)}, u32[]{:S(2)}) collective-permute-start(f32[320,128]{1,0:T(8,128)S(1)} %slice.16), channel_id=1, source_target_pairs={{0,1},{1,0},{2,3},{3,2},{4,5},{5,4},{6,7},{7,6},{8,9},{9,8},{10,11... | collective-permute-start | bytes 491528 | tf_op jit(solution)/shard_map/ppermute | solution.py:822
  12.8 6.9 %copy-start.1 = (f32[16,16,320]{2,1,0:T(8,128)S(1)}, f32[16,16,320]{2,1,0:T(8,128)}, u32[]{:S(2)}) copy-start(f32[16,16,320]{2,1,0:T(8,128)} %param.6) | copy-start | bytes 983044
  12.8 6.9 %copy-start.2 = (f32[16,16,128]{2,1,0:T(8,128)S(1)}, f32[16,16,128]{2,1,0:T(8,128)}, u32[]{:S(2)}) copy-start(f32[16,16,128]{2,1,0:T(8,128)} %param.7) | copy-start | bytes 393220
  14.9 2.0 %collective-permute-start = (f32[16,1088]{1,0:T(8,128)S(1)}, f32[16,1088]{1,0:T(8,128)S(1)}, u32[]{:S(2)}, u32[]{:S(2)}) collective-permute-start(f32[16,1088]{1,0:T(8,128)S(1)} %get-tuple-element.27), channel_id=1, source_target_pairs={{0,1},{1,0},{2,3},{3,2},{4,5},{5,4},{6,7},{7,6},{8,9},{9,8},{10,11... | collective-permute-start | bytes 208904 | tf_op jit(solution)/shard_map/ppermute | solution.py:753
  15.4 4.3 %collective-permute-start.1 = (f32[16,1088]{1,0:T(8,128)S(1)}, f32[16,1088]{1,0:T(8,128)S(1)}, u32[]{:S(2)}, u32[]{:S(2)}) collective-permute-start(f32[16,1088]{1,0:T(8,128)S(1)} %get-tuple-element.28), channel_id=1, source_target_pairs={{0,3},{1,2},{2,1},{3,0},{4,7},{5,6},{6,5},{7,4},{8,11},{9,10},{10,... | collective-permute-start | bytes 208904 | tf_op jit(solution)/shard_map/ppermute | solution.py:752
  19.7 5.6 %copy-start = (bf16[320,320]{1,0:T(8,128)(2,1)S(1)}, bf16[320,320]{1,0:T(8,128)(2,1)}, u32[]{:S(2)}) copy-start(bf16[320,320]{1,0:T(8,128)(2,1)} %refs_4_.1) | copy-start | bytes 614404
  19.9 6.7 %collective-permute-start.2 = (f32[16,896]{1,0:T(8,128)S(1)}, f32[16,896]{1,0:T(8,128)S(1)}, u32[]{:S(2)}, u32[]{:S(2)}) collective-permute-start(f32[16,896]{1,0:T(8,128)S(1)} %get-tuple-element.34), channel_id=1, source_target_pairs={{0,4},{4,0},{8,12},{12,8},{16,20},{20,16},{24,28},{28,24},{1,5},{5... | collective-permute-start | bytes 172040 | tf_op jit(solution)/shard_map/ppermute | solution.py:753
  21.7 3.6 %copy-start.6 = (s32[16,1]{0,1:T(1,128)S(1)}, s32[16,1]{0,1:T(1,128)}, u32[]{:S(2)}) copy-start(s32[16,1]{0,1:T(1,128)} %param.9) | copy-start | bytes 196
  21.7 6.9 %collective-permute-start.3 = (f32[16,896]{1,0:T(8,128)S(1)}, f32[16,896]{1,0:T(8,128)S(1)}, u32[]{:S(2)}, u32[]{:S(2)}) collective-permute-start(f32[16,896]{1,0:T(8,128)S(1)} %get-tuple-element.35), channel_id=1, source_target_pairs={{0,28},{4,8},{8,4},{12,16},{16,12},{20,24},{24,20},{28,0},{1,29},{... | collective-permute-start | bytes 172040 | tf_op jit(solution)/shard_map/ppermute | solution.py:752
  28.6 1.1 %copy-start.5 = (bf16[320,320]{1,0:T(8,128)(2,1)S(1)}, bf16[320,320]{1,0:T(8,128)(2,1)}, u32[]{:S(2)}) copy-start(bf16[320,320]{1,0:T(8,128)(2,1)} %refs_5_.3) | copy-start | bytes 614404
  31.6 11.0 %copy-start.4 = (bf16[16,32,320]{2,1,0:T(8,128)(2,1)S(1)}, bf16[16,32,320]{2,1,0:T(8,128)(2,1)}, u32[]{:S(2)}) copy-start(bf16[16,32,320]{2,1,0:T(8,128)(2,1)} %param.10) | copy-start | bytes 983044
  31.7 1.7 %collective-permute-start.7 = (f32[24,321]{1,0:T(8,128)S(1)}, f32[24,321]{1,0:T(8,128)S(1)}, u32[]{:S(2)}, u32[]{:S(2)}) collective-permute-start(f32[24,321]{1,0:T(8,128)S(1)} %get-tuple-element.42), channel_id=1, source_target_pairs={{0,1},{1,0},{2,3},{3,2},{4,5},{5,4},{6,7},{7,6},{8,9},{9,8},{10,11... | collective-permute-start | bytes 92456 | tf_op jit(solution)/shard_map/ppermute | solution.py:753
  31.7 3.4 %collective-permute-start.8 = (f32[24,321]{1,0:T(8,128)S(1)}, f32[24,321]{1,0:T(8,128)S(1)}, u32[]{:S(2)}, u32[]{:S(2)}) collective-permute-start(f32[24,321]{1,0:T(8,128)S(1)} %get-tuple-element.43), channel_id=1, source_target_pairs={{0,3},{1,2},{2,1},{3,0},{4,7},{5,6},{6,5},{7,4},{8,11},{9,10},{10,... | collective-permute-start | bytes 92456 | tf_op jit(solution)/shard_map/ppermute | solution.py:752
  35.2 9.9 %collective-permute-start.10 = (f32[16,320]{1,0:T(8,128)S(1)}, f32[16,320]{1,0:T(8,128)S(1)}, u32[]{:S(2)}, u32[]{:S(2)}) collective-permute-start(f32[16,320]{1,0:T(8,128)S(1)} %get-tuple-element.47.mine_a), channel_id=1, source_target_pairs={{0,4},{4,0},{8,12},{12,8},{16,20},{20,16},{24,28},{28,24},{1,5},{5... | collective-permute-start | bytes 61448 | tf_op jit(solution)/shard_map/ppermute | solution.py:753
  35.3 9.8 %collective-permute-start.11 = (f32[16,320]{1,0:T(8,128)S(1)}, f32[16,320]{1,0:T(8,128)S(1)}, u32[]{:S(2)}, u32[]{:S(2)}) collective-permute-start(f32[16,320]{1,0:T(8,128)S(1)} %get-tuple-element.48.mine_b), channel_id=1, source_target_pairs={{0,28},{4,8},{8,4},{12,16},{16,12},{20,24},{24,20},{28,0},{1,29},{... | collective-permute-start | bytes 61448 | tf_op jit(solution)/shard_map/ppermute | solution.py:752
  38.9 3.7 %collective-permute-start.9 = (f32[8,321]{1,0:T(8,128)S(1)}, f32[8,321]{1,0:T(8,128)S(1)}, u32[]{:S(2)}, u32[]{:S(2)}) collective-permute-start(f32[8,321]{1,0:T(8,128)S(1)} %slice.14), channel_id=1, source_target_pairs={{0,2},{1,3},{2,0},{3,1},{4,6},{5,7},{6,4},{7,5},{8,10},{9,11},{10,... | collective-permute-start | bytes 30824 | tf_op jit(solution)/shard_map/ppermute | solution.py:855
where the time goes:
time: 45.9 us; the launch traced here: 45.7 us
  starting transfers between devices  17.4 us (38%)
  waiting for transfers between devices  16.5 us (36%)
  Pallas kernels  9.95 us (22%)
  local copies, waits for them, and re-layouts  1.04 us (2%)
  between operations  0.8 us (2%)
    ppermute x4, starting transfers between devices, ring(): from_b = lax.ppermute(to_b, axis, upper_pairs(count))  10.3 us
    pallas_call x9, Pallas kernels, call(): pl.pallas_call(kernel, out_shape=[jax.ShapeDtypeStruct(shape, dtype) for...  9.95 us
    ppermute x1, waiting for transfers between devices, on_device(): lax.ppermute(pairs[m - 1], 'crm', xor[2 * m])  7.71 us
    ppermute x4, waiting for transfers between devices, ring(): from_b = lax.ppermute(to_b, axis, upper_pairs(count))  6.64 us
    ppermute x1, starting transfers between devices, on_device(): lax.ppermute(pairs[m - 1], 'crm', xor[2 * m])  3.06 us
    ppermute x4, starting transfers between devices, ring(): from_a = lax.ppermute(to_a, axis, lower_pairs(count))  2.5 us
    ppermute x1, waiting for transfers between devices, on_device(): forcings.append(lax.ppermute(sends[8 * k:8 * k + 8], 'crm', xor[k]))  2.17 us
    ppermute x1, starting transfers between devices, on_device(): forcings.append(lax.ppermute(sends[8 * k:8 * k + 8], 'crm', xor[k]))  1.52 us
  transfers between devices with their start and end apart: 12, of which 5 were waited for; matrix products, arithmetic and copies ran while one was open for 0% of the time, Pallas kernels for 16%

commit v1 on v0

--- a/solution.py
+++ b/solution.py
@@ -10,7 +10,6 @@
 
 
 SUB = 4
-HIGHEST = lax.Precision.HIGHEST
 CRM_STEP = 0.5
 DIFFUSION = 0.2
 COUPLING = 0.5
@@ -72,15 +71,14 @@
     return out
 
 
-def sublane_coefficients(rows, width):
-    position = lax.broadcasted_iota(jnp.int32, (rows, width), 0) & 3
+def sublane_coefficients(width):
+    position = lax.broadcasted_iota(jnp.int32, (8, width), 0) & 3
     table = []
-    for shift in range(-3, 4):
-        value = jnp.zeros((rows, width), jnp.float32)
+    for move in range(NODES):
+        value = jnp.zeros((8, width), jnp.float32)
         for at in range(NODES):
-            if 0 <= at + shift < NODES:
-                value = jnp.where(position == at, DERIV[at][at + shift], value)
-        table.append(value)
+            value = jnp.where(position == at, DERIV[at][(at + move) % NODES], value)
+        table.append((value, position < NODES - move))
     return table
 
 
@@ -89,11 +87,14 @@
     blocks = []
     for at in range(0, field.shape[0], 8):
         part = field[at : at + 8]
-        total = None
-        for index, shift in enumerate(range(-3, 4)):
-            moved = part if shift == 0 else pltpu.roll(part, (-shift) % 8, 0)
-            term = table[index][:, :width] * moved
-            total = term if total is None else total + term
+        total = table[0][0][:, :width] * part
+        for move in range(1, NODES):
+            moved = jnp.where(
+                table[move][1][:, :width],
+                pltpu.roll(part, 8 - move, 0),
+                pltpu.roll(part, NODES - move, 0),
+            )
+            total = total + table[move][0][:, :width] * moved
         blocks.append(total)
     return blocks[0] if len(blocks) == 1 else jnp.concatenate(blocks, axis=0)
 
@@ -132,10 +133,16 @@
     )
 
 
-def local_update(base_ref, field_ref, mixed_ref, wind_ref, out_ref, size_x, size_y, levels, average):
+def local_update(base_ref, field_ref, mix, wind_ref, out_ref, size_x, size_y, levels, average,
+                 mixed_ref=None):
     channels = field_ref.shape[1]
-    table = sublane_coefficients(8, 2 * levels)
+    table = sublane_coefficients(2 * levels)
+    strip = NODES * size_y
     for element in range(size_x // NODES):
+        whole = pl.ds(element * strip, strip)
+        mixed = mix_all(field_ref[whole, :], mix)
+        if mixed_ref is not None:
+            mixed_ref[whole, :] = mixed
         rows = [pl.ds((NODES * element + i) * size_y, size_y) for i in range(NODES)]
         wind = [winds(wind_ref[row, :], levels) for row in rows]
         for begin, end in lane_tiles(channels, 2 * levels):
@@ -144,9 +151,10 @@
             slopes = dx_rows(values)
             for i in range(NODES):
                 along_x, along_y = wind[i][0][:, :width], wind[i][1][:, :width]
+                base = values[i] if base_ref is field_ref else base_ref[rows[i], begin:end]
                 result = (
-                    base_ref[rows[i], begin:end]
-                    + mixed_ref[rows[i], begin:end]
+                    base
+                    + mixed[i * size_y : (i + 1) * size_y, begin:end]
                     - (along_x * slopes[i] + along_y * dsub(values[i], table))
                 )
                 out_ref[rows[i], begin:end] = sub_average(result) if average else result
@@ -175,12 +183,24 @@
     )
 
 
+def select_rows(chosen, values):
+    high = to_bf16(values)
+    rest = values - high.astype(jnp.float32)
+    middle = to_bf16(rest)
+    low = to_bf16(rest - middle.astype(jnp.float32))
+    return jnp.dot(
+        jnp.concatenate([chosen] * 3, axis=1),
+        jnp.concatenate([high, middle, low], axis=0),
+        preferred_element_type=jnp.float32,
+    )
+
+
 def is_even(rank):
     return (rank[0] & 1) == 0
 
 
 def begin_kernel(size_x, size_y, levels, rank, state_in, wind_in, mix_in, partial, to_a, to_b,
-                 state, wind, mix, mixed, message, arrivals):
+                 state, wind, mix, message, arrivals):
     channels = state.shape[1]
     copies = [
         pltpu.make_async_copy(source, target, arrivals.at[index])
@@ -190,11 +210,9 @@
     ]
     for copy in copies:
         copy.start()
-    copies[0].wait()
-    copies[1].wait()
-    mixed[...] = mix_all(state[...], mix[...])
-    copies[2].wait()
-    local_update(state, state, mixed, wind, partial, size_x, size_y, levels, True)
+    for copy in copies:
+        copy.wait()
+    local_update(state, state, mix[...], wind, partial, size_x, size_y, levels, True)
     average_rows(partial, size_x, size_y)
     to_left, to_right = message.at[0], message.at[1]
     for out, column, near, row in ((to_left, 0, 0, 0), (to_right, size_y - 1, size_y - NODES, 3)):
@@ -285,29 +303,28 @@
 
 
 def ready_kernel(size_x, size_y, levels, capacity, rank, owner, partial, state, wind, mix,
-                 from_a, from_b, field, mixed, total, sides, onehot):
+                 from_a, from_b, field, mixed, total, sides, gather, spread):
     channels = state.shape[1]
     from_left, from_right = in_order(rank, from_a, from_b)
-    shape = onehot.shape
     parts = 8 // capacity
-    lanes = lax.broadcasted_iota(jnp.int32, shape, 1) >> 2
-    named = jnp.zeros(shape, jnp.int32)
-    for c in range(owner.shape[0]):
-        named = jnp.where(lanes == c, owner[c], named)
-    position = jnp.zeros(shape, jnp.int32)
-    for c in range(owner.shape[0]):
-        position = position + jnp.where((lanes > c) & (named == owner[c]), 1, 0)
-    offset = rank[0] ^ named
-    slot = (offset * capacity + position) * parts
-    rows = lax.broadcasted_iota(jnp.int32, shape, 0)
-    onehot[...] = jnp.where((rows >= slot) & (rows < slot + parts), 1.0, 0.0)
+    for out, node_axis in ((gather, 1), (spread, 0)):
+        columns = lax.broadcasted_iota(jnp.int32, out.shape, node_axis) >> 2
+        named = jnp.zeros(out.shape, jnp.int32)
+        for c in range(owner.shape[0]):
+            named = jnp.where(columns == c, owner[c], named)
+        position = jnp.zeros(out.shape, jnp.int32)
+        for c in range(owner.shape[0]):
+            position = position + jnp.where((columns > c) & (named == owner[c]), 1, 0)
+        slot = ((rank[0] ^ named) * capacity + position) * parts
+        rows = lax.broadcasted_iota(jnp.int32, out.shape, 1 - node_axis)
+        count = parts if node_axis else 1
+        out[...] = jnp.where((rows >= slot) & (rows < slot + count), 1.0, 0.0).astype(jnp.bfloat16)
     left, right = side_changes(size_x, size_y, partial, from_left, from_right)
     for x in range(size_x):
         row = pl.ds(x * size_y, size_y)
         field[row, :] = edge_rows(partial[row, :], left[x : x + 1], right[x : x + 1])
-    mixed[...] = mix_all(field[...], mix[...])
-    local_update(state, field, mixed, wind, total, size_x, size_y, levels, True)
-    table = sublane_coefficients(8, channels)
+    local_update(state, field, mix[...], wind, total, size_x, size_y, levels, True, mixed)
+    table = sublane_coefficients(channels)
     for side, (message, y, change, factor) in enumerate(
         ((from_left, 0, left, LAST), (from_right, size_y - 1, right, FIRST))
     ):
@@ -379,9 +396,8 @@
 
 def interleave(states, start, channels, turned, rows):
     for lane, (begin, end) in enumerate(lane_tiles(channels, 128)):
-        turned[lane, 0:rows, 0 : end - begin] = states[pl.ds(start, rows), begin:end].astype(
-            jnp.float32
-        )
+        value = states[pl.ds(start, rows), begin:end].astype(jnp.float32)
+        turned[lane, 0:rows, 0 : end - begin] = value + value
 
     def tile(t, lane):
         return turned[lane, pl.ds(t, 8, stride=rows // 8), :]
@@ -409,18 +425,18 @@
             pack(tile, channels, pairs[k // 2 - 1].at[at : at + length], rows)
 
 
-def cloud_run(states, forcing, mix, rows, parts, tendency, finals):
-    blocks = states.shape[0] // rows
+def cloud_run(states, blocks, forcing, mix, rows, parts, tendency, finals):
     count = rows // 8
     columns = count * parts
+    half = mix[...] * 0.5
     means, totals = {}, {}
     for step in range(SUB):
         last = step == SUB - 1
-        for begin in range(0, blocks, 2):
-            group = range(begin, min(begin + 2, blocks))
-            mixed = mix_all(states[begin * rows : (group[-1] + 1) * rows, :], mix[...])
+        for begin in range(0, len(blocks), 2):
+            group = range(begin, min(begin + 2, len(blocks)))
+            mixed = mix_all(states[begin * rows : (group[-1] + 1) * rows, :], half)
             for block in group:
-                push = forcing[8 * block : 8 * block + 8, :]
+                push = forcing[8 * blocks[block] : 8 * blocks[block] + 8, :]
 
                 def read(t):
                     at = block * rows + 8 * t
@@ -430,8 +446,8 @@
                     total = read(0)
                     for t in range(1, count):
                         total = total + read(t)
-                    means[block] = part_sum(total, parts) * (1.0 / columns)
-                gain = CRM_STEP * (push - means[block])
+                    means[block] = part_sum(total, parts) * (0.5 / columns)
+                gain = 2.0 * CRM_STEP * (push - means[block])
                 keep = not last or block in finals
                 total = None
                 if keep:
@@ -446,20 +462,19 @@
                         states[block * rows + 8 * t : block * rows + 8 * t + 8, :] = (
                             (1.0 - 2.0 * CRM_STEP * DIFFUSION) * here
                             + CRM_STEP * DIFFUSION * (behind + ahead)
-                            + CRM_STEP * turn
-                            + gain
+                        ) + ((2.0 * CRM_STEP) * turn + gain)
+                        behind, here = here, ahead
+                if tendency is not None or not last:
+                    mean = (
+                        means[block] + part_sum(total, parts) * (CRM_STEP / columns) + 0.5 * gain
+                    )
+                    means[block] = mean
+                    if tendency is not None:
+                        totals[block] = (
+                            mean - push if step == 0 else totals[block] + (mean - push)
                         )
-                        behind, here = here, ahead
-                if tendency is not None:
-                    mean = means[block] + part_sum(total, parts) * (CRM_STEP / columns) + gain
-                    totals[block] = mean - push if step == 0 else totals[block] + (mean - push)
-                    means[block] = mean
-                elif not last:
-                    means[block] = (
-                        means[block] + part_sum(total, parts) * (CRM_STEP / columns) + gain
-                    )
     if tendency is not None:
-        for block in range(blocks):
+        for block in range(len(blocks)):
             tendency[8 * block : 8 * block + 8, :] = totals[block] * (1.0 / SUB)
 
 
@@ -469,7 +484,7 @@
     for lane, (begin, end) in enumerate(lane_tiles(channels, 128)):
         width = end - begin
         for t in range(count):
-            value = states[start + 8 * t : start + 8 * t + 8, begin:end]
+            value = 0.5 * states[start + 8 * t : start + 8 * t + 8, begin:end]
             if width < 128:
                 value = jnp.concatenate([value, jnp.zeros((8, 128 - width), jnp.float32)], axis=1)
             turned[lane, pl.ds(t, 8, stride=count), :] = value
@@ -484,15 +499,15 @@
             )
 
 
-def second_kernel(size_x, size_y, levels, place, field, second, known, sides, onehot, wind, mix,
-                  from_a, from_b, work, forcing, mixed, total, reduced):
+def second_kernel(size_x, size_y, levels, place, field, second, known, sides, gather, wind, mix,
+                  from_a, from_b, work, forcing, total, reduced):
     from_up, from_down = in_order(place, from_a, from_b)
     channels = field.shape[1]
     span = 2 * channels + 2 * levels
     pieces = span // (2 * levels)
     last_row = pl.ds((size_x - 1) * size_y, size_y)
     first_row = pl.ds(0, size_y)
-    small = sublane_coefficients(8, channels)
+    small = sublane_coefficients(channels)
     ups = 0.5 * (from_up[:, 0:channels] - field[first_row, :])
     downs = 0.5 * (from_down[:, 0:channels] - field[last_row, :])
     remixed = mix_all(
@@ -574,28 +589,25 @@
         beyond = edge_rows(beyond, ends[0], ends[1])
         total[row, :] = 0.5 * (total[row, :] + beyond)
     average_rows(total, size_x, size_y)
+    phase = lax.broadcasted_iota(jnp.int32, (size_y, channels), 0) & 3
+    weight = jnp.where(
+        (phase == 0) | (phase == 3), float(QUADRATURE[0] / 4.0), float(QUADRATURE[1] / 4.0)
+    )
     for element in range(size_x // NODES):
         value = None
         for i in range(NODES):
             term = float(QUADRATURE[i]) * total[pl.ds((NODES * element + i) * size_y, size_y), :]
             value = term if value is None else value + term
-        reduced[pl.ds(element * size_y, size_y), :] = value
-    phase = lax.broadcasted_iota(jnp.int32, onehot.shape, 1) & 3
-    weight = jnp.where(
-        (phase == 0) | (phase == 3), float(QUADRATURE[0] / 4.0), float(QUADRATURE[1] / 4.0)
-    )
-    forcing[...] = jnp.dot(
-        onehot[...] * weight, reduced[...], precision=HIGHEST, preferred_element_type=jnp.float32
-    )
-    mixed[...] = mix_all(total[...], mix[...])
-    local_update(total, total, mixed, wind, work, size_x, size_y, levels, False)
+        reduced[pl.ds(element * size_y, size_y), :] = weight * value
+    forcing[...] = select_rows(gather[...], reduced[...])
+    local_update(total, total, mix[...], wind, work, size_x, size_y, levels, False)
 
 
 def home_kernel(size_x, size_y, groups, capacity, *refs):
-    rank, work, forcing, onehot, mix, cloud_mix, own, near, far = refs[:9]
-    pairs = refs[9 : 8 + groups // 2]
-    out, to_a, to_b, sends, own_final = refs[8 + groups // 2 : 13 + groups // 2]
-    reduced, tendency, cloud, message = refs[13 + groups // 2 :]
+    rank, work, forcing, gather, spread, mix, cloud_mix, own, near, far = refs[:10]
+    pairs = refs[10 : 9 + groups // 2]
+    out, to_a, to_b, sends, own_final = refs[9 + groups // 2 : 14 + groups // 2]
+    reduced, tendency, cloud, message = refs[14 + groups // 2 :]
     channels = work.shape[1]
     parts = 8 // capacity
     rows = own.shape[0]
@@ -607,24 +619,19 @@
         unpack(
             far.at[(m - 1) * length : m * length], channels, cloud, (2 * m + 1) * rows, rows
         )
-    cloud_run(cloud, forcing, cloud_mix, rows, parts, tendency, (0,))
+    cloud_run(
+        cloud, range(groups), forcing, cloud_mix, rows, parts, tendency, (0,)
+    )
     own_final[...] = cloud[0:rows, :]
     tend = tendency[...]
     change = COUPLING * (tend + mix_all(tend, mix[...]))
-    part = lax.broadcasted_iota(jnp.int32, onehot.shape, 0) & (parts - 1)
-    reduced[...] = lax.dot_general(
-        jnp.where(part == 0, onehot[...], 0.0),
-        change,
-        (((0,), (0,)), ((), ())),
-        precision=HIGHEST,
-        preferred_element_type=jnp.float32,
-    )
+    reduced[...] = select_rows(spread[...], change)
     for x in range(size_x):
         row = pl.ds(x * size_y, size_y)
         element = pl.ds((x // NODES) * size_y, size_y)
         out[row, :] = sub_average(work[row, :] + reduced[element, :])
     average_rows(out, size_x, size_y)
-    occupied = jnp.max(onehot[...], axis=1, keepdims=True)
+    occupied = jnp.max(gather[...].astype(jnp.float32), axis=1, keepdims=True)
     sends[:, 0:channels] = forcing[...]
     sends[:, channels : channels + 1] = occupied
     message[0] = column_of(out, 0, size_x, size_y)
@@ -673,7 +680,8 @@
         at = (k & 1) * length
         unpack(pairs[k // 2 - 1].at[at : at + length], channels, cloud, (k - 1) * rows, rows)
         forcing[8 * (k - 1) : 8 * k, :] = forcings[k - 1][:, 0:channels]
-    cloud_run(cloud, forcing, mix, rows, parts, None, tuple(range(groups - 1)))
+    blocks = tuple(range(groups - 1))
+    cloud_run(cloud, blocks, forcing, mix, rows, parts, None, blocks)
     for k in range(groups):
         start = pl.multiple_of((rank[0] ^ k) * rows, rows)
         source, at = (cloud, (k - 1) * rows) if k else (own_final, 0)
@@ -779,7 +787,7 @@
         functools.partial(begin_kernel, size_x, size_y, levels),
         [grid, column_message, column_message],
         [
-            grid, ((nodes, 2 * levels), f32), (dyn_mix.shape, dyn_mix.dtype), grid,
+            grid, ((nodes, 2 * levels), f32), (dyn_mix.shape, dyn_mix.dtype),
             ((2,) + column_message[0], f32), DMA((3,)),
         ],
         rank, state, wind, dyn_mix,
@@ -809,11 +817,12 @@
         smem=(0, 1),
     )
     row_a, row_b = ring(to_a, to_b, "elem")
-    field, known, total, sides, onehot = call(
+    field, known, total, sides, gather, spread = call(
         functools.partial(ready_kernel, size_x, size_y, levels, capacity),
         [
             grid, grid, grid, ((2, 4, size_x, channels), f32),
-            ((8 * groups, elements * size_y), f32),
+            ((8 * groups, elements * size_y), jnp.bfloat16),
+            ((elements * size_y, 8 * groups), jnp.bfloat16),
         ],
         [],
         rank, owners, partial, state, wind, dyn_mix, column_a, column_b,
@@ -825,8 +834,8 @@
     work, forcing = call(
         functools.partial(second_kernel, size_x, size_y, levels),
         [grid, ((8 * groups, channels), f32)],
-        [grid, grid, ((elements * size_y, channels), f32)],
-        place, field, total, known, sides, onehot, wind, dyn_mix, row_a, row_b,
+        [grid, ((elements * size_y, channels), f32)],
+        place, field, total, known, sides, gather, wind, dyn_mix, row_a, row_b,
         smem=(0,),
     )
     edge = ((size_x + 8, channels + 1), f32)
@@ -839,7 +848,7 @@
             ((groups * rows, channels), f32),
             ((2, size_x, channels), f32),
         ],
-        rank, work, forcing, onehot, dyn_mix, crm_mix, own, near_in, far_in, *pairs_in,
+        rank, work, forcing, gather, spread, dyn_mix, crm_mix, own, near_in, far_in, *pairs_in,
         smem=(0,),
     )
 

time: 45.9 us -> 45.3 us (0.987)
  Pallas kernels: 9.95 us -> 9.41 us
    pallas_call x9, Pallas kernels: 9.95 us -> 9.41 us  [call(): pl.pallas_call(kernel, out_shape=[jax.ShapeDtypeStruct(shape, dtype) for...]
  transfers between devices with their start and end apart: 12 -> 12, of which waited for: 5 -> 5; matrix products, arithmetic and copies ran while one was open for 0% -> 0% of each run, Pallas kernels for 16% -> 15%
where the time goes in v1:
time: 45.3 us; the launch traced here: 45.1 us
  starting transfers between devices  17.4 us (38%)
  waiting for transfers between devices  16.5 us (36%)
  Pallas kernels  9.41 us (21%)
  local copies, waits for them, and re-layouts  1.04 us (2%)
  between operations  0.8 us (2%)
    ppermute x4, starting transfers between devices, ring(): from_b = lax.ppermute(to_b, axis, upper_pairs(count))  10.3 us
    pallas_call x9, Pallas kernels, call(): pl.pallas_call(kernel, out_shape=[jax.ShapeDtypeStruct(shape, dtype) for...  9.41 us
    ppermute x1, waiting for transfers between devices, on_device(): lax.ppermute(pairs[m - 1], 'crm', xor[2 * m])  7.71 us
    ppermute x4, waiting for transfers between devices, ring(): from_b = lax.ppermute(to_b, axis, upper_pairs(count))  6.56 us
    ppermute x1, starting transfers between devices, on_device(): lax.ppermute(pairs[m - 1], 'crm', xor[2 * m])  3.06 us
    ppermute x4, starting transfers between devices, ring(): from_a = lax.ppermute(to_a, axis, lower_pairs(count))  2.49 us
    ppermute x1, waiting for transfers between devices, on_device(): forcings.append(lax.ppermute(sends[8 * k:8 * k + 8], 'crm', xor[k]))  2.17 us
    ppermute x1, starting transfers between devices, on_device(): forcings.append(lax.ppermute(sends[8 * k:8 * k + 8], 'crm', xor[k]))  1.52 us
  transfers between devices with their start and end apart: 12, of which 5 were waited for; matrix products, arithmetic and copies ran while one was open for 0% of the time, Pallas kernels for 15%

profile of v1, /device:TPU:0, one launch (start us, length us, event | category | flops | bytes accessed | tf_op | source)
XLA Modules:
  0.0 45.1 jit_solution(3740368717290366186)
XLA Ops:
  0.6 0.0 copy-start.3
  0.6 1.0 %copy-done.3 = bf16[16,32,320]{2,1,0:T(8,128)(2,1)S(1)} copy-done((bf16[16,32,320]{2,1,0:T(8,128)(2,1)S(1)}, bf16[16,32,320]{2,1,0:T(8,128)(2,1)}, u32[]{:S(2)}) %copy-start.3) | copy-done | bytes 327704
  1.6 0.3 shard_map.81
  1.9 3.1 %collective-permute-start.5 = (f32[640,128]{1,0:T(8,128)S(1)}, f32[640,128]{1,0:T(8,128)S(1)}, u32[]{:S(2)}, u32[]{:S(2)}) collective-permute-start(f32[640,128]{1,0:T(8,128)S(1)} %get-tuple-element.42.refs_9_), channel_id=1, source_target_pairs={{0,2},{1,3},{2,0},{3,1},{4,6},{5,7},{6,4},{7,5},{8,10},{9,11},{10,... | collective-permute-start | bytes 983048 | tf_op jit(solution)/shard_map/ppermute | solution.py:807
  5.0 0.0 collective-permute-start.4
  5.0 7.7 %collective-permute-done.5.refs_10_ = f32[640,128]{1,0:T(8,128)S(1)} collective-permute-done((f32[640,128]{1,0:T(8,128)S(1)}, f32[640,128]{1,0:T(8,128)S(1)}, u32[]{:S(2)}, u32[]{:S(2)}) %collective-permute-start.5) | collective-permute-done | bytes 327712 | tf_op jit(solution)/shard_map/ppermute | solution.py:807
  12.7 0.1 collective-permute-start.6
  12.8 0.0 copy-start.1
  12.8 0.0 copy-start.2
  12.8 2.0 %shard_map.77 = (f32[256,320]{1,0:T(8,128)S(1)}, f32[16,1088]{1,0:T(8,128)S(1)}, f32[16,1088]{1,0:T(8,128)S(1)}) custom-call(s32[1]{0:T(128)} %bitcast.1.rank.refs_0_, f32[256,320]{1,0:T(8,128)} %bitcast.8, f32[256,128]{1,0:T(8,128)} %bitcast.11, bf16[320,320]{1,0:T(8,128)(2,1)} %refs_5_.2), custom_call_target="tpu_custom_call" | custom-call | tf_op jit(solution)/shard_map/pallas_call | solution.py:737
  14.8 0.5 %collective-permute-start = (f32[16,1088]{1,0:T(8,128)S(1)}, f32[16,1088]{1,0:T(8,128)S(1)}, u32[]{:S(2)}, u32[]{:S(2)}) collective-permute-start(f32[16,1088]{1,0:T(8,128)S(1)} %get-tuple-element.28), channel_id=1, source_target_pairs={{0,1},{1,0},{2,3},{3,2},{4,5},{5,4},{6,7},{7,6},{8,9},{9,8},{10,11... | collective-permute-start | bytes 208904 | tf_op jit(solution)/shard_map/ppermute | solution.py:761
  15.3 1.4 %collective-permute-start.1 = (f32[16,1088]{1,0:T(8,128)S(1)}, f32[16,1088]{1,0:T(8,128)S(1)}, u32[]{:S(2)}, u32[]{:S(2)}) collective-permute-start(f32[16,1088]{1,0:T(8,128)S(1)} %get-tuple-element.29), channel_id=1, source_target_pairs={{0,3},{1,2},{2,1},{3,0},{4,7},{5,6},{6,5},{7,4},{8,11},{9,10},{10,... | collective-permute-start | bytes 208904 | tf_op jit(solution)/shard_map/ppermute | solution.py:760
  16.8 0.0 collective-permute-done.from_a
  16.8 2.9 %collective-permute-done.1.from_b = f32[16,1088]{1,0:T(8,128)S(1)} collective-permute-done((f32[16,1088]{1,0:T(8,128)S(1)}, f32[16,1088]{1,0:T(8,128)S(1)}, u32[]{:S(2)}, u32[]{:S(2)}) %collective-permute-start.1) | collective-permute-done | bytes 69664 | tf_op jit(solution)/shard_map/ppermute | solution.py:760
  19.6 0.2 shard_map.79
  19.8 1.8 %collective-permute-start.2 = (f32[16,896]{1,0:T(8,128)S(1)}, f32[16,896]{1,0:T(8,128)S(1)}, u32[]{:S(2)}, u32[]{:S(2)}) collective-permute-start(f32[16,896]{1,0:T(8,128)S(1)} %get-tuple-element.35), channel_id=1, source_target_pairs={{0,4},{4,0},{8,12},{12,8},{16,20},{20,16},{24,28},{28,24},{1,5},{5... | collective-permute-start | bytes 172040 | tf_op jit(solution)/shard_map/ppermute | solution.py:761
  21.6 3.6 %collective-permute-start.3 = (f32[16,896]{1,0:T(8,128)S(1)}, f32[16,896]{1,0:T(8,128)S(1)}, u32[]{:S(2)}, u32[]{:S(2)}) collective-permute-start(f32[16,896]{1,0:T(8,128)S(1)} %get-tuple-element.36), channel_id=1, source_target_pairs={{0,28},{4,8},{8,4},{12,16},{16,12},{20,24},{24,20},{28,0},{1,29},{... | collective-permute-start | bytes 172040 | tf_op jit(solution)/shard_map/ppermute | solution.py:760
  25.2 1.4 %shard_map.78 = (f32[256,320]{1,0:T(8,128)S(1)}, f32[256,320]{1,0:T(8,128)S(1)}, f32[256,320]{1,0:T(8,128)S(1)}, f32[2,4,16,320]{3,2,1,0:T(8,128)S(1)}, bf16[32,...) custom-call(s32[1]{0:T(128)} %bitcast.1.rank.refs_0_, s32[16]{0:T(128)S(1)} %bitcast.17, ...), custom_call_target="tpu_custom_call" | custom-call | tf_op jit(solution)/shard_map/pallas_call | solution.py:737
  26.6 1.9 %collective-permute-done.3.from_b = f32[16,896]{1,0:T(8,128)S(1)} collective-permute-done((f32[16,896]{1,0:T(8,128)S(1)}, f32[16,896]{1,0:T(8,128)S(1)}, u32[]{:S(2)}, u32[]{:S(2)}) %collective-permute-start.3) | collective-permute-done | bytes 57376 | tf_op jit(solution)/shard_map/ppermute | solution.py:760
  28.5 1.0 %shard_map.80 = (f32[256,320]{1,0:T(8,128)S(1)}, f32[32,320]{1,0:T(8,128)S(1)}) custom-call(s32[1]{0:T(128)} %bitcast.place, f32[256,320]{1,0:T(8,128)S(1)} %get-tuple-element.30.field, f32[256,320]{1,0:T(8,128)S(1)} %get-tuple-element.31.second, f32[256,320]{1,0:T(8,128)S(1)} %get-tuple-element.32.known, f32[2,4,16,320]{3,2,1,0:T(8,128)S(1)} %get-tuple-element.33.sides, ...), custom_call_target="tpu_custom_call" | custom-call | tf_op jit(solution)/shard_map/pallas_call | solution.py:737
  29.5 0.0 collective-permute-done.4.refs_8_
  29.6 1.7 %shard_map.82 = (f32[256,320]{1,0:T(8,128)S(1)}, f32[24,321]{1,0:T(8,128)S(1)}, f32[24,321]{1,0:T(8,128)S(1)}, f32[32,321]{1,0:T(8,128)S(1)}, f32[128,320]{1,0:T(8,128)S(1)}) custom-call(s32[1]{0:T(128)} %bitcast.1.rank.refs_0_, f32[256,320]{1,0:T(8,128)S(1)} %get-tuple-element.37.refs_1_, f32[32,320]{1,0:T(8,128)S(1)} %get-tuple-element.38.refs_2_, ...), custom_call_target="tpu_custom_call" | custom-call | tf_op jit(solution)/shard_map/pallas_call | solution.py:737
  31.2 0.0 copy-start.4
  31.3 0.1 collective-permute-start.7
  31.3 1.6 %collective-permute-start.8 = (f32[24,321]{1,0:T(8,128)S(1)}, f32[24,321]{1,0:T(8,128)S(1)}, u32[]{:S(2)}, u32[]{:S(2)}) collective-permute-start(f32[24,321]{1,0:T(8,128)S(1)} %get-tuple-element.45), channel_id=1, source_target_pairs={{0,3},{1,2},{2,1},{3,0},{4,7},{5,6},{6,5},{7,4},{8,11},{9,10},{10,... | collective-permute-start | bytes 92456 | tf_op jit(solution)/shard_map/ppermute | solution.py:760
  33.0 1.8 %collective-permute-done.8.refs_3_.from_b = f32[24,321]{1,0:T(8,128)S(1)} collective-permute-done((f32[24,321]{1,0:T(8,128)S(1)}, f32[24,321]{1,0:T(8,128)S(1)}, u32[]{:S(2)}, u32[]{:S(2)}) %collective-permute-start.8) | collective-permute-done | bytes 30848 | tf_op jit(solution)/shard_map/ppermute | solution.py:760
  34.8 0.1 collective-permute-start.10
  34.9 3.6 %collective-permute-start.11 = (f32[16,320]{1,0:T(8,128)S(1)}, f32[16,320]{1,0:T(8,128)S(1)}, u32[]{:S(2)}, u32[]{:S(2)}) collective-permute-start(f32[16,320]{1,0:T(8,128)S(1)} %get-tuple-element.50.mine_b), channel_id=1, source_target_pairs={{0,28},{4,8},{8,4},{12,16},{16,12},{20,24},{24,20},{28,0},{1,29},{... | collective-permute-start | bytes 61448 | tf_op jit(solution)/shard_map/ppermute | solution.py:760
  38.5 1.5 %collective-permute-start.9 = (f32[8,321]{1,0:T(8,128)S(1)}, f32[8,321]{1,0:T(8,128)S(1)}, u32[]{:S(2)}, u32[]{:S(2)}) collective-permute-start(f32[8,321]{1,0:T(8,128)S(1)} %slice.14), channel_id=1, source_target_pairs={{0,2},{1,3},{2,0},{3,1},{4,6},{5,7},{6,4},{7,5},{8,10},{9,11},{10,... | collective-permute-start | bytes 30824 | tf_op jit(solution)/shard_map/ppermute | solution.py:864
  40.1 2.2 %collective-permute-done.9.refs_11_ = f32[8,321]{1,0:T(8,128)S(1)} collective-permute-done((f32[8,321]{1,0:T(8,128)S(1)}, f32[8,321]{1,0:T(8,128)S(1)}, u32[]{:S(2)}, u32[]{:S(2)}) %collective-permute-start.9) | collective-permute-done | bytes 10304 | tf_op jit(solution)/shard_map/ppermute | solution.py:864
  42.2 2.2 %shard_map.83 = (f32[256,320]{1,0:T(8,128)}, bf16[512,320]{1,0:T(8,128)(2,1)}) custom-call(s32[1]{0:T(128)} %bitcast.1.rank.refs_0_, f32[256,320]{1,0:T(8,128)S(1)} %get-tuple-element.43.refs_1_.partial, f32[24,321]{1,0:T(8,128)S(1)} %collective-permute-done.7.refs_2_.from_a, f32[24,321]{1,0:T(8,128)S(1)} %collective-permute-done.8.refs_3_.from_b, ...), custom_call_target="tpu_custom_call" | custom-call | tf_op jit(solution)/shard_map/pallas_call | solution.py:737
  44.5 0.6 %shard_map.85 = f32[256,320]{1,0:T(8,128)} custom-call(s32[1]{0:T(128)} %bitcast.place, f32[256,320]{1,0:T(8,128)} %get-tuple-element.48.fields_in, f32[16,320]{1,0:T(8,128)S(1)} %get-tuple-element.49.mine_a, f32[16,320]{1,0:T(8,128)S(1)} %get-tuple-element.50.mine_b, f32[16,320]{1,0:T(8,128)S(1)} %collective-permute-done.10.from_a, ...), custom_call_target="tpu_custom_call", output_to_operand_aliasing={{}: (1, {})} | custom-call | tf_op jit(solution)/shard_map/pallas_call | solution.py:737
  (19 shorter events, 0.1 us)
Async XLA Ops:
  0.6 1.0 %copy-start.3 = (bf16[16,32,320]{2,1,0:T(8,128)(2,1)S(1)}, bf16[16,32,320]{2,1,0:T(8,128)(2,1)}, u32[]{:S(2)}) copy-start(bf16[16,32,320]{2,1,0:T(8,128)(2,1)} %param.10) | copy-start | bytes 983044
  1.9 10.8 %collective-permute-start.5 = (f32[640,128]{1,0:T(8,128)S(1)}, f32[640,128]{1,0:T(8,128)S(1)}, u32[]{:S(2)}, u32[]{:S(2)}) collective-permute-start(f32[640,128]{1,0:T(8,128)S(1)} %get-tuple-element.42.refs_9_), channel_id=1, source_target_pairs={{0,2},{1,3},{2,0},{3,1},{4,6},{5,7},{6,4},{7,5},{8,10},{9,11},{10,... | collective-permute-start | bytes 983048 | tf_op jit(solution)/shard_map/ppermute | solution.py:807
  5.0 24.5 %collective-permute-start.4 = (f32[320,128]{1,0:T(8,128)S(1)}, f32[320,128]{1,0:T(8,128)S(1)}, u32[]{:S(2)}, u32[]{:S(2)}) collective-permute-start(f32[320,128]{1,0:T(8,128)S(1)} %get-tuple-element.41.refs_8_), channel_id=1, source_target_pairs={{0,1},{1,0},{2,3},{3,2},{4,5},{5,4},{6,7},{7,6},{8,9},{9,8},{10,11... | collective-permute-start | bytes 491528 | tf_op jit(solution)/shard_map/ppermute | solution.py:808
  12.7 16.8 %collective-permute-start.6 = (f32[320,128]{1,0:T(8,128)S(1)}, f32[320,128]{1,0:T(8,128)S(1)}, u32[]{:S(2)}, u32[]{:S(2)}) collective-permute-start(f32[320,128]{1,0:T(8,128)S(1)} %slice.16), channel_id=1, source_target_pairs={{0,1},{1,0},{2,3},{3,2},{4,5},{5,4},{6,7},{7,6},{8,9},{9,8},{10,11... | collective-permute-start | bytes 491528 | tf_op jit(solution)/shard_map/ppermute | solution.py:831
  12.8 6.8 %copy-start.1 = (f32[16,16,320]{2,1,0:T(8,128)S(1)}, f32[16,16,320]{2,1,0:T(8,128)}, u32[]{:S(2)}) copy-start(f32[16,16,320]{2,1,0:T(8,128)} %param.6) | copy-start | bytes 983044
  12.8 6.8 %copy-start.2 = (f32[16,16,128]{2,1,0:T(8,128)S(1)}, f32[16,16,128]{2,1,0:T(8,128)}, u32[]{:S(2)}) copy-start(f32[16,16,128]{2,1,0:T(8,128)} %param.7) | copy-start | bytes 393220
  14.8 2.0 %collective-permute-start = (f32[16,1088]{1,0:T(8,128)S(1)}, f32[16,1088]{1,0:T(8,128)S(1)}, u32[]{:S(2)}, u32[]{:S(2)}) collective-permute-start(f32[16,1088]{1,0:T(8,128)S(1)} %get-tuple-element.28), channel_id=1, source_target_pairs={{0,1},{1,0},{2,3},{3,2},{4,5},{5,4},{6,7},{7,6},{8,9},{9,8},{10,11... | collective-permute-start | bytes 208904 | tf_op jit(solution)/shard_map/ppermute | solution.py:761
  15.3 4.3 %collective-permute-start.1 = (f32[16,1088]{1,0:T(8,128)S(1)}, f32[16,1088]{1,0:T(8,128)S(1)}, u32[]{:S(2)}, u32[]{:S(2)}) collective-permute-start(f32[16,1088]{1,0:T(8,128)S(1)} %get-tuple-element.29), channel_id=1, source_target_pairs={{0,3},{1,2},{2,1},{3,0},{4,7},{5,6},{6,5},{7,4},{8,11},{9,10},{10,... | collective-permute-start | bytes 208904 | tf_op jit(solution)/shard_map/ppermute | solution.py:760
  19.6 5.6 %copy-start = (bf16[320,320]{1,0:T(8,128)(2,1)S(1)}, bf16[320,320]{1,0:T(8,128)(2,1)}, u32[]{:S(2)}) copy-start(bf16[320,320]{1,0:T(8,128)(2,1)} %refs_5_.2) | copy-start | bytes 614404
  19.8 6.8 %collective-permute-start.2 = (f32[16,896]{1,0:T(8,128)S(1)}, f32[16,896]{1,0:T(8,128)S(1)}, u32[]{:S(2)}, u32[]{:S(2)}) collective-permute-start(f32[16,896]{1,0:T(8,128)S(1)} %get-tuple-element.35), channel_id=1, source_target_pairs={{0,4},{4,0},{8,12},{12,8},{16,20},{20,16},{24,28},{28,24},{1,5},{5... | collective-permute-start | bytes 172040 | tf_op jit(solution)/shard_map/ppermute | solution.py:761
  21.6 3.6 %copy-start.6 = (s32[16,1]{0,1:T(1,128)S(1)}, s32[16,1]{0,1:T(1,128)}, u32[]{:S(2)}) copy-start(s32[16,1]{0,1:T(1,128)} %param.9) | copy-start | bytes 196
  21.6 6.9 %collective-permute-start.3 = (f32[16,896]{1,0:T(8,128)S(1)}, f32[16,896]{1,0:T(8,128)S(1)}, u32[]{:S(2)}, u32[]{:S(2)}) collective-permute-start(f32[16,896]{1,0:T(8,128)S(1)} %get-tuple-element.36), channel_id=1, source_target_pairs={{0,28},{4,8},{8,4},{12,16},{16,12},{20,24},{24,20},{28,0},{1,29},{... | collective-permute-start | bytes 172040 | tf_op jit(solution)/shard_map/ppermute | solution.py:760
  28.5 1.0 %copy-start.5 = (bf16[320,320]{1,0:T(8,128)(2,1)S(1)}, bf16[320,320]{1,0:T(8,128)(2,1)}, u32[]{:S(2)}) copy-start(bf16[320,320]{1,0:T(8,128)(2,1)} %refs_5_.3) | copy-start | bytes 614404
  31.2 11.0 %copy-start.4 = (bf16[16,32,320]{2,1,0:T(8,128)(2,1)S(1)}, bf16[16,32,320]{2,1,0:T(8,128)(2,1)}, u32[]{:S(2)}) copy-start(bf16[16,32,320]{2,1,0:T(8,128)(2,1)} %param.10) | copy-start | bytes 983044
  31.3 1.7 %collective-permute-start.7 = (f32[24,321]{1,0:T(8,128)S(1)}, f32[24,321]{1,0:T(8,128)S(1)}, u32[]{:S(2)}, u32[]{:S(2)}) collective-permute-start(f32[24,321]{1,0:T(8,128)S(1)} %get-tuple-element.44), channel_id=1, source_target_pairs={{0,1},{1,0},{2,3},{3,2},{4,5},{5,4},{6,7},{7,6},{8,9},{9,8},{10,11... | collective-permute-start | bytes 92456 | tf_op jit(solution)/shard_map/ppermute | solution.py:761
  31.3 3.4 %collective-permute-start.8 = (f32[24,321]{1,0:T(8,128)S(1)}, f32[24,321]{1,0:T(8,128)S(1)}, u32[]{:S(2)}, u32[]{:S(2)}) collective-permute-start(f32[24,321]{1,0:T(8,128)S(1)} %get-tuple-element.45), channel_id=1, source_target_pairs={{0,3},{1,2},{2,1},{3,0},{4,7},{5,6},{6,5},{7,4},{8,11},{9,10},{10,... | collective-permute-start | bytes 92456 | tf_op jit(solution)/shard_map/ppermute | solution.py:760
  34.8 9.6 %collective-permute-start.10 = (f32[16,320]{1,0:T(8,128)S(1)}, f32[16,320]{1,0:T(8,128)S(1)}, u32[]{:S(2)}, u32[]{:S(2)}) collective-permute-start(f32[16,320]{1,0:T(8,128)S(1)} %get-tuple-element.49.mine_a), channel_id=1, source_target_pairs={{0,4},{4,0},{8,12},{12,8},{16,20},{20,16},{24,28},{28,24},{1,5},{5... | collective-permute-start | bytes 61448 | tf_op jit(solution)/shard_map/ppermute | solution.py:761
  34.9 9.6 %collective-permute-start.11 = (f32[16,320]{1,0:T(8,128)S(1)}, f32[16,320]{1,0:T(8,128)S(1)}, u32[]{:S(2)}, u32[]{:S(2)}) collective-permute-start(f32[16,320]{1,0:T(8,128)S(1)} %get-tuple-element.50.mine_b), channel_id=1, source_target_pairs={{0,28},{4,8},{8,4},{12,16},{16,12},{20,24},{24,20},{28,0},{1,29},{... | collective-permute-start | bytes 61448 | tf_op jit(solution)/shard_map/ppermute | solution.py:760
  38.5 3.7 %collective-permute-start.9 = (f32[8,321]{1,0:T(8,128)S(1)}, f32[8,321]{1,0:T(8,128)S(1)}, u32[]{:S(2)}, u32[]{:S(2)}) collective-permute-start(f32[8,321]{1,0:T(8,128)S(1)} %slice.14), channel_id=1, source_target_pairs={{0,2},{1,3},{2,0},{3,1},{4,6},{5,7},{6,4},{7,5},{8,10},{9,11},{10,... | collective-permute-start | bytes 30824 | tf_op jit(solution)/shard_map/ppermute | solution.py:864

commit v2 on v1

--- a/solution.py
+++ b/solution.py
@@ -134,7 +134,7 @@
 
 
 def local_update(base_ref, field_ref, mix, wind_ref, out_ref, size_x, size_y, levels, average,
-                 mixed_ref=None):
+                 mixed_ref=None, change_ref=None):
     channels = field_ref.shape[1]
     table = sublane_coefficients(2 * levels)
     strip = NODES * size_y
@@ -157,6 +157,8 @@
                     + mixed[i * size_y : (i + 1) * size_y, begin:end]
                     - (along_x * slopes[i] + along_y * dsub(values[i], table))
                 )
+                if change_ref is not None:
+                    result = result + change_ref[pl.ds(element * size_y, size_y), begin:end]
                 out_ref[rows[i], begin:end] = sub_average(result) if average else result
 
 
@@ -175,11 +177,23 @@
 
 
 def column_parts(message, channels, levels):
+    span = 2 * channels + 2 * levels
+    tiles = lane_tiles(channels, 128)
+    slopes = [
+        jnp.concatenate(
+            [
+                message[end * len(tiles) + p : end * len(tiles) + p + 1, span : span + last - first]
+                for p, (first, last) in enumerate(tiles)
+            ],
+            axis=1,
+        )
+        for end in range(2)
+    ]
     return (
         message[:, 0:channels],
         message[:, channels : 2 * channels],
-        message[:, 2 * channels : 3 * channels],
-        message[:, 3 * channels : 3 * channels + 2 * levels],
+        message[:, 2 * channels : span],
+        slopes,
     )
 
 
@@ -221,10 +235,20 @@
         for j in range(NODES):
             term = DERIV[row][j] * values[j]
             slope = term if slope is None else slope + term
+        pair = column_of(wind, column, size_x, size_y)
+        _, along_y = full_winds(pair, levels, channels)
+        span = 2 * channels + 2 * levels
         out[:, 0:channels] = values[row]
-        out[:, channels : 2 * channels] = slope
-        out[:, 2 * channels : 3 * channels] = column_of(state, column, size_x, size_y)
-        out[:, 3 * channels : 3 * channels + 2 * levels] = column_of(wind, column, size_x, size_y)
+        out[:, channels : 2 * channels] = (
+            column_of(state, column, size_x, size_y) - along_y * slope
+        )
+        out[:, 2 * channels : span] = pair
+        out[:, span : span + 128] = jnp.zeros((size_x, 128), jnp.float32)
+        tiles = lane_tiles(channels, 128)
+        for end, x in enumerate((0, size_x - 1)):
+            for piece, (first, last) in enumerate(tiles):
+                at = end * len(tiles) + piece
+                out[at : at + 1, span : span + last - first] = slope[x : x + 1, first:last]
     even = is_even(rank)
     to_a[...] = jnp.where(even, message[1], message[0])
     to_b[...] = jnp.where(even, message[0], message[1])
@@ -249,11 +273,15 @@
     channels = state.shape[1]
     from_left, from_right = in_order(rank, from_a, from_b)
     to_up, to_down = message.at[0], message.at[1]
-    left_value, left_slope, left_state, left_wind = column_parts(from_left, channels, levels)
-    right_value, right_slope, right_state, right_wind = column_parts(from_right, channels, levels)
+    left_value, left_part, left_wind, left_slopes = column_parts(from_left, channels, levels)
+    right_value, right_part, right_wind, right_slopes = column_parts(
+        from_right, channels, levels
+    )
     span = 2 * channels + 2 * levels
     pieces = span // (2 * levels)
-    for out, x, near, kind in ((to_up, 0, 0, 0), (to_down, size_x - 1, size_x - NODES, 3)):
+    for end, (out, x, near, kind) in enumerate(
+        ((to_up, 0, 0, 0), (to_down, size_x - 1, size_x - NODES, 3))
+    ):
         slope = None
         for j in range(NODES):
             value = partial[pl.ds((near + j) * size_y, size_y), :]
@@ -271,20 +299,21 @@
         out[:, channels : 2 * channels] = state[row, :] - along_x * slope
         out[:, 2 * channels : span] = wind[row, :]
         corners = (
-            (left_slope[x : x + 1] - LAST * changes[0], left_state, left_wind, slope[0:1]),
+            (left_slopes[end], LAST * changes[0], left_part, left_wind, slope[0:1]),
             (
-                right_slope[x : x + 1] - FIRST * changes[1],
-                right_state,
+                right_slopes[end],
+                FIRST * changes[1],
+                right_part,
                 right_wind,
                 slope[size_y - 1 : size_y],
             ),
         )
-        for side, (side_slope, side_state, side_wind, corner_slope) in enumerate(corners):
+        for side, (side_slope, fix, side_part, side_wind, corner_slope) in enumerate(corners):
             pair = side_wind[x : x + 1]
-            corner_x, _ = full_winds(pair, levels, channels)
-            line[side : side + 1, 0:channels] = side_slope
+            corner_x, corner_y = full_winds(pair, levels, channels)
+            line[side : side + 1, 0:channels] = side_slope - fix
             line[side : side + 1, channels : 2 * channels] = (
-                side_state[x : x + 1] - corner_x * corner_slope
+                side_part[x : x + 1] + corner_y * side_slope - corner_x * corner_slope
             )
             line[side : side + 1, 2 * channels : span] = pair
             for piece in range(pieces):
@@ -328,19 +357,19 @@
     for side, (message, y, change, factor) in enumerate(
         ((from_left, 0, left, LAST), (from_right, size_y - 1, right, FIRST))
     ):
-        _, slope, side_state, side_wind = column_parts(message, channels, levels)
-        slope = slope - factor * change
+        _, side_part, side_wind, slopes = column_parts(message, channels, levels)
         along_x, along_y = full_winds(side_wind, levels, channels)
-        beyond = (
-            side_state
+        sides[side, 0] = (
+            side_part
             + column_of(mixed, y, size_x, size_y)
-            - (
-                along_x * dsub(column_of(field, y, size_x, size_y), table)
-                + along_y * slope
-            )
-        )
-        sides[side, 0] = beyond
-        sides[side, 1] = slope
+            - along_x * dsub(column_of(field, y, size_x, size_y), table)
+            + factor * (along_y * change)
+        )
+        sides[side, 1] = end_rows(
+            size_x,
+            slopes[0] - factor * change[0:1],
+            slopes[1] - factor * change[size_x - 1 : size_x],
+        )
         sides[side, 2] = along_x
         sides[side, 3] = along_y
 
@@ -406,23 +435,17 @@
 
 
 def widen_kernel(groups, rank, states, *refs):
-    own, near = refs[:2]
-    pairs = refs[2 : 1 + groups // 2]
-    turned = refs[-1]
+    own, outs, turned = refs[0], refs[1:groups], refs[groups]
     rows, channels = own.shape
-    length = near.shape[0]
     for k in range(groups):
         start = pl.multiple_of((rank[0] ^ k) * rows, rows)
         tile = interleave(states, start, channels, turned.at[k], rows)
-        if k == 0:
+        if k:
+            pack(tile, channels, outs[k - 1], rows)
+        else:
             for t in range(rows // 8):
                 for lane, (begin, end) in enumerate(lane_tiles(channels, 128)):
                     own[8 * t : 8 * t + 8, begin:end] = tile(t, lane)[:, : end - begin]
-        elif k == 1:
-            pack(tile, channels, near, rows)
-        else:
-            at = (k & 1) * length
-            pack(tile, channels, pairs[k // 2 - 1].at[at : at + length], rows)
 
 
 def cloud_run(states, blocks, forcing, mix, rows, parts, tendency, finals):
@@ -500,7 +523,7 @@
 
 
 def second_kernel(size_x, size_y, levels, place, field, second, known, sides, gather, wind, mix,
-                  from_a, from_b, work, forcing, total, reduced):
+                  from_a, from_b, total, work, forcing, reduced):
     from_up, from_down = in_order(place, from_a, from_b)
     channels = field.shape[1]
     span = 2 * channels + 2 * levels
@@ -600,47 +623,68 @@
             value = term if value is None else value + term
         reduced[pl.ds(element * size_y, size_y), :] = weight * value
     forcing[...] = select_rows(gather[...], reduced[...])
-    local_update(total, total, mix[...], wind, work, size_x, size_y, levels, False)
+    ends = [
+        [column_of(total, near + j, size_x, size_y) for j in range(NODES)]
+        for near in (0, size_y - NODES)
+    ]
+    remixed = mix_all(jnp.concatenate([ends[0][0], ends[1][3]], axis=0), mix[...])
+    for side, (y, kind) in enumerate(((0, 0), (size_y - 1, 3))):
+        slope = None
+        for j in range(NODES):
+            term = DERIV[kind][j] * ends[side][j]
+            slope = term if slope is None else slope + term
+        along_x, along_y = full_winds(column_of(wind, y, size_x, size_y), levels, channels)
+        column = ends[side][kind]
+        work[side] = (
+            column
+            + remixed[side * size_x : (side + 1) * size_x]
+            - (along_x * dsub(column, small) + along_y * slope)
+        )
 
 
 def home_kernel(size_x, size_y, groups, capacity, *refs):
-    rank, work, forcing, gather, spread, mix, cloud_mix, own, near, far = refs[:10]
-    pairs = refs[10 : 9 + groups // 2]
-    out, to_a, to_b, sends, own_final = refs[9 + groups // 2 : 14 + groups // 2]
-    reduced, tendency, cloud, message = refs[14 + groups // 2 :]
-    channels = work.shape[1]
+    rank, edges, forcing, gather, spread, mix, cloud_mix, own = refs[:8]
+    arrived = refs[8 : 7 + groups]
+    out, to_a, to_b, sends, own_final = refs[7 + groups : 12 + groups]
+    tendency, cloud, message = refs[12 + groups :]
+    channels = forcing.shape[1]
     parts = 8 // capacity
     rows = own.shape[0]
-    length = near.shape[0]
     cloud[0:rows, :] = own[...]
-    unpack(near, channels, cloud, rows, rows)
-    for m in range(1, groups // 2):
-        unpack(pairs[m - 1].at[0:length], channels, cloud, 2 * m * rows, rows)
-        unpack(
-            far.at[(m - 1) * length : m * length], channels, cloud, (2 * m + 1) * rows, rows
-        )
+    for k in range(1, groups):
+        unpack(arrived[k - 1], channels, cloud, k * rows, rows)
     cloud_run(
         cloud, range(groups), forcing, cloud_mix, rows, parts, tendency, (0,)
     )
     own_final[...] = cloud[0:rows, :]
     tend = tendency[...]
     change = COUPLING * (tend + mix_all(tend, mix[...]))
-    reduced[...] = select_rows(spread[...], change)
-    for x in range(size_x):
-        row = pl.ds(x * size_y, size_y)
-        element = pl.ds((x // NODES) * size_y, size_y)
-        out[row, :] = sub_average(work[row, :] + reduced[element, :])
-    average_rows(out, size_x, size_y)
+    out[...] = select_rows(spread[...], change)
     occupied = jnp.max(gather[...].astype(jnp.float32), axis=1, keepdims=True)
     sends[:, 0:channels] = forcing[...]
     sends[:, channels : channels + 1] = occupied
-    message[0] = column_of(out, 0, size_x, size_y)
-    message[1] = column_of(out, size_y - 1, size_x, size_y)
+    for side, y in ((0, 0), (1, size_y - 1)):
+        own_change = jnp.concatenate(
+            [
+                jnp.broadcast_to(
+                    out[(x // NODES) * size_y + y : (x // NODES) * size_y + y + 1, :],
+                    (NODES, channels),
+                )
+                for x in range(0, size_x, NODES)
+            ],
+            axis=0,
+        )
+        message[side] = sub_average(edges[side] + own_change)
     even = is_even(rank)
     to_a[0:size_x, 0:channels] = jnp.where(even, message[1], message[0])
     to_b[0:size_x, 0:channels] = jnp.where(even, message[0], message[1])
     to_a[size_x : size_x + 8, :] = sends[8:16, :]
     to_b[size_x : size_x + 8, :] = sends[8 * groups - 8 : 8 * groups, :]
+
+
+def fields_kernel(size_x, size_y, levels, second, wind, mix, change, out):
+    local_update(second, second, mix[...], wind, out, size_x, size_y, levels, True, None, change)
+    average_rows(out, size_x, size_y)
 
 
 def last_turn_kernel(size_x, size_y, rank, place, partial, from_a, from_b, to_a, to_b, ends):
@@ -659,14 +703,13 @@
 
 
 def owner_kernel(size_x, size_y, groups, capacity, *refs):
-    rank, partial, from_a, from_b, states, mix, own_final, sends, near = refs[:9]
-    pairs = refs[9 : 8 + groups // 2]
-    forcings = refs[8 + groups // 2 : 7 + groups // 2 + groups]
-    fields, out, field, cloud, forcing, turned, ready, done = refs[7 + groups // 2 + groups :]
+    rank, partial, from_a, from_b, states, mix, own_final, sends = refs[:8]
+    wide = refs[8 : 7 + groups]
+    forcings = refs[7 + groups : 6 + 2 * groups]
+    fields, out, field, cloud, forcing, turned, ready, done = refs[6 + 2 * groups :]
     channels = partial.shape[1]
     parts = 8 // capacity
     rows = own_final.shape[0]
-    length = near.shape[0]
     from_left, from_right = in_order(rank, from_a, from_b)
     left, right = side_changes(size_x, size_y, partial, from_left, from_right)
     for x in range(size_x):
@@ -674,11 +717,8 @@
         field[row, :] = edge_rows(partial[row, :], left[x : x + 1], right[x : x + 1])
     copies = [pltpu.make_async_copy(field, fields, done.at[groups])]
     copies[0].start()
-    unpack(near, channels, cloud, 0, rows)
-    forcing[0:8, :] = forcings[0][:, 0:channels]
-    for k in range(2, groups):
-        at = (k & 1) * length
-        unpack(pairs[k // 2 - 1].at[at : at + length], channels, cloud, (k - 1) * rows, rows)
+    for k in range(1, groups):
+        unpack(wide[k - 1], channels, cloud, (k - 1) * rows, rows)
         forcing[8 * (k - 1) : 8 * k, :] = forcings[k - 1][:, 0:channels]
     blocks = tuple(range(groups - 1))
     cloud_run(cloud, blocks, forcing, mix, rows, parts, None, blocks)
@@ -782,7 +822,7 @@
     grid = ((nodes, channels), f32)
     xor = [[(i, i ^ k) for i in range(groups)] for k in range(groups)]
 
-    column_message = ((size_x, 3 * channels + 2 * levels), f32)
+    column_message = ((size_x, 2 * channels + 2 * levels + 128), f32)
     partial, to_a, to_b = call(
         functools.partial(begin_kernel, size_x, size_y, levels),
         [grid, column_message, column_message],
@@ -796,16 +836,14 @@
     column_a, column_b = ring(to_a, to_b, "crm")
 
     length = packing(rows, channels)[2]
-    own, near, *pairs = call(
+    own, *wide = call(
         functools.partial(widen_kernel, groups),
-        [((rows, channels), f32), ((length, 128), f32)]
-        + [((2 * length, 128), f32)] * (groups // 2 - 1),
+        [((rows, channels), f32)] + [((length, 128), f32)] * (groups - 1),
         [((groups, lane_count, rows, 128), f32)],
         rank, clouds,
         smem=(0,),
     )
-    pairs_in = [lax.ppermute(pairs[m - 1], "crm", xor[2 * m]) for m in range(1, groups // 2)]
-    near_in = lax.ppermute(near, "crm", xor[1])
+    arrived = [lax.ppermute(wide[k - 1], "crm", xor[k]) for k in range(1, groups)]
 
     span = 2 * channels + 2 * levels
     row_message = ((size_y, span + 2 * levels), f32)
@@ -828,27 +866,23 @@
         rank, owners, partial, state, wind, dyn_mix, column_a, column_b,
         smem=(0, 1),
     )
-    far_in = lax.ppermute(
-        jnp.concatenate([value[length:] for value in pairs_in], axis=0), "crm", xor[1]
-    )
-    work, forcing = call(
+    second, edges, forcing = call(
         functools.partial(second_kernel, size_x, size_y, levels),
-        [grid, ((8 * groups, channels), f32)],
-        [grid, ((elements * size_y, channels), f32)],
+        [grid, ((2, size_x, channels), f32), ((8 * groups, channels), f32)],
+        [((elements * size_y, channels), f32)],
         place, field, total, known, sides, gather, wind, dyn_mix, row_a, row_b,
         smem=(0,),
     )
     edge = ((size_x + 8, channels + 1), f32)
-    partial, to_a, to_b, sends, own_final = call(
+    change, to_a, to_b, sends, own_final = call(
         functools.partial(home_kernel, size_x, size_y, groups, capacity),
-        [grid, edge, edge, ((8 * groups, channels + 1), f32), ((rows, channels), f32)],
+        [((elements * size_y, channels), f32), edge, edge, ((8 * groups, channels + 1), f32), ((rows, channels), f32)],
         [
-            ((elements * size_y, channels), f32),
             ((8 * groups, channels), f32),
             ((groups * rows, channels), f32),
             ((2, size_x, channels), f32),
         ],
-        rank, work, forcing, gather, spread, dyn_mix, crm_mix, own, near_in, far_in, *pairs_in,
+        rank, edges, forcing, gather, spread, dyn_mix, crm_mix, own, *arrived,
         smem=(0,),
     )
 
@@ -862,6 +896,12 @@
             forcings.append(column_b[size_x:])
         else:
             forcings.append(lax.ppermute(sends[8 * k : 8 * k + 8], "crm", xor[k]))
+    (partial,) = call(
+        functools.partial(fields_kernel, size_x, size_y, levels),
+        [grid],
+        [],
+        second, wind, dyn_mix, change,
+    )
     mine_a, mine_b = call(
         functools.partial(last_turn_kernel, size_x, size_y),
         [((size_y, channels), f32)] * 2,
@@ -881,8 +921,8 @@
             ((groups, rows, channels), clouds.dtype),
             DMA((groups + 1,)),
         ],
-        rank, partial, column_a, column_b, clouds, crm_mix, own_final, sends, near,
-        *pairs, *forcings,
+        rank, partial, column_a, column_b, clouds, crm_mix, own_final, sends,
+        *wide, *forcings,
         smem=(0,),
         far_out=(0, 1),
     )

time: 45.3 us -> 39.5 us (0.87)
  waiting for transfers between devices: 16.5 us -> 10.5 us
    ppermute x3, waiting for transfers between devices: 7.71 us -> 0.01 us  [on_device(): lax.ppermute(wide[k - 1], 'crm', xor[k])]
    ppermute x4, waiting for transfers between devices: 6.56 us -> 8.36 us  [ring(): from_b = lax.ppermute(to_b, axis, upper_pairs(count))]
    ppermute x4, starting transfers between devices: 2.49 us -> 1.86 us  [ring(): from_a = lax.ppermute(to_a, axis, lower_pairs(count))]
    pallas_call x9 -> x10, Pallas kernels: 9.41 us -> 9.69 us  [call(): pl.pallas_call(kernel, out_shape=[jax.ShapeDtypeStruct(shape, dtype) for...]
  transfers between devices with their start and end apart: 12 -> 12, of which waited for: 5 -> 4; matrix products, arithmetic and copies ran while one was open for 0% -> 0% of each run, Pallas kernels for 15% -> 18%
where the time goes in v2:
time: 39.5 us; the launch traced here: 39.3 us
  starting transfers between devices  17.1 us (43%)
  waiting for transfers between devices  10.5 us (27%)
  Pallas kernels  9.69 us (25%)
  local copies, waits for them, and re-layouts  1.17 us (3%)
  between operations  0.79 us (2%)
    ppermute x4, starting transfers between devices, ring(): from_b = lax.ppermute(to_b, axis, upper_pairs(count))  10.5 us
    pallas_call x10, Pallas kernels, call(): pl.pallas_call(kernel, out_shape=[jax.ShapeDtypeStruct(shape, dtype) for...  9.69 us
    ppermute x4, waiting for transfers between devices, ring(): from_b = lax.ppermute(to_b, axis, upper_pairs(count))  8.36 us
    ppermute x3, starting transfers between devices, on_device(): lax.ppermute(wide[k - 1], 'crm', xor[k])  3.18 us
    ppermute x1, waiting for transfers between devices, on_device(): forcings.append(lax.ppermute(sends[8 * k:8 * k + 8], 'crm', xor[k]))  2.17 us
    ppermute x4, starting transfers between devices, ring(): from_a = lax.ppermute(to_a, axis, lower_pairs(count))  1.86 us
    ppermute x1, starting transfers between devices, on_device(): forcings.append(lax.ppermute(sends[8 * k:8 * k + 8], 'crm', xor[k]))  1.52 us
    unnamed x14, local copies, waits for them, and re-layouts  1.17 us
  transfers between devices with their start and end apart: 12, of which 4 were waited for; matrix products, arithmetic and copies ran while one was open for 0% of the time, Pallas kernels for 18%

profile of v2, /device:TPU:0, one launch (start us, length us, event | category | flops | bytes accessed | tf_op | source)
XLA Modules:
  0.0 39.3 jit_solution(5339704570672596071)
XLA Ops:
  0.6 0.0 copy-start.3
  0.6 1.0 %copy-done.3 = bf16[16,32,320]{2,1,0:T(8,128)(2,1)S(1)} copy-done((bf16[16,32,320]{2,1,0:T(8,128)(2,1)S(1)}, bf16[16,32,320]{2,1,0:T(8,128)(2,1)}, u32[]{:S(2)}) %copy-start.3) | copy-done | bytes 327704
  1.6 0.3 shard_map.81
  1.9 0.6 %collective-permute-start.4 = (f32[320,128]{1,0:T(8,128)S(1)}, f32[320,128]{1,0:T(8,128)S(1)}, u32[]{:S(2)}, u32[]{:S(2)}) collective-permute-start(f32[320,128]{1,0:T(8,128)S(1)} %get-tuple-element.44.refs_8_), channel_id=1, source_target_pairs={{0,1},{1,0},{2,3},{3,2},{4,5},{5,4},{6,7},{7,6},{8,9},{9,8},{10,11... | collective-permute-start | bytes 491528 | tf_op jit(solution)/shard_map/ppermute | solution.py:846
  2.5 2.6 %collective-permute-start.5 = (f32[320,128]{1,0:T(8,128)S(1)}, f32[320,128]{1,0:T(8,128)S(1)}, u32[]{:S(2)}, u32[]{:S(2)}) collective-permute-start(f32[320,128]{1,0:T(8,128)S(1)} %get-tuple-element.45.refs_9_), channel_id=1, source_target_pairs={{0,2},{1,3},{2,0},{3,1},{4,6},{5,7},{6,4},{7,5},{8,10},{9,11},{10,... | collective-permute-start | bytes 491528 | tf_op jit(solution)/shard_map/ppermute | solution.py:846
  5.1 0.0 collective-permute-start.6
  5.1 2.0 %shard_map.77 = (f32[256,320]{1,0:T(8,128)S(1)}, f32[16,896]{1,0:T(8,128)S(1)}, f32[16,896]{1,0:T(8,128)S(1)}) custom-call(s32[1]{0:T(128)} %bitcast.1.rank.refs_0_, f32[256,320]{1,0:T(8,128)} %bitcast.8, f32[256,128]{1,0:T(8,128)} %bitcast.11, bf16[320,320]{1,0:T(8,128)(2,1)} %mix.5), custom_call_target="tpu_custom_call" | custom-call | tf_op jit(solution)/shard_map/pallas_call | solution.py:777
  7.1 0.2 collective-permute-start
  7.3 1.7 %collective-permute-start.1 = (f32[16,896]{1,0:T(8,128)S(1)}, f32[16,896]{1,0:T(8,128)S(1)}, u32[]{:S(2)}, u32[]{:S(2)}) collective-permute-start(f32[16,896]{1,0:T(8,128)S(1)} %get-tuple-element.31), channel_id=1, source_target_pairs={{0,3},{1,2},{2,1},{3,0},{4,7},{5,6},{6,5},{7,4},{8,11},{9,10},{10,... | collective-permute-start | bytes 172040 | tf_op jit(solution)/shard_map/ppermute | solution.py:800
  9.0 5.3 %collective-permute-done.1.from_b = f32[16,896]{1,0:T(8,128)S(1)} collective-permute-done((f32[16,896]{1,0:T(8,128)S(1)}, f32[16,896]{1,0:T(8,128)S(1)}, u32[]{:S(2)}, u32[]{:S(2)}) %collective-permute-start.1) | collective-permute-done | bytes 57376 | tf_op jit(solution)/shard_map/ppermute | solution.py:800
  14.3 0.2 shard_map.79
  14.5 1.5 %collective-permute-start.2 = (f32[16,896]{1,0:T(8,128)S(1)}, f32[16,896]{1,0:T(8,128)S(1)}, u32[]{:S(2)}, u32[]{:S(2)}) collective-permute-start(f32[16,896]{1,0:T(8,128)S(1)} %get-tuple-element.37), channel_id=1, source_target_pairs={{0,4},{4,0},{8,12},{12,8},{16,20},{20,16},{24,28},{28,24},{1,5},{5... | collective-permute-start | bytes 172040 | tf_op jit(solution)/shard_map/ppermute | solution.py:801
  16.1 3.6 %collective-permute-start.3 = (f32[16,896]{1,0:T(8,128)S(1)}, f32[16,896]{1,0:T(8,128)S(1)}, u32[]{:S(2)}, u32[]{:S(2)}) collective-permute-start(f32[16,896]{1,0:T(8,128)S(1)} %get-tuple-element.38), channel_id=1, source_target_pairs={{0,28},{4,8},{8,4},{12,16},{16,12},{20,24},{24,20},{28,0},{1,29},{... | collective-permute-start | bytes 172040 | tf_op jit(solution)/shard_map/ppermute | solution.py:800
  19.6 1.4 %shard_map.78 = (f32[256,320]{1,0:T(8,128)S(1)}, f32[256,320]{1,0:T(8,128)S(1)}, f32[256,320]{1,0:T(8,128)S(1)}, f32[2,4,16,320]{3,2,1,0:T(8,128)S(1)}, bf16[32,...) custom-call(s32[1]{0:T(128)} %bitcast.1.rank.refs_0_, s32[16]{0:T(128)S(1)} %bitcast.18, ...), custom_call_target="tpu_custom_call" | custom-call | tf_op jit(solution)/shard_map/pallas_call | solution.py:777
  21.1 0.0 collective-permute-done.2.from_a
  21.1 1.9 %collective-permute-done.3.from_b = f32[16,896]{1,0:T(8,128)S(1)} collective-permute-done((f32[16,896]{1,0:T(8,128)S(1)}, f32[16,896]{1,0:T(8,128)S(1)}, u32[]{:S(2)}, u32[]{:S(2)}) %collective-permute-start.3) | collective-permute-done | bytes 57376 | tf_op jit(solution)/shard_map/ppermute | solution.py:800
  22.9 0.7 %shard_map.80 = (f32[256,320]{1,0:T(8,128)S(1)}, f32[2,16,320]{2,1,0:T(8,128)S(1)}, f32[32,320]{1,0:T(8,128)S(1)}) custom-call(s32[1]{0:T(128)} %bitcast.place, f32[256,320]{1,0:T(8,128)S(1)} %get-tuple-element.32.field, f32[256,320]{1,0:T(8,128)S(1)} %get-tuple-element.33.second, f32[256,320]{1,0:T(8,128)S(1)} %get-tuple-element.34.known, ...), custom_call_target="tpu_custom_call" | custom-call | tf_op jit(solution)/shard_map/pallas_call | solution.py:777
  23.7 0.0 collective-permute-done.5.refs_9_
  23.7 0.0 collective-permute-done.6.refs_10_
  23.7 0.2 copy-done.5
  23.9 1.6 %shard_map.82 = (f32[64,320]{1,0:T(8,128)S(1)}, f32[24,321]{1,0:T(8,128)S(1)}, f32[24,321]{1,0:T(8,128)S(1)}, f32[32,321]{1,0:T(8,128)S(1)}, f32[128,320]{1,0:T(8,128)S(1)}) custom-call(s32[1]{0:T(128)} %bitcast.1.rank.refs_0_, f32[2,16,320]{2,1,0:T(8,128)S(1)} %get-tuple-element.40.refs_1_, f32[32,320]{1,0:T(8,128)S(1)} %get-tuple-element.41.refs_2_, ...), custom_call_target="tpu_custom_call" | custom-call | tf_op jit(solution)/shard_map/pallas_call | solution.py:777
  25.5 0.1 collective-permute-start.7
  25.5 1.6 %collective-permute-start.8 = (f32[24,321]{1,0:T(8,128)S(1)}, f32[24,321]{1,0:T(8,128)S(1)}, u32[]{:S(2)}, u32[]{:S(2)}) collective-permute-start(f32[24,321]{1,0:T(8,128)S(1)} %get-tuple-element.49), channel_id=1, source_target_pairs={{0,3},{1,2},{2,1},{3,0},{4,7},{5,6},{6,5},{7,4},{8,11},{9,10},{10,... | collective-permute-start | bytes 92456 | tf_op jit(solution)/shard_map/ppermute | solution.py:800
  27.2 0.6 %shard_map.83.refs_1_.partial = f32[256,320]{1,0:T(8,128)S(1)} custom-call(f32[256,320]{1,0:T(8,128)S(1)} %get-tuple-element.39.second, f32[256,128]{1,0:T(8,128)S(1)} %bitcast.15, bf16[320,320]{1,0:T(8,128)(2,1)S(1)} %copy-done, f32[64,320]{1,0:T(8,128)S(1)} %get-tuple-element.47.change), custom_call_target="tpu_custom_call" | custom-call | tf_op jit(solution)/shard_map/pallas_call | solution.py:777
  27.8 0.0 copy-start.4
  27.8 1.2 %collective-permute-done.8.refs_3_.from_b = f32[24,321]{1,0:T(8,128)S(1)} collective-permute-done((f32[24,321]{1,0:T(8,128)S(1)}, f32[24,321]{1,0:T(8,128)S(1)}, u32[]{:S(2)}, u32[]{:S(2)}) %collective-permute-start.8) | collective-permute-done | bytes 30848 | tf_op jit(solution)/shard_map/ppermute | solution.py:800
  29.0 0.1 collective-permute-start.10
  29.1 3.6 %collective-permute-start.11 = (f32[16,320]{1,0:T(8,128)S(1)}, f32[16,320]{1,0:T(8,128)S(1)}, u32[]{:S(2)}, u32[]{:S(2)}) collective-permute-start(f32[16,320]{1,0:T(8,128)S(1)} %get-tuple-element.54.mine_b), channel_id=1, source_target_pairs={{0,28},{4,8},{8,4},{12,16},{16,12},{20,24},{24,20},{28,0},{1,29},{... | collective-permute-start | bytes 61448 | tf_op jit(solution)/shard_map/ppermute | solution.py:800
  32.7 1.5 %collective-permute-start.9 = (f32[8,321]{1,0:T(8,128)S(1)}, f32[8,321]{1,0:T(8,128)S(1)}, u32[]{:S(2)}, u32[]{:S(2)}) collective-permute-start(f32[8,321]{1,0:T(8,128)S(1)} %slice.10), channel_id=1, source_target_pairs={{0,2},{1,3},{2,0},{3,1},{4,6},{5,7},{6,4},{7,5},{8,10},{9,11},{10,... | collective-permute-start | bytes 30824 | tf_op jit(solution)/shard_map/ppermute | solution.py:898
  34.3 2.2 %collective-permute-done.9.refs_12_ = f32[8,321]{1,0:T(8,128)S(1)} collective-permute-done((f32[8,321]{1,0:T(8,128)S(1)}, f32[8,321]{1,0:T(8,128)S(1)}, u32[]{:S(2)}, u32[]{:S(2)}) %collective-permute-start.9) | collective-permute-done | bytes 10304 | tf_op jit(solution)/shard_map/ppermute | solution.py:898
  36.4 2.2 %shard_map.84 = (f32[256,320]{1,0:T(8,128)}, bf16[512,320]{1,0:T(8,128)(2,1)}) custom-call(s32[1]{0:T(128)} %bitcast.1.rank.refs_0_, f32[256,320]{1,0:T(8,128)S(1)} %shard_map.83.refs_1_.partial, f32[24,321]{1,0:T(8,128)S(1)} %collective-permute-done.7.refs_2_.from_a, f32[24,321]{1,0:T(8,128)S(1)} %collective-permute-done.8.refs_3_.from_b, ...), custom_call_target="tpu_custom_call" | custom-call | tf_op jit(solution)/shard_map/pallas_call | solution.py:777
  38.7 0.6 %shard_map.86 = f32[256,320]{1,0:T(8,128)} custom-call(s32[1]{0:T(128)} %bitcast.place, f32[256,320]{1,0:T(8,128)} %get-tuple-element.52.fields_in, f32[16,320]{1,0:T(8,128)S(1)} %get-tuple-element.53.mine_a, f32[16,320]{1,0:T(8,128)S(1)} %get-tuple-element.54.mine_b, f32[16,320]{1,0:T(8,128)S(1)} %collective-permute-done.10.from_a, ...), custom_call_target="tpu_custom_call", output_to_operand_aliasing={{}: (1, {})} | custom-call | tf_op jit(solution)/shard_map/pallas_call | solution.py:777
  (19 shorter events, 0.1 us)
Async XLA Ops:
  0.6 1.0 %copy-start.3 = (bf16[16,32,320]{2,1,0:T(8,128)(2,1)S(1)}, bf16[16,32,320]{2,1,0:T(8,128)(2,1)}, u32[]{:S(2)}) copy-start(bf16[16,32,320]{2,1,0:T(8,128)(2,1)} %param.10) | copy-start | bytes 983044
  1.9 21.8 %collective-permute-start.4 = (f32[320,128]{1,0:T(8,128)S(1)}, f32[320,128]{1,0:T(8,128)S(1)}, u32[]{:S(2)}, u32[]{:S(2)}) collective-permute-start(f32[320,128]{1,0:T(8,128)S(1)} %get-tuple-element.44.refs_8_), channel_id=1, source_target_pairs={{0,1},{1,0},{2,3},{3,2},{4,5},{5,4},{6,7},{7,6},{8,9},{9,8},{10,11... | collective-permute-start | bytes 491528 | tf_op jit(solution)/shard_map/ppermute | solution.py:846
  2.5 21.2 %collective-permute-start.5 = (f32[320,128]{1,0:T(8,128)S(1)}, f32[320,128]{1,0:T(8,128)S(1)}, u32[]{:S(2)}, u32[]{:S(2)}) collective-permute-start(f32[320,128]{1,0:T(8,128)S(1)} %get-tuple-element.45.refs_9_), channel_id=1, source_target_pairs={{0,2},{1,3},{2,0},{3,1},{4,6},{5,7},{6,4},{7,5},{8,10},{9,11},{10,... | collective-permute-start | bytes 491528 | tf_op jit(solution)/shard_map/ppermute | solution.py:846
  5.1 18.6 %collective-permute-start.6 = (f32[320,128]{1,0:T(8,128)S(1)}, f32[320,128]{1,0:T(8,128)S(1)}, u32[]{:S(2)}, u32[]{:S(2)}) collective-permute-start(f32[320,128]{1,0:T(8,128)S(1)} %get-tuple-element.46.refs_10_), channel_id=1, source_target_pairs={{0,3},{1,2},{2,1},{3,0},{4,7},{5,6},{6,5},{7,4},{8,11},{9,10},{10,... | collective-permute-start | bytes 491528 | tf_op jit(solution)/shard_map/ppermute | solution.py:846
  5.1 9.2 %copy-start.1 = (f32[16,16,320]{2,1,0:T(8,128)S(1)}, f32[16,16,320]{2,1,0:T(8,128)}, u32[]{:S(2)}) copy-start(f32[16,16,320]{2,1,0:T(8,128)} %param.6) | copy-start | bytes 983044
  5.1 9.2 %copy-start.2 = (f32[16,16,128]{2,1,0:T(8,128)S(1)}, f32[16,16,128]{2,1,0:T(8,128)}, u32[]{:S(2)}) copy-start(f32[16,16,128]{2,1,0:T(8,128)} %param.7) | copy-start | bytes 393220
  7.1 1.9 %collective-permute-start = (f32[16,896]{1,0:T(8,128)S(1)}, f32[16,896]{1,0:T(8,128)S(1)}, u32[]{:S(2)}, u32[]{:S(2)}) collective-permute-start(f32[16,896]{1,0:T(8,128)S(1)} %get-tuple-element.30), channel_id=1, source_target_pairs={{0,1},{1,0},{2,3},{3,2},{4,5},{5,4},{6,7},{7,6},{8,9},{9,8},{10,11... | collective-permute-start | bytes 172040 | tf_op jit(solution)/shard_map/ppermute | solution.py:801
  7.3 7.0 %collective-permute-start.1 = (f32[16,896]{1,0:T(8,128)S(1)}, f32[16,896]{1,0:T(8,128)S(1)}, u32[]{:S(2)}, u32[]{:S(2)}) collective-permute-start(f32[16,896]{1,0:T(8,128)S(1)} %get-tuple-element.31), channel_id=1, source_target_pairs={{0,3},{1,2},{2,1},{3,0},{4,7},{5,6},{6,5},{7,4},{8,11},{9,10},{10,... | collective-permute-start | bytes 172040 | tf_op jit(solution)/shard_map/ppermute | solution.py:800
  14.3 5.3 %copy-start = (bf16[320,320]{1,0:T(8,128)(2,1)S(1)}, bf16[320,320]{1,0:T(8,128)(2,1)}, u32[]{:S(2)}) copy-start(bf16[320,320]{1,0:T(8,128)(2,1)} %mix.5) | copy-start | bytes 614404
  14.5 6.5 %collective-permute-start.2 = (f32[16,896]{1,0:T(8,128)S(1)}, f32[16,896]{1,0:T(8,128)S(1)}, u32[]{:S(2)}, u32[]{:S(2)}) collective-permute-start(f32[16,896]{1,0:T(8,128)S(1)} %get-tuple-element.37), channel_id=1, source_target_pairs={{0,4},{4,0},{8,12},{12,8},{16,20},{20,16},{24,28},{28,24},{1,5},{5... | collective-permute-start | bytes 172040 | tf_op jit(solution)/shard_map/ppermute | solution.py:801
  16.0 3.6 %copy-start.6 = (s32[16,1]{0,1:T(1,128)S(1)}, s32[16,1]{0,1:T(1,128)}, u32[]{:S(2)}) copy-start(s32[16,1]{0,1:T(1,128)} %param.9) | copy-start | bytes 196
  16.1 6.9 %collective-permute-start.3 = (f32[16,896]{1,0:T(8,128)S(1)}, f32[16,896]{1,0:T(8,128)S(1)}, u32[]{:S(2)}, u32[]{:S(2)}) collective-permute-start(f32[16,896]{1,0:T(8,128)S(1)} %get-tuple-element.38), channel_id=1, source_target_pairs={{0,28},{4,8},{8,4},{12,16},{16,12},{20,24},{24,20},{28,0},{1,29},{... | collective-permute-start | bytes 172040 | tf_op jit(solution)/shard_map/ppermute | solution.py:800
  22.9 0.9 %copy-start.5 = (bf16[320,320]{1,0:T(8,128)(2,1)S(1)}, bf16[320,320]{1,0:T(8,128)(2,1)}, u32[]{:S(2)}) copy-start(bf16[320,320]{1,0:T(8,128)(2,1)} %refs_5_.3) | copy-start | bytes 614404
  25.5 2.3 %collective-permute-start.7 = (f32[24,321]{1,0:T(8,128)S(1)}, f32[24,321]{1,0:T(8,128)S(1)}, u32[]{:S(2)}, u32[]{:S(2)}) collective-permute-start(f32[24,321]{1,0:T(8,128)S(1)} %get-tuple-element.48), channel_id=1, source_target_pairs={{0,1},{1,0},{2,3},{3,2},{4,5},{5,4},{6,7},{7,6},{8,9},{9,8},{10,11... | collective-permute-start | bytes 92456 | tf_op jit(solution)/shard_map/ppermute | solution.py:801
  25.5 3.4 %collective-permute-start.8 = (f32[24,321]{1,0:T(8,128)S(1)}, f32[24,321]{1,0:T(8,128)S(1)}, u32[]{:S(2)}, u32[]{:S(2)}) collective-permute-start(f32[24,321]{1,0:T(8,128)S(1)} %get-tuple-element.49), channel_id=1, source_target_pairs={{0,3},{1,2},{2,1},{3,0},{4,7},{5,6},{6,5},{7,4},{8,11},{9,10},{10,... | collective-permute-start | bytes 92456 | tf_op jit(solution)/shard_map/ppermute | solution.py:800
  27.8 8.7 %copy-start.4 = (bf16[16,32,320]{2,1,0:T(8,128)(2,1)S(1)}, bf16[16,32,320]{2,1,0:T(8,128)(2,1)}, u32[]{:S(2)}) copy-start(bf16[16,32,320]{2,1,0:T(8,128)(2,1)} %param.10) | copy-start | bytes 983044
  29.0 9.6 %collective-permute-start.10 = (f32[16,320]{1,0:T(8,128)S(1)}, f32[16,320]{1,0:T(8,128)S(1)}, u32[]{:S(2)}, u32[]{:S(2)}) collective-permute-start(f32[16,320]{1,0:T(8,128)S(1)} %get-tuple-element.53.mine_a), channel_id=1, source_target_pairs={{0,4},{4,0},{8,12},{12,8},{16,20},{20,16},{24,28},{28,24},{1,5},{5... | collective-permute-start | bytes 61448 | tf_op jit(solution)/shard_map/ppermute | solution.py:801
  29.1 9.6 %collective-permute-start.11 = (f32[16,320]{1,0:T(8,128)S(1)}, f32[16,320]{1,0:T(8,128)S(1)}, u32[]{:S(2)}, u32[]{:S(2)}) collective-permute-start(f32[16,320]{1,0:T(8,128)S(1)} %get-tuple-element.54.mine_b), channel_id=1, source_target_pairs={{0,28},{4,8},{8,4},{12,16},{16,12},{20,24},{24,20},{28,0},{1,29},{... | collective-permute-start | bytes 61448 | tf_op jit(solution)/shard_map/ppermute | solution.py:800
  32.7 3.7 %collective-permute-start.9 = (f32[8,321]{1,0:T(8,128)S(1)}, f32[8,321]{1,0:T(8,128)S(1)}, u32[]{:S(2)}, u32[]{:S(2)}) collective-permute-start(f32[8,321]{1,0:T(8,128)S(1)} %slice.10), channel_id=1, source_target_pairs={{0,2},{1,3},{2,0},{3,1},{4,6},{5,7},{6,4},{7,5},{8,10},{9,11},{10,... | collective-permute-start | bytes 30824 | tf_op jit(solution)/shard_map/ppermute | solution.py:898

commit v3 on v2

--- a/solution.py
+++ b/solution.py
@@ -64,7 +64,7 @@
     for i in range(NODES):
         total = None
         for j in range(NODES):
-            if DERIV[i][j] != 0.0 and not (i == j and abs(DERIV[i][j]) < 1e-6):
+            if abs(DERIV[i][j]) > 1e-6:
                 term = DERIV[i][j] * rows[j]
                 total = term if total is None else total + term
         out.append(total)
@@ -133,33 +133,67 @@
     )
 
 
-def local_update(base_ref, field_ref, mix, wind_ref, out_ref, size_x, size_y, levels, average,
+def strip_derivatives(size_y):
+    matrix = np.asarray(DERIV, np.float64)
+    both = np.concatenate(
+        [np.kron(matrix, np.eye(size_y)), np.kron(np.eye(size_y), matrix)], axis=0
+    )
+    high = both.astype(jnp.bfloat16)
+    low = (both - high.astype(np.float64)).astype(jnp.bfloat16)
+    return jnp.asarray(np.concatenate([high, high, low], axis=1))
+
+
+def strip_products(field_ref, mix, slopes_ref, size_x, size_y):
+    strip = NODES * size_y
+    products = []
+    for element in range(size_x // NODES):
+        field = field_ref[pl.ds(element * strip, strip), :]
+        high = to_bf16(field)
+        slopes = None
+        if 2 * element >= size_x // NODES:
+            low = to_bf16(field - high.astype(jnp.float32))
+            slopes = jnp.dot(
+                slopes_ref[...],
+                jnp.concatenate([high, low, high], axis=0),
+                preferred_element_type=jnp.float32,
+            )
+        products.append((jnp.dot(high, mix, preferred_element_type=jnp.float32), slopes))
+    return products
+
+
+def local_update(base_ref, field_ref, products, wind_ref, out_ref, size_y, levels,
                  mixed_ref=None, change_ref=None):
-    channels = field_ref.shape[1]
+    channels = out_ref.shape[1]
+    strip = NODES * size_y
     table = sublane_coefficients(2 * levels)
-    strip = NODES * size_y
-    for element in range(size_x // NODES):
-        whole = pl.ds(element * strip, strip)
-        mixed = mix_all(field_ref[whole, :], mix)
+    for element, (mixed, slopes) in enumerate(products):
         if mixed_ref is not None:
-            mixed_ref[whole, :] = mixed
+            mixed_ref[pl.ds(element * strip, strip), :] = mixed
         rows = [pl.ds((NODES * element + i) * size_y, size_y) for i in range(NODES)]
         wind = [winds(wind_ref[row, :], levels) for row in rows]
         for begin, end in lane_tiles(channels, 2 * levels):
-            width = end - begin
-            values = [field_ref[row, begin:end] for row in rows]
-            slopes = dx_rows(values)
+            if slopes is None:
+                values = [field_ref[row, begin:end] for row in rows]
+                along = dx_rows(values)
+                across = [dsub(value, table) for value in values]
+            else:
+                along, across = (
+                    [
+                        slopes[at + i * size_y : at + (i + 1) * size_y, begin:end]
+                        for i in range(NODES)
+                    ]
+                    for at in (0, strip)
+                )
             for i in range(NODES):
-                along_x, along_y = wind[i][0][:, :width], wind[i][1][:, :width]
-                base = values[i] if base_ref is field_ref else base_ref[rows[i], begin:end]
+                wind_x, wind_y = wind[i][0][:, : end - begin], wind[i][1][:, : end - begin]
                 result = (
-                    base
+                    base_ref[rows[i], begin:end]
                     + mixed[i * size_y : (i + 1) * size_y, begin:end]
-                    - (along_x * slopes[i] + along_y * dsub(values[i], table))
+                    - (wind_x * along[i] + wind_y * across[i])
                 )
                 if change_ref is not None:
                     result = result + change_ref[pl.ds(element * size_y, size_y), begin:end]
-                out_ref[rows[i], begin:end] = sub_average(result) if average else result
+                out_ref[rows[i], begin:end] = sub_average(result)
 
 
 def to_bf16(value):
@@ -213,20 +247,21 @@
     return (rank[0] & 1) == 0
 
 
-def begin_kernel(size_x, size_y, levels, rank, state_in, wind_in, mix_in, partial, to_a, to_b,
-                 state, wind, mix, message, arrivals):
+def begin_kernel(size_x, size_y, levels, rank, state_in, wind_in, mix_in, slopes_in,
+                 partial, to_a, to_b, state, wind, mix, slopes, message, arrivals):
     channels = state.shape[1]
     copies = [
         pltpu.make_async_copy(source, target, arrivals.at[index])
         for index, (source, target) in enumerate(
-            ((state_in, state), (mix_in, mix), (wind_in, wind))
+            ((state_in, state), (mix_in, mix), (slopes_in, slopes), (wind_in, wind))
         )
     ]
     for copy in copies:
         copy.start()
     for copy in copies:
         copy.wait()
-    local_update(state, state, mix[...], wind, partial, size_x, size_y, levels, True)
+    products = strip_products(state, mix[...], slopes, size_x, size_y)
+    local_update(state, state, products, wind, partial, size_y, levels)
     average_rows(partial, size_x, size_y)
     to_left, to_right = message.at[0], message.at[1]
     for out, column, near, row in ((to_left, 0, 0, 0), (to_right, size_y - 1, size_y - NODES, 3)):
@@ -331,10 +366,43 @@
     to_b[...] = jnp.where(even, message[0], message[1])
 
 
-def ready_kernel(size_x, size_y, levels, capacity, rank, owner, partial, state, wind, mix,
-                 from_a, from_b, field, mixed, total, sides, gather, spread):
+def ready_kernel(size_x, size_y, levels, capacity, rank, owner_in, cloud_mix_in, partial,
+                 state, wind, mix, slopes, from_a, from_b,
+                 field, mixed, total, sides, gather, spread, cloud_mix, owner, arrivals):
     channels = state.shape[1]
     from_left, from_right = in_order(rank, from_a, from_b)
+    copies = [
+        pltpu.make_async_copy(owner_in, owner, arrivals.at[0]),
+        pltpu.make_async_copy(cloud_mix_in, cloud_mix, arrivals.at[1]),
+    ]
+    for copy in copies:
+        copy.start()
+    left, right = side_changes(size_x, size_y, partial, from_left, from_right)
+    for x in range(size_x):
+        row = pl.ds(x * size_y, size_y)
+        field[row, :] = edge_rows(partial[row, :], left[x : x + 1], right[x : x + 1])
+    products = strip_products(field, mix[...], slopes, size_x, size_y)
+    local_update(state, field, products, wind, total, size_y, levels, mixed)
+    table = sublane_coefficients(channels)
+    for side, (message, y, change, factor) in enumerate(
+        ((from_left, 0, left, LAST), (from_right, size_y - 1, right, FIRST))
+    ):
+        _, side_part, side_wind, ends = column_parts(message, channels, levels)
+        along_x, along_y = full_winds(side_wind, levels, channels)
+        sides[side, 0] = (
+            side_part
+            + column_of(mixed, y, size_x, size_y)
+            - along_x * dsub(column_of(field, y, size_x, size_y), table)
+            + factor * (along_y * change)
+        )
+        sides[side, 1] = end_rows(
+            size_x,
+            ends[0] - factor * change[0:1],
+            ends[1] - factor * change[size_x - 1 : size_x],
+        )
+        sides[side, 2] = along_x
+        sides[side, 3] = along_y
+    copies[0].wait()
     parts = 8 // capacity
     for out, node_axis in ((gather, 1), (spread, 0)):
         columns = lax.broadcasted_iota(jnp.int32, out.shape, node_axis) >> 2
@@ -348,30 +416,8 @@
         rows = lax.broadcasted_iota(jnp.int32, out.shape, 1 - node_axis)
         count = parts if node_axis else 1
         out[...] = jnp.where((rows >= slot) & (rows < slot + count), 1.0, 0.0).astype(jnp.bfloat16)
-    left, right = side_changes(size_x, size_y, partial, from_left, from_right)
-    for x in range(size_x):
-        row = pl.ds(x * size_y, size_y)
-        field[row, :] = edge_rows(partial[row, :], left[x : x + 1], right[x : x + 1])
-    local_update(state, field, mix[...], wind, total, size_x, size_y, levels, True, mixed)
-    table = sublane_coefficients(channels)
-    for side, (message, y, change, factor) in enumerate(
-        ((from_left, 0, left, LAST), (from_right, size_y - 1, right, FIRST))
-    ):
-        _, side_part, side_wind, slopes = column_parts(message, channels, levels)
-        along_x, along_y = full_winds(side_wind, levels, channels)
-        sides[side, 0] = (
-            side_part
-            + column_of(mixed, y, size_x, size_y)
-            - along_x * dsub(column_of(field, y, size_x, size_y), table)
-            + factor * (along_y * change)
-        )
-        sides[side, 1] = end_rows(
-            size_x,
-            slopes[0] - factor * change[0:1],
-            slopes[1] - factor * change[size_x - 1 : size_x],
-        )
-        sides[side, 2] = along_x
-        sides[side, 3] = along_y
+    copies[1].wait()
+    cloud_mix[...] = cloud_mix[...] * 0.5
 
 
 def part_roll(value, parts, by):
@@ -451,7 +497,7 @@
 def cloud_run(states, blocks, forcing, mix, rows, parts, tendency, finals):
     count = rows // 8
     columns = count * parts
-    half = mix[...] * 0.5
+    half = mix[...]
     means, totals = {}, {}
     for step in range(SUB):
         last = step == SUB - 1
@@ -485,7 +531,7 @@
                         states[block * rows + 8 * t : block * rows + 8 * t + 8, :] = (
                             (1.0 - 2.0 * CRM_STEP * DIFFUSION) * here
                             + CRM_STEP * DIFFUSION * (behind + ahead)
-                        ) + ((2.0 * CRM_STEP) * turn + gain)
+                        ) + (turn + gain)
                         behind, here = here, ahead
                 if tendency is not None or not last:
                     mean = (
@@ -522,7 +568,7 @@
             )
 
 
-def second_kernel(size_x, size_y, levels, place, field, second, known, sides, gather, wind, mix,
+def second_kernel(size_x, size_y, levels, place, field, total_in, known, sides, gather, wind, mix,
                   from_a, from_b, total, work, forcing, reduced):
     from_up, from_down = in_order(place, from_a, from_b)
     channels = field.shape[1]
@@ -537,7 +583,6 @@
         jnp.concatenate([field[first_row, :] + ups, field[last_row, :] + downs], axis=0), mix[...]
     )
     new_mixed = (remixed[0:size_y], remixed[size_y : 2 * size_y])
-    total[...] = second[...]
     edge_mixed = []
     for index, (x, near, end, change) in enumerate(
         ((0, 0, 0, ups), (size_x - 1, size_x - NODES, 3, downs))
@@ -682,8 +727,9 @@
     to_b[size_x : size_x + 8, :] = sends[8 * groups - 8 : 8 * groups, :]
 
 
-def fields_kernel(size_x, size_y, levels, second, wind, mix, change, out):
-    local_update(second, second, mix[...], wind, out, size_x, size_y, levels, True, None, change)
+def fields_kernel(size_x, size_y, levels, second, wind, mix, slopes, change, out):
+    products = strip_products(second, mix[...], slopes, size_x, size_y)
+    local_update(second, second, products, wind, out, size_y, levels, None, change)
     average_rows(out, size_x, size_y)
 
 
@@ -823,15 +869,16 @@
     xor = [[(i, i ^ k) for i in range(groups)] for k in range(groups)]
 
     column_message = ((size_x, 2 * channels + 2 * levels + 128), f32)
-    partial, to_a, to_b = call(
+    slopes = strip_derivatives(size_y)
+    partial, to_a, to_b, state, wind, dyn_mix, slopes = call(
         functools.partial(begin_kernel, size_x, size_y, levels),
-        [grid, column_message, column_message],
         [
-            grid, ((nodes, 2 * levels), f32), (dyn_mix.shape, dyn_mix.dtype),
-            ((2,) + column_message[0], f32), DMA((3,)),
+            grid, column_message, column_message, grid, ((nodes, 2 * levels), f32),
+            (dyn_mix.shape, dyn_mix.dtype), (slopes.shape, slopes.dtype),
         ],
-        rank, state, wind, dyn_mix,
-        smem=(0,), far=(1, 2, 3),
+        [((2,) + column_message[0], f32), DMA((4,))],
+        rank, state, wind, dyn_mix, slopes,
+        smem=(0,), far=(1, 2, 3, 4),
     )
     column_a, column_b = ring(to_a, to_b, "crm")
 
@@ -855,23 +902,24 @@
         smem=(0, 1),
     )
     row_a, row_b = ring(to_a, to_b, "elem")
-    field, known, total, sides, gather, spread = call(
+    field, known, total, sides, gather, spread, crm_mix = call(
         functools.partial(ready_kernel, size_x, size_y, levels, capacity),
         [
             grid, grid, grid, ((2, 4, size_x, channels), f32),
             ((8 * groups, elements * size_y), jnp.bfloat16),
             ((elements * size_y, 8 * groups), jnp.bfloat16),
+            (crm_mix.shape, crm_mix.dtype),
         ],
-        [],
-        rank, owners, partial, state, wind, dyn_mix, column_a, column_b,
-        smem=(0, 1),
+        [pltpu.SMEM(owners.shape, owners.dtype), DMA((2,))],
+        rank, owners, crm_mix, partial, state, wind, dyn_mix, slopes, column_a, column_b,
+        smem=(0,), far=(1, 2),
     )
     second, edges, forcing = call(
         functools.partial(second_kernel, size_x, size_y, levels),
         [grid, ((2, size_x, channels), f32), ((8 * groups, channels), f32)],
         [((elements * size_y, channels), f32)],
         place, field, total, known, sides, gather, wind, dyn_mix, row_a, row_b,
-        smem=(0,),
+        smem=(0,), aliases={2: 0},
     )
     edge = ((size_x + 8, channels + 1), f32)
     change, to_a, to_b, sends, own_final = call(
@@ -900,7 +948,7 @@
         functools.partial(fields_kernel, size_x, size_y, levels),
         [grid],
         [],
-        second, wind, dyn_mix, change,
+        second, wind, dyn_mix, slopes, change,
     )
     mine_a, mine_b = call(
         functools.partial(last_turn_kernel, size_x, size_y),

time: 39.5 us -> 39.5 us (level)
    unnamed x14 -> x4, local copies, waits for them, and re-layouts: 1.17 us -> 1 us
where the time goes in v3:
time: 39.5 us; the launch traced here: 39.3 us
  starting transfers between devices  17.1 us (43%)
  waiting for transfers between devices  10.6 us (27%)
  Pallas kernels  9.84 us (25%)
  local copies, waits for them, and re-layouts  1 us (3%)
  between operations  0.79 us (2%)
    ppermute x4, starting transfers between devices, ring(): from_b = lax.ppermute(to_b, axis, upper_pairs(count))  10.5 us
    pallas_call x10, Pallas kernels, call(): pl.pallas_call(kernel, out_shape=[jax.ShapeDtypeStruct(shape, dtype) for...  9.84 us
    ppermute x4, waiting for transfers between devices, ring(): from_b = lax.ppermute(to_b, axis, upper_pairs(count))  8.41 us
    ppermute x3, starting transfers between devices, on_device(): lax.ppermute(wide[k - 1], 'crm', xor[k])  3.18 us
    ppermute x1, waiting for transfers between devices, on_device(): forcings.append(lax.ppermute(sends[8 * k:8 * k + 8], 'crm', xor[k]))  2.17 us
    ppermute x4, starting transfers between devices, ring(): from_a = lax.ppermute(to_a, axis, lower_pairs(count))  1.86 us
    ppermute x1, starting transfers between devices, on_device(): forcings.append(lax.ppermute(sends[8 * k:8 * k + 8], 'crm', xor[k]))  1.52 us
    unnamed x4, local copies, waits for them, and re-layouts  1 us
  transfers between devices with their start and end apart: 12, of which 4 were waited for; matrix products, arithmetic and copies ran while one was open for 0% of the time, Pallas kernels for 18%

profile of v3, /device:TPU:0, one launch (start us, length us, event | category | flops | bytes accessed | tf_op | source)
XLA Modules:
  0.0 39.3 jit_solution(16830669629826335052)
XLA Ops:
  0.6 0.0 copy-start
  0.6 1.0 %copy-done = bf16[16,32,320]{2,1,0:T(8,128)(2,1)S(1)} copy-done((bf16[16,32,320]{2,1,0:T(8,128)(2,1)S(1)}, bf16[16,32,320]{2,1,0:T(8,128)(2,1)}, u32[]{:S(2)}) %copy-start) | copy-done | bytes 327704
  1.6 0.3 shard_map.90
  1.9 0.6 %collective-permute-start.4 = (f32[320,128]{1,0:T(8,128)S(1)}, f32[320,128]{1,0:T(8,128)S(1)}, u32[]{:S(2)}, u32[]{:S(2)}) collective-permute-start(f32[320,128]{1,0:T(8,128)S(1)} %get-tuple-element.54.refs_8_), channel_id=1, source_target_pairs={{0,1},{1,0},{2,3},{3,2},{4,5},{5,4},{6,7},{7,6},{8,9},{9,8},{10,11... | collective-permute-start | bytes 491528 | tf_op jit(solution)/shard_map/ppermute | solution.py:893
  2.5 2.6 %collective-permute-start.5 = (f32[320,128]{1,0:T(8,128)S(1)}, f32[320,128]{1,0:T(8,128)S(1)}, u32[]{:S(2)}, u32[]{:S(2)}) collective-permute-start(f32[320,128]{1,0:T(8,128)S(1)} %get-tuple-element.55.refs_9_), channel_id=1, source_target_pairs={{0,2},{1,3},{2,0},{3,1},{4,6},{5,7},{6,4},{7,5},{8,10},{9,11},{10,... | collective-permute-start | bytes 491528 | tf_op jit(solution)/shard_map/ppermute | solution.py:893
  5.1 0.0 collective-permute-start.6
  5.1 1.9 %shard_map.86 = (f32[256,320]{1,0:T(8,128)S(1)}, f32[16,896]{1,0:T(8,128)S(1)}, f32[16,896]{1,0:T(8,128)S(1)}, f32[256,320]{1,0:T(8,128)S(1)}, f32[256,128]{1,0:...) custom-call(s32[1]{0:T(128)} %bitcast.1.rank.refs_0_, f32[256,320]{1,0:T(8,128)} %bitcast.10, ...), custom_call_target="tpu_custom_call" | custom-call | tf_op jit(solution)/shard_map/pallas_call | solution.py:823
  7.0 0.2 collective-permute-start
  7.2 1.7 %collective-permute-start.1 = (f32[16,896]{1,0:T(8,128)S(1)}, f32[16,896]{1,0:T(8,128)S(1)}, u32[]{:S(2)}, u32[]{:S(2)}) collective-permute-start(f32[16,896]{1,0:T(8,128)S(1)} %get-tuple-element.40), channel_id=1, source_target_pairs={{0,3},{1,2},{2,1},{3,0},{4,7},{5,6},{6,5},{7,4},{8,11},{9,10},{10,... | collective-permute-start | bytes 172040 | tf_op jit(solution)/shard_map/ppermute | solution.py:846
  8.9 0.0 collective-permute-done.from_a
  8.9 5.4 %collective-permute-done.1.from_b = f32[16,896]{1,0:T(8,128)S(1)} collective-permute-done((f32[16,896]{1,0:T(8,128)S(1)}, f32[16,896]{1,0:T(8,128)S(1)}, u32[]{:S(2)}, u32[]{:S(2)}) %collective-permute-start.1) | collective-permute-done | bytes 57376 | tf_op jit(solution)/shard_map/ppermute | solution.py:846
  14.3 0.2 shard_map.88
  14.5 1.5 %collective-permute-start.2 = (f32[16,896]{1,0:T(8,128)S(1)}, f32[16,896]{1,0:T(8,128)S(1)}, u32[]{:S(2)}, u32[]{:S(2)}) collective-permute-start(f32[16,896]{1,0:T(8,128)S(1)} %get-tuple-element.46), channel_id=1, source_target_pairs={{0,4},{4,0},{8,12},{12,8},{16,20},{20,16},{24,28},{28,24},{1,5},{5... | collective-permute-start | bytes 172040 | tf_op jit(solution)/shard_map/ppermute | solution.py:847
  16.0 3.6 %collective-permute-start.3 = (f32[16,896]{1,0:T(8,128)S(1)}, f32[16,896]{1,0:T(8,128)S(1)}, u32[]{:S(2)}, u32[]{:S(2)}) collective-permute-start(f32[16,896]{1,0:T(8,128)S(1)} %get-tuple-element.47), channel_id=1, source_target_pairs={{0,28},{4,8},{8,4},{12,16},{16,12},{20,24},{24,20},{28,0},{1,29},{... | collective-permute-start | bytes 172040 | tf_op jit(solution)/shard_map/ppermute | solution.py:846
  19.6 1.6 %shard_map.87 = (f32[256,320]{1,0:T(8,128)S(1)}, f32[256,320]{1,0:T(8,128)S(1)}, f32[256,320]{1,0:T(8,128)S(1)}, f32[2,4,16,320]{3,2,1,0:T(8,128)S(1)}, bf16[32,...) custom-call(s32[1]{0:T(128)} %bitcast.1.rank.refs_0_, s32[16]{0:T(128)} %bitcast.13, ...), custom_call_target="tpu_custom_call" | custom-call | tf_op jit(solution)/shard_map/pallas_call | solution.py:823
  21.2 1.7 %collective-permute-done.3.from_b = f32[16,896]{1,0:T(8,128)S(1)} collective-permute-done((f32[16,896]{1,0:T(8,128)S(1)}, f32[16,896]{1,0:T(8,128)S(1)}, u32[]{:S(2)}, u32[]{:S(2)}) %collective-permute-start.3) | collective-permute-done | bytes 57376 | tf_op jit(solution)/shard_map/ppermute | solution.py:846
  22.9 0.8 %shard_map.89 = (f32[256,320]{1,0:T(8,128)S(1)}, f32[2,16,320]{2,1,0:T(8,128)S(1)}, f32[32,320]{1,0:T(8,128)S(1)}) custom-call(s32[1]{0:T(128)} %bitcast.place, f32[256,320]{1,0:T(8,128)S(1)} %get-tuple-element.41.field, f32[256,320]{1,0:T(8,128)S(1)} %get-tuple-element.42.total_in, ...), custom_call_target="tpu_custom_call", output_to_operand_aliasing={{0}: (2, {})} | custom-call | tf_op jit(solution)/shard_map/pallas_call | solution.py:823
  23.7 0.0 collective-permute-done.4.refs_8_
  23.7 0.0 collective-permute-done.6.refs_10_
  23.7 1.7 %shard_map.91 = (f32[64,320]{1,0:T(8,128)S(1)}, f32[24,321]{1,0:T(8,128)S(1)}, f32[24,321]{1,0:T(8,128)S(1)}, f32[32,321]{1,0:T(8,128)S(1)}, f32[128,320]{1,0:T(8,128)S(1)}) custom-call(s32[1]{0:T(128)} %bitcast.1.rank.refs_0_, f32[2,16,320]{2,1,0:T(8,128)S(1)} %get-tuple-element.49.refs_1_, f32[32,320]{1,0:T(8,128)S(1)} %get-tuple-element.50.refs_2_, ...), custom_call_target="tpu_custom_call" | custom-call | tf_op jit(solution)/shard_map/pallas_call | solution.py:823
  25.4 0.1 collective-permute-start.7
  25.5 1.6 %collective-permute-start.8 = (f32[24,321]{1,0:T(8,128)S(1)}, f32[24,321]{1,0:T(8,128)S(1)}, u32[]{:S(2)}, u32[]{:S(2)}) collective-permute-start(f32[24,321]{1,0:T(8,128)S(1)} %get-tuple-element.59), channel_id=1, source_target_pairs={{0,3},{1,2},{2,1},{3,0},{4,7},{5,6},{6,5},{7,4},{8,11},{9,10},{10,... | collective-permute-start | bytes 92456 | tf_op jit(solution)/shard_map/ppermute | solution.py:846
  27.1 0.6 %shard_map.92.refs_1_.partial = f32[256,320]{1,0:T(8,128)S(1)} custom-call(f32[256,320]{1,0:T(8,128)S(1)} %get-tuple-element.48.second, f32[256,128]{1,0:T(8,128)S(1)} %get-tuple-element.36.wind, bf16[320,320]{1,0:T(8,128)(2,1)S(1)} %get-tuple-element.37.mix.refs_5_, bf16[128,192]{1,0:T(8,128)(2,1)S(1)} %get-tuple-element.38.slopes, ...), custom_call_target="tpu_custom_call" | custom-call | tf_op jit(solution)/shard_map/pallas_call | solution.py:823
  27.6 0.0 copy-start.1
  27.7 0.0 collective-permute-done.7.refs_2_.from_a
  27.7 1.2 %collective-permute-done.8.refs_3_.from_b = f32[24,321]{1,0:T(8,128)S(1)} collective-permute-done((f32[24,321]{1,0:T(8,128)S(1)}, f32[24,321]{1,0:T(8,128)S(1)}, u32[]{:S(2)}, u32[]{:S(2)}) %collective-permute-start.8) | collective-permute-done | bytes 30848 | tf_op jit(solution)/shard_map/ppermute | solution.py:846
  28.9 0.1 collective-permute-start.10
  29.0 3.6 %collective-permute-start.11 = (f32[16,320]{1,0:T(8,128)S(1)}, f32[16,320]{1,0:T(8,128)S(1)}, u32[]{:S(2)}, u32[]{:S(2)}) collective-permute-start(f32[16,320]{1,0:T(8,128)S(1)} %get-tuple-element.64.mine_b), channel_id=1, source_target_pairs={{0,28},{4,8},{8,4},{12,16},{16,12},{20,24},{24,20},{28,0},{1,29},{... | collective-permute-start | bytes 61448 | tf_op jit(solution)/shard_map/ppermute | solution.py:846
  32.6 1.5 %collective-permute-start.9 = (f32[8,321]{1,0:T(8,128)S(1)}, f32[8,321]{1,0:T(8,128)S(1)}, u32[]{:S(2)}, u32[]{:S(2)}) collective-permute-start(f32[8,321]{1,0:T(8,128)S(1)} %slice.10), channel_id=1, source_target_pairs={{0,2},{1,3},{2,0},{3,1},{4,6},{5,7},{6,4},{7,5},{8,10},{9,11},{10,... | collective-permute-start | bytes 30824 | tf_op jit(solution)/shard_map/ppermute | solution.py:946
  34.2 2.2 %collective-permute-done.9.refs_12_ = f32[8,321]{1,0:T(8,128)S(1)} collective-permute-done((f32[8,321]{1,0:T(8,128)S(1)}, f32[8,321]{1,0:T(8,128)S(1)}, u32[]{:S(2)}, u32[]{:S(2)}) %collective-permute-start.9) | collective-permute-done | bytes 10304 | tf_op jit(solution)/shard_map/ppermute | solution.py:946
  36.3 2.3 %shard_map.93 = (f32[256,320]{1,0:T(8,128)}, bf16[512,320]{1,0:T(8,128)(2,1)}) custom-call(s32[1]{0:T(128)} %bitcast.1.rank.refs_0_, f32[256,320]{1,0:T(8,128)S(1)} %shard_map.92.refs_1_.partial, f32[24,321]{1,0:T(8,128)S(1)} %collective-permute-done.7.refs_2_.from_a, f32[24,321]{1,0:T(8,128)S(1)} %collective-permute-done.8.refs_3_.from_b, ...), custom_call_target="tpu_custom_call" | custom-call | tf_op jit(solution)/shard_map/pallas_call | solution.py:823
  38.7 0.6 %shard_map.95 = f32[256,320]{1,0:T(8,128)} custom-call(s32[1]{0:T(128)} %bitcast.place, f32[256,320]{1,0:T(8,128)} %get-tuple-element.62.fields_in, f32[16,320]{1,0:T(8,128)S(1)} %get-tuple-element.63.mine_a, f32[16,320]{1,0:T(8,128)S(1)} %get-tuple-element.64.mine_b, f32[16,320]{1,0:T(8,128)S(1)} %collective-permute-done.10.from_a, ...), custom_call_target="tpu_custom_call", output_to_operand_aliasing={{}: (1, {})} | custom-call | tf_op jit(solution)/shard_map/pallas_call | solution.py:823
  (9 shorter events, 0.0 us)
Async XLA Ops:
  0.6 1.0 %copy-start = (bf16[16,32,320]{2,1,0:T(8,128)(2,1)S(1)}, bf16[16,32,320]{2,1,0:T(8,128)(2,1)}, u32[]{:S(2)}) copy-start(bf16[16,32,320]{2,1,0:T(8,128)(2,1)} %param.11) | copy-start | bytes 983044
  1.9 21.8 %collective-permute-start.4 = (f32[320,128]{1,0:T(8,128)S(1)}, f32[320,128]{1,0:T(8,128)S(1)}, u32[]{:S(2)}, u32[]{:S(2)}) collective-permute-start(f32[320,128]{1,0:T(8,128)S(1)} %get-tuple-element.54.refs_8_), channel_id=1, source_target_pairs={{0,1},{1,0},{2,3},{3,2},{4,5},{5,4},{6,7},{7,6},{8,9},{9,8},{10,11... | collective-permute-start | bytes 491528 | tf_op jit(solution)/shard_map/ppermute | solution.py:893
  2.5 21.2 %collective-permute-start.5 = (f32[320,128]{1,0:T(8,128)S(1)}, f32[320,128]{1,0:T(8,128)S(1)}, u32[]{:S(2)}, u32[]{:S(2)}) collective-permute-start(f32[320,128]{1,0:T(8,128)S(1)} %get-tuple-element.55.refs_9_), channel_id=1, source_target_pairs={{0,2},{1,3},{2,0},{3,1},{4,6},{5,7},{6,4},{7,5},{8,10},{9,11},{10,... | collective-permute-start | bytes 491528 | tf_op jit(solution)/shard_map/ppermute | solution.py:893
  5.1 18.6 %collective-permute-start.6 = (f32[320,128]{1,0:T(8,128)S(1)}, f32[320,128]{1,0:T(8,128)S(1)}, u32[]{:S(2)}, u32[]{:S(2)}) collective-permute-start(f32[320,128]{1,0:T(8,128)S(1)} %get-tuple-element.56.refs_10_), channel_id=1, source_target_pairs={{0,3},{1,2},{2,1},{3,0},{4,7},{5,6},{6,5},{7,4},{8,11},{9,10},{10,... | collective-permute-start | bytes 491528 | tf_op jit(solution)/shard_map/ppermute | solution.py:893
  7.0 1.9 %collective-permute-start = (f32[16,896]{1,0:T(8,128)S(1)}, f32[16,896]{1,0:T(8,128)S(1)}, u32[]{:S(2)}, u32[]{:S(2)}) collective-permute-start(f32[16,896]{1,0:T(8,128)S(1)} %get-tuple-element.39), channel_id=1, source_target_pairs={{0,1},{1,0},{2,3},{3,2},{4,5},{5,4},{6,7},{7,6},{8,9},{9,8},{10,11... | collective-permute-start | bytes 172040 | tf_op jit(solution)/shard_map/ppermute | solution.py:847
  7.2 7.1 %collective-permute-start.1 = (f32[16,896]{1,0:T(8,128)S(1)}, f32[16,896]{1,0:T(8,128)S(1)}, u32[]{:S(2)}, u32[]{:S(2)}) collective-permute-start(f32[16,896]{1,0:T(8,128)S(1)} %get-tuple-element.40), channel_id=1, source_target_pairs={{0,3},{1,2},{2,1},{3,0},{4,7},{5,6},{6,5},{7,4},{8,11},{9,10},{10,... | collective-permute-start | bytes 172040 | tf_op jit(solution)/shard_map/ppermute | solution.py:846
  14.5 6.6 %collective-permute-start.2 = (f32[16,896]{1,0:T(8,128)S(1)}, f32[16,896]{1,0:T(8,128)S(1)}, u32[]{:S(2)}, u32[]{:S(2)}) collective-permute-start(f32[16,896]{1,0:T(8,128)S(1)} %get-tuple-element.46), channel_id=1, source_target_pairs={{0,4},{4,0},{8,12},{12,8},{16,20},{20,16},{24,28},{28,24},{1,5},{5... | collective-permute-start | bytes 172040 | tf_op jit(solution)/shard_map/ppermute | solution.py:847
  16.0 6.9 %collective-permute-start.3 = (f32[16,896]{1,0:T(8,128)S(1)}, f32[16,896]{1,0:T(8,128)S(1)}, u32[]{:S(2)}, u32[]{:S(2)}) collective-permute-start(f32[16,896]{1,0:T(8,128)S(1)} %get-tuple-element.47), channel_id=1, source_target_pairs={{0,28},{4,8},{8,4},{12,16},{16,12},{20,24},{24,20},{28,0},{1,29},{... | collective-permute-start | bytes 172040 | tf_op jit(solution)/shard_map/ppermute | solution.py:846
  25.4 2.3 %collective-permute-start.7 = (f32[24,321]{1,0:T(8,128)S(1)}, f32[24,321]{1,0:T(8,128)S(1)}, u32[]{:S(2)}, u32[]{:S(2)}) collective-permute-start(f32[24,321]{1,0:T(8,128)S(1)} %get-tuple-element.58), channel_id=1, source_target_pairs={{0,1},{1,0},{2,3},{3,2},{4,5},{5,4},{6,7},{7,6},{8,9},{9,8},{10,11... | collective-permute-start | bytes 92456 | tf_op jit(solution)/shard_map/ppermute | solution.py:847
  25.5 3.4 %collective-permute-start.8 = (f32[24,321]{1,0:T(8,128)S(1)}, f32[24,321]{1,0:T(8,128)S(1)}, u32[]{:S(2)}, u32[]{:S(2)}) collective-permute-start(f32[24,321]{1,0:T(8,128)S(1)} %get-tuple-element.59), channel_id=1, source_target_pairs={{0,3},{1,2},{2,1},{3,0},{4,7},{5,6},{6,5},{7,4},{8,11},{9,10},{10,... | collective-permute-start | bytes 92456 | tf_op jit(solution)/shard_map/ppermute | solution.py:846
  27.6 8.7 %copy-start.1 = (bf16[16,32,320]{2,1,0:T(8,128)(2,1)S(1)}, bf16[16,32,320]{2,1,0:T(8,128)(2,1)}, u32[]{:S(2)}) copy-start(bf16[16,32,320]{2,1,0:T(8,128)(2,1)} %param.11) | copy-start | bytes 983044
  28.9 9.7 %collective-permute-start.10 = (f32[16,320]{1,0:T(8,128)S(1)}, f32[16,320]{1,0:T(8,128)S(1)}, u32[]{:S(2)}, u32[]{:S(2)}) collective-permute-start(f32[16,320]{1,0:T(8,128)S(1)} %get-tuple-element.63.mine_a), channel_id=1, source_target_pairs={{0,4},{4,0},{8,12},{12,8},{16,20},{20,16},{24,28},{28,24},{1,5},{5... | collective-permute-start | bytes 61448 | tf_op jit(solution)/shard_map/ppermute | solution.py:847
  29.0 9.7 %collective-permute-start.11 = (f32[16,320]{1,0:T(8,128)S(1)}, f32[16,320]{1,0:T(8,128)S(1)}, u32[]{:S(2)}, u32[]{:S(2)}) collective-permute-start(f32[16,320]{1,0:T(8,128)S(1)} %get-tuple-element.64.mine_b), channel_id=1, source_target_pairs={{0,28},{4,8},{8,4},{12,16},{16,12},{20,24},{24,20},{28,0},{1,29},{... | collective-permute-start | bytes 61448 | tf_op jit(solution)/shard_map/ppermute | solution.py:846
  32.6 3.7 %collective-permute-start.9 = (f32[8,321]{1,0:T(8,128)S(1)}, f32[8,321]{1,0:T(8,128)S(1)}, u32[]{:S(2)}, u32[]{:S(2)}) collective-permute-start(f32[8,321]{1,0:T(8,128)S(1)} %slice.10), channel_id=1, source_target_pairs={{0,2},{1,3},{2,0},{3,1},{4,6},{5,7},{6,4},{7,5},{8,10},{9,11},{10,... | collective-permute-start | bytes 30824 | tf_op jit(solution)/shard_map/ppermute | solution.py:946

commit v4 on v3

--- a/solution.py
+++ b/solution.py
@@ -162,7 +162,7 @@
 
 
 def local_update(base_ref, field_ref, products, wind_ref, out_ref, size_y, levels,
-                 mixed_ref=None, change_ref=None):
+                 mixed_ref=None):
     channels = out_ref.shape[1]
     strip = NODES * size_y
     table = sublane_coefficients(2 * levels)
@@ -191,8 +191,6 @@
                     + mixed[i * size_y : (i + 1) * size_y, begin:end]
                     - (wind_x * along[i] + wind_y * across[i])
                 )
-                if change_ref is not None:
-                    result = result + change_ref[pl.ds(element * size_y, size_y), begin:end]
                 out_ref[rows[i], begin:end] = sub_average(result)
 
 
@@ -668,23 +666,15 @@
             value = term if value is None else value + term
         reduced[pl.ds(element * size_y, size_y), :] = weight * value
     forcing[...] = select_rows(gather[...], reduced[...])
-    ends = [
-        [column_of(total, near + j, size_x, size_y) for j in range(NODES)]
-        for near in (0, size_y - NODES)
-    ]
-    remixed = mix_all(jnp.concatenate([ends[0][0], ends[1][3]], axis=0), mix[...])
-    for side, (y, kind) in enumerate(((0, 0), (size_y - 1, 3))):
+    for side, (y, near, kind) in enumerate(((0, 0, 0), (size_y - 1, size_y - NODES, 3))):
+        values = [column_of(total, near + j, size_x, size_y) for j in range(NODES)]
         slope = None
         for j in range(NODES):
-            term = DERIV[kind][j] * ends[side][j]
+            term = DERIV[kind][j] * values[j]
             slope = term if slope is None else slope + term
         along_x, along_y = full_winds(column_of(wind, y, size_x, size_y), levels, channels)
-        column = ends[side][kind]
-        work[side] = (
-            column
-            + remixed[side * size_x : (side + 1) * size_x]
-            - (along_x * dsub(column, small) + along_y * slope)
-        )
+        work[side, 0] = values[kind]
+        work[side, 1] = along_x * dsub(values[kind], small) + along_y * slope
 
 
 def home_kernel(size_x, size_y, groups, capacity, *refs):
@@ -703,23 +693,25 @@
     )
     own_final[...] = cloud[0:rows, :]
     tend = tendency[...]
-    change = COUPLING * (tend + mix_all(tend, mix[...]))
-    out[...] = select_rows(spread[...], change)
+    out[...] = select_rows(spread[...], COUPLING * tend)
     occupied = jnp.max(gather[...].astype(jnp.float32), axis=1, keepdims=True)
     sends[:, 0:channels] = forcing[...]
     sends[:, channels : channels + 1] = occupied
+    coupled = []
     for side, y in ((0, 0), (1, size_y - 1)):
-        own_change = jnp.concatenate(
-            [
-                jnp.broadcast_to(
-                    out[(x // NODES) * size_y + y : (x // NODES) * size_y + y + 1, :],
-                    (NODES, channels),
-                )
-                for x in range(0, size_x, NODES)
-            ],
-            axis=0,
-        )
-        message[side] = sub_average(edges[side] + own_change)
+        half = [
+            jnp.broadcast_to(
+                out[(x // NODES) * size_y + y : (x // NODES) * size_y + y + 1, :],
+                (NODES, channels),
+            )
+            for x in range(0, size_x, NODES)
+        ]
+        coupled.append(edges[side, 0] + jnp.concatenate(half, axis=0))
+    mixed = mix_all(jnp.concatenate(coupled, axis=0), mix[...])
+    for side in range(2):
+        message[side] = sub_average(
+            coupled[side] + mixed[side * size_x : (side + 1) * size_x] - edges[side, 1]
+        )
     even = is_even(rank)
     to_a[0:size_x, 0:channels] = jnp.where(even, message[1], message[0])
     to_b[0:size_x, 0:channels] = jnp.where(even, message[0], message[1])
@@ -727,9 +719,12 @@
     to_b[size_x : size_x + 8, :] = sends[8 * groups - 8 : 8 * groups, :]
 
 
-def fields_kernel(size_x, size_y, levels, second, wind, mix, slopes, change, out):
-    products = strip_products(second, mix[...], slopes, size_x, size_y)
-    local_update(second, second, products, wind, out, size_y, levels, None, change)
+def fields_kernel(size_x, size_y, levels, second, wind, mix, slopes, half, out, coupled):
+    for x in range(size_x):
+        row = pl.ds(x * size_y, size_y)
+        coupled[row, :] = second[row, :] + half[pl.ds(x // NODES * size_y, size_y), :]
+    products = strip_products(coupled, mix[...], slopes, size_x, size_y)
+    local_update(coupled, coupled, products, wind, out, size_y, levels)
     average_rows(out, size_x, size_y)
 
 
@@ -916,13 +911,13 @@
     )
     second, edges, forcing = call(
         functools.partial(second_kernel, size_x, size_y, levels),
-        [grid, ((2, size_x, channels), f32), ((8 * groups, channels), f32)],
+        [grid, ((2, 2, size_x, channels), f32), ((8 * groups, channels), f32)],
         [((elements * size_y, channels), f32)],
         place, field, total, known, sides, gather, wind, dyn_mix, row_a, row_b,
         smem=(0,), aliases={2: 0},
     )
     edge = ((size_x + 8, channels + 1), f32)
-    change, to_a, to_b, sends, own_final = call(
+    half, to_a, to_b, sends, own_final = call(
         functools.partial(home_kernel, size_x, size_y, groups, capacity),
         [((elements * size_y, channels), f32), edge, edge, ((8 * groups, channels + 1), f32), ((rows, channels), f32)],
         [
@@ -947,8 +942,8 @@
     (partial,) = call(
         functools.partial(fields_kernel, size_x, size_y, levels),
         [grid],
-        [],
-        second, wind, dyn_mix, slopes, change,
+        [grid],
+        second, wind, dyn_mix, slopes, half,
     )
     mine_a, mine_b = call(
         functools.partial(last_turn_kernel, size_x, size_y),

time: 39.5 us -> 39.6 us (level)
  no operation moved by 1% of the time
where the time goes in v4:
time: 39.6 us; the launch traced here: 39.4 us
  starting transfers between devices  17.1 us (43%)
  waiting for transfers between devices  10.6 us (27%)
  Pallas kernels  9.86 us (25%)
  local copies, waits for them, and re-layouts  1 us (3%)
  between operations  0.78 us (2%)
    ppermute x4, starting transfers between devices, ring(): from_b = lax.ppermute(to_b, axis, upper_pairs(count))  10.5 us
    pallas_call x10, Pallas kernels, call(): pl.pallas_call(kernel, out_shape=[jax.ShapeDtypeStruct(shape, dtype) for...  9.86 us
    ppermute x4, waiting for transfers between devices, ring(): from_b = lax.ppermute(to_b, axis, upper_pairs(count))  8.42 us
    ppermute x3, starting transfers between devices, on_device(): lax.ppermute(wide[k - 1], 'crm', xor[k])  3.18 us
    ppermute x1, waiting for transfers between devices, on_device(): forcings.append(lax.ppermute(sends[8 * k:8 * k + 8], 'crm', xor[k]))  2.17 us
    ppermute x4, starting transfers between devices, ring(): from_a = lax.ppermute(to_a, axis, lower_pairs(count))  1.86 us
    ppermute x1, starting transfers between devices, on_device(): forcings.append(lax.ppermute(sends[8 * k:8 * k + 8], 'crm', xor[k]))  1.52 us
    unnamed x4, local copies, waits for them, and re-layouts  1 us
  transfers between devices with their start and end apart: 12, of which 4 were waited for; matrix products, arithmetic and copies ran while one was open for 0% of the time, Pallas kernels for 18%

profile of v4, /device:TPU:0, one launch (start us, length us, event | category | flops | bytes accessed | tf_op | source)
XLA Modules:
  0.0 39.4 jit_solution(3997110164497851739)
XLA Ops:
  0.6 0.0 copy-start
  0.6 1.0 %copy-done = bf16[16,32,320]{2,1,0:T(8,128)(2,1)S(1)} copy-done((bf16[16,32,320]{2,1,0:T(8,128)(2,1)S(1)}, bf16[16,32,320]{2,1,0:T(8,128)(2,1)}, u32[]{:S(2)}) %copy-start) | copy-done | bytes 327704
  1.6 0.3 shard_map.90
  1.9 0.6 %collective-permute-start.4 = (f32[320,128]{1,0:T(8,128)S(1)}, f32[320,128]{1,0:T(8,128)S(1)}, u32[]{:S(2)}, u32[]{:S(2)}) collective-permute-start(f32[320,128]{1,0:T(8,128)S(1)} %get-tuple-element.54.refs_8_), channel_id=1, source_target_pairs={{0,1},{1,0},{2,3},{3,2},{4,5},{5,4},{6,7},{7,6},{8,9},{9,8},{10,11... | collective-permute-start | bytes 491528 | tf_op jit(solution)/shard_map/ppermute | solution.py:888
  2.5 2.6 %collective-permute-start.5 = (f32[320,128]{1,0:T(8,128)S(1)}, f32[320,128]{1,0:T(8,128)S(1)}, u32[]{:S(2)}, u32[]{:S(2)}) collective-permute-start(f32[320,128]{1,0:T(8,128)S(1)} %get-tuple-element.55.refs_9_), channel_id=1, source_target_pairs={{0,2},{1,3},{2,0},{3,1},{4,6},{5,7},{6,4},{7,5},{8,10},{9,11},{10,... | collective-permute-start | bytes 491528 | tf_op jit(solution)/shard_map/ppermute | solution.py:888
  5.1 0.0 collective-permute-start.6
  5.1 1.9 %shard_map.86 = (f32[256,320]{1,0:T(8,128)S(1)}, f32[16,896]{1,0:T(8,128)S(1)}, f32[16,896]{1,0:T(8,128)S(1)}, f32[256,320]{1,0:T(8,128)S(1)}, f32[256,128]{1,0:...) custom-call(s32[1]{0:T(128)} %bitcast.1.rank.refs_0_, f32[256,320]{1,0:T(8,128)} %bitcast.10, ...), custom_call_target="tpu_custom_call" | custom-call | tf_op jit(solution)/shard_map/pallas_call | solution.py:818
  7.0 0.2 collective-permute-start
  7.2 1.7 %collective-permute-start.1 = (f32[16,896]{1,0:T(8,128)S(1)}, f32[16,896]{1,0:T(8,128)S(1)}, u32[]{:S(2)}, u32[]{:S(2)}) collective-permute-start(f32[16,896]{1,0:T(8,128)S(1)} %get-tuple-element.40), channel_id=1, source_target_pairs={{0,3},{1,2},{2,1},{3,0},{4,7},{5,6},{6,5},{7,4},{8,11},{9,10},{10,... | collective-permute-start | bytes 172040 | tf_op jit(solution)/shard_map/ppermute | solution.py:841
  8.9 0.0 collective-permute-done.from_a
  8.9 5.4 %collective-permute-done.1.from_b = f32[16,896]{1,0:T(8,128)S(1)} collective-permute-done((f32[16,896]{1,0:T(8,128)S(1)}, f32[16,896]{1,0:T(8,128)S(1)}, u32[]{:S(2)}, u32[]{:S(2)}) %collective-permute-start.1) | collective-permute-done | bytes 57376 | tf_op jit(solution)/shard_map/ppermute | solution.py:841
  14.3 0.2 shard_map.88
  14.5 1.5 %collective-permute-start.2 = (f32[16,896]{1,0:T(8,128)S(1)}, f32[16,896]{1,0:T(8,128)S(1)}, u32[]{:S(2)}, u32[]{:S(2)}) collective-permute-start(f32[16,896]{1,0:T(8,128)S(1)} %get-tuple-element.46), channel_id=1, source_target_pairs={{0,4},{4,0},{8,12},{12,8},{16,20},{20,16},{24,28},{28,24},{1,5},{5... | collective-permute-start | bytes 172040 | tf_op jit(solution)/shard_map/ppermute | solution.py:842
  16.0 3.6 %collective-permute-start.3 = (f32[16,896]{1,0:T(8,128)S(1)}, f32[16,896]{1,0:T(8,128)S(1)}, u32[]{:S(2)}, u32[]{:S(2)}) collective-permute-start(f32[16,896]{1,0:T(8,128)S(1)} %get-tuple-element.47), channel_id=1, source_target_pairs={{0,28},{4,8},{8,4},{12,16},{16,12},{20,24},{24,20},{28,0},{1,29},{... | collective-permute-start | bytes 172040 | tf_op jit(solution)/shard_map/ppermute | solution.py:841
  19.6 1.6 %shard_map.87 = (f32[256,320]{1,0:T(8,128)S(1)}, f32[256,320]{1,0:T(8,128)S(1)}, f32[256,320]{1,0:T(8,128)S(1)}, f32[2,4,16,320]{3,2,1,0:T(8,128)S(1)}, bf16[32,...) custom-call(s32[1]{0:T(128)} %bitcast.1.rank.refs_0_, s32[16]{0:T(128)} %bitcast.13, ...), custom_call_target="tpu_custom_call" | custom-call | tf_op jit(solution)/shard_map/pallas_call | solution.py:818
  21.2 1.7 %collective-permute-done.3.from_b = f32[16,896]{1,0:T(8,128)S(1)} collective-permute-done((f32[16,896]{1,0:T(8,128)S(1)}, f32[16,896]{1,0:T(8,128)S(1)}, u32[]{:S(2)}, u32[]{:S(2)}) %collective-permute-start.3) | collective-permute-done | bytes 57376 | tf_op jit(solution)/shard_map/ppermute | solution.py:841
  22.9 0.8 %shard_map.89 = (f32[256,320]{1,0:T(8,128)S(1)}, f32[2,2,16,320]{3,2,1,0:T(8,128)S(1)}, f32[32,320]{1,0:T(8,128)S(1)}) custom-call(s32[1]{0:T(128)} %bitcast.place, f32[256,320]{1,0:T(8,128)S(1)} %get-tuple-element.41.field, f32[256,320]{1,0:T(8,128)S(1)} %get-tuple-element.42.total_in, ...), custom_call_target="tpu_custom_call", output_to_operand_aliasing={{0}: (2, {})} | custom-call | tf_op jit(solution)/shard_map/pallas_call | solution.py:818
  23.7 0.0 collective-permute-done.4.refs_8_
  23.7 0.0 collective-permute-done.6.refs_10_
  23.7 1.6 %shard_map.91 = (f32[64,320]{1,0:T(8,128)S(1)}, f32[24,321]{1,0:T(8,128)S(1)}, f32[24,321]{1,0:T(8,128)S(1)}, f32[32,321]{1,0:T(8,128)S(1)}, f32[128,320]{1,0:T(8,128)S(1)}) custom-call(s32[1]{0:T(128)} %bitcast.1.rank.refs_0_, f32[2,2,16,320]{3,2,1,0:T(8,128)S(1)} %get-tuple-element.49.refs_1_, f32[32,320]{1,0:T(8,128)S(1)} %get-tuple-element.50.refs_2_, ...), custom_call_target="tpu_custom_call" | custom-call | tf_op jit(solution)/shard_map/pallas_call | solution.py:818
  25.4 0.1 collective-permute-start.7
  25.5 1.6 %collective-permute-start.8 = (f32[24,321]{1,0:T(8,128)S(1)}, f32[24,321]{1,0:T(8,128)S(1)}, u32[]{:S(2)}, u32[]{:S(2)}) collective-permute-start(f32[24,321]{1,0:T(8,128)S(1)} %get-tuple-element.59), channel_id=1, source_target_pairs={{0,3},{1,2},{2,1},{3,0},{4,7},{5,6},{6,5},{7,4},{8,11},{9,10},{10,... | collective-permute-start | bytes 92456 | tf_op jit(solution)/shard_map/ppermute | solution.py:841
  27.1 0.5 %shard_map.92.refs_1_.partial = f32[256,320]{1,0:T(8,128)S(1)} custom-call(f32[256,320]{1,0:T(8,128)S(1)} %get-tuple-element.48.second, f32[256,128]{1,0:T(8,128)S(1)} %get-tuple-element.36.wind, bf16[320,320]{1,0:T(8,128)(2,1)S(1)} %get-tuple-element.37.mix.refs_5_, bf16[128,192]{1,0:T(8,128)(2,1)S(1)} %get-tuple-element.38.slopes, ...), custom_call_target="tpu_custom_call" | custom-call | tf_op jit(solution)/shard_map/pallas_call | solution.py:818
  27.6 0.0 copy-start.1
  27.7 0.0 collective-permute-done.7.refs_2_.from_a
  27.7 1.3 %collective-permute-done.8.refs_3_.from_b = f32[24,321]{1,0:T(8,128)S(1)} collective-permute-done((f32[24,321]{1,0:T(8,128)S(1)}, f32[24,321]{1,0:T(8,128)S(1)}, u32[]{:S(2)}, u32[]{:S(2)}) %collective-permute-start.8) | collective-permute-done | bytes 30848 | tf_op jit(solution)/shard_map/ppermute | solution.py:841
  29.0 0.1 collective-permute-start.10
  29.0 3.6 %collective-permute-start.11 = (f32[16,320]{1,0:T(8,128)S(1)}, f32[16,320]{1,0:T(8,128)S(1)}, u32[]{:S(2)}, u32[]{:S(2)}) collective-permute-start(f32[16,320]{1,0:T(8,128)S(1)} %get-tuple-element.64.mine_b), channel_id=1, source_target_pairs={{0,28},{4,8},{8,4},{12,16},{16,12},{20,24},{24,20},{28,0},{1,29},{... | collective-permute-start | bytes 61448 | tf_op jit(solution)/shard_map/ppermute | solution.py:841
  32.7 1.5 %collective-permute-start.9 = (f32[8,321]{1,0:T(8,128)S(1)}, f32[8,321]{1,0:T(8,128)S(1)}, u32[]{:S(2)}, u32[]{:S(2)}) collective-permute-start(f32[8,321]{1,0:T(8,128)S(1)} %slice.10), channel_id=1, source_target_pairs={{0,2},{1,3},{2,0},{3,1},{4,6},{5,7},{6,4},{7,5},{8,10},{9,11},{10,... | collective-permute-start | bytes 30824 | tf_op jit(solution)/shard_map/ppermute | solution.py:941
  34.2 2.2 %collective-permute-done.9.refs_12_ = f32[8,321]{1,0:T(8,128)S(1)} collective-permute-done((f32[8,321]{1,0:T(8,128)S(1)}, f32[8,321]{1,0:T(8,128)S(1)}, u32[]{:S(2)}, u32[]{:S(2)}) %collective-permute-start.9) | collective-permute-done | bytes 10304 | tf_op jit(solution)/shard_map/ppermute | solution.py:941
  36.4 2.3 %shard_map.93 = (f32[256,320]{1,0:T(8,128)}, bf16[512,320]{1,0:T(8,128)(2,1)}) custom-call(s32[1]{0:T(128)} %bitcast.1.rank.refs_0_, f32[256,320]{1,0:T(8,128)S(1)} %shard_map.92.refs_1_.partial, f32[24,321]{1,0:T(8,128)S(1)} %collective-permute-done.7.refs_2_.from_a, f32[24,321]{1,0:T(8,128)S(1)} %collective-permute-done.8.refs_3_.from_b, ...), custom_call_target="tpu_custom_call" | custom-call | tf_op jit(solution)/shard_map/pallas_call | solution.py:818
  38.7 0.6 %shard_map.95 = f32[256,320]{1,0:T(8,128)} custom-call(s32[1]{0:T(128)} %bitcast.place, f32[256,320]{1,0:T(8,128)} %get-tuple-element.62.fields_in, f32[16,320]{1,0:T(8,128)S(1)} %get-tuple-element.63.mine_a, f32[16,320]{1,0:T(8,128)S(1)} %get-tuple-element.64.mine_b, f32[16,320]{1,0:T(8,128)S(1)} %collective-permute-done.10.from_a, ...), custom_call_target="tpu_custom_call", output_to_operand_aliasing={{}: (1, {})} | custom-call | tf_op jit(solution)/shard_map/pallas_call | solution.py:818
  (9 shorter events, 0.0 us)
Async XLA Ops:
  0.6 1.0 %copy-start = (bf16[16,32,320]{2,1,0:T(8,128)(2,1)S(1)}, bf16[16,32,320]{2,1,0:T(8,128)(2,1)}, u32[]{:S(2)}) copy-start(bf16[16,32,320]{2,1,0:T(8,128)(2,1)} %param.11) | copy-start | bytes 983044
  1.9 21.8 %collective-permute-start.4 = (f32[320,128]{1,0:T(8,128)S(1)}, f32[320,128]{1,0:T(8,128)S(1)}, u32[]{:S(2)}, u32[]{:S(2)}) collective-permute-start(f32[320,128]{1,0:T(8,128)S(1)} %get-tuple-element.54.refs_8_), channel_id=1, source_target_pairs={{0,1},{1,0},{2,3},{3,2},{4,5},{5,4},{6,7},{7,6},{8,9},{9,8},{10,11... | collective-permute-start | bytes 491528 | tf_op jit(solution)/shard_map/ppermute | solution.py:888
  2.5 21.2 %collective-permute-start.5 = (f32[320,128]{1,0:T(8,128)S(1)}, f32[320,128]{1,0:T(8,128)S(1)}, u32[]{:S(2)}, u32[]{:S(2)}) collective-permute-start(f32[320,128]{1,0:T(8,128)S(1)} %get-tuple-element.55.refs_9_), channel_id=1, source_target_pairs={{0,2},{1,3},{2,0},{3,1},{4,6},{5,7},{6,4},{7,5},{8,10},{9,11},{10,... | collective-permute-start | bytes 491528 | tf_op jit(solution)/shard_map/ppermute | solution.py:888
  5.1 18.7 %collective-permute-start.6 = (f32[320,128]{1,0:T(8,128)S(1)}, f32[320,128]{1,0:T(8,128)S(1)}, u32[]{:S(2)}, u32[]{:S(2)}) collective-permute-start(f32[320,128]{1,0:T(8,128)S(1)} %get-tuple-element.56.refs_10_), channel_id=1, source_target_pairs={{0,3},{1,2},{2,1},{3,0},{4,7},{5,6},{6,5},{7,4},{8,11},{9,10},{10,... | collective-permute-start | bytes 491528 | tf_op jit(solution)/shard_map/ppermute | solution.py:888
  7.0 1.9 %collective-permute-start = (f32[16,896]{1,0:T(8,128)S(1)}, f32[16,896]{1,0:T(8,128)S(1)}, u32[]{:S(2)}, u32[]{:S(2)}) collective-permute-start(f32[16,896]{1,0:T(8,128)S(1)} %get-tuple-element.39), channel_id=1, source_target_pairs={{0,1},{1,0},{2,3},{3,2},{4,5},{5,4},{6,7},{7,6},{8,9},{9,8},{10,11... | collective-permute-start | bytes 172040 | tf_op jit(solution)/shard_map/ppermute | solution.py:842
  7.2 7.1 %collective-permute-start.1 = (f32[16,896]{1,0:T(8,128)S(1)}, f32[16,896]{1,0:T(8,128)S(1)}, u32[]{:S(2)}, u32[]{:S(2)}) collective-permute-start(f32[16,896]{1,0:T(8,128)S(1)} %get-tuple-element.40), channel_id=1, source_target_pairs={{0,3},{1,2},{2,1},{3,0},{4,7},{5,6},{6,5},{7,4},{8,11},{9,10},{10,... | collective-permute-start | bytes 172040 | tf_op jit(solution)/shard_map/ppermute | solution.py:841
  14.5 6.6 %collective-permute-start.2 = (f32[16,896]{1,0:T(8,128)S(1)}, f32[16,896]{1,0:T(8,128)S(1)}, u32[]{:S(2)}, u32[]{:S(2)}) collective-permute-start(f32[16,896]{1,0:T(8,128)S(1)} %get-tuple-element.46), channel_id=1, source_target_pairs={{0,4},{4,0},{8,12},{12,8},{16,20},{20,16},{24,28},{28,24},{1,5},{5... | collective-permute-start | bytes 172040 | tf_op jit(solution)/shard_map/ppermute | solution.py:842
  16.0 6.9 %collective-permute-start.3 = (f32[16,896]{1,0:T(8,128)S(1)}, f32[16,896]{1,0:T(8,128)S(1)}, u32[]{:S(2)}, u32[]{:S(2)}) collective-permute-start(f32[16,896]{1,0:T(8,128)S(1)} %get-tuple-element.47), channel_id=1, source_target_pairs={{0,28},{4,8},{8,4},{12,16},{16,12},{20,24},{24,20},{28,0},{1,29},{... | collective-permute-start | bytes 172040 | tf_op jit(solution)/shard_map/ppermute | solution.py:841
  25.4 2.3 %collective-permute-start.7 = (f32[24,321]{1,0:T(8,128)S(1)}, f32[24,321]{1,0:T(8,128)S(1)}, u32[]{:S(2)}, u32[]{:S(2)}) collective-permute-start(f32[24,321]{1,0:T(8,128)S(1)} %get-tuple-element.58), channel_id=1, source_target_pairs={{0,1},{1,0},{2,3},{3,2},{4,5},{5,4},{6,7},{7,6},{8,9},{9,8},{10,11... | collective-permute-start | bytes 92456 | tf_op jit(solution)/shard_map/ppermute | solution.py:842
  25.5 3.4 %collective-permute-start.8 = (f32[24,321]{1,0:T(8,128)S(1)}, f32[24,321]{1,0:T(8,128)S(1)}, u32[]{:S(2)}, u32[]{:S(2)}) collective-permute-start(f32[24,321]{1,0:T(8,128)S(1)} %get-tuple-element.59), channel_id=1, source_target_pairs={{0,3},{1,2},{2,1},{3,0},{4,7},{5,6},{6,5},{7,4},{8,11},{9,10},{10,... | collective-permute-start | bytes 92456 | tf_op jit(solution)/shard_map/ppermute | solution.py:841
  27.6 8.7 %copy-start.1 = (bf16[16,32,320]{2,1,0:T(8,128)(2,1)S(1)}, bf16[16,32,320]{2,1,0:T(8,128)(2,1)}, u32[]{:S(2)}) copy-start(bf16[16,32,320]{2,1,0:T(8,128)(2,1)} %param.11) | copy-start | bytes 983044
  29.0 9.7 %collective-permute-start.10 = (f32[16,320]{1,0:T(8,128)S(1)}, f32[16,320]{1,0:T(8,128)S(1)}, u32[]{:S(2)}, u32[]{:S(2)}) collective-permute-start(f32[16,320]{1,0:T(8,128)S(1)} %get-tuple-element.63.mine_a), channel_id=1, source_target_pairs={{0,4},{4,0},{8,12},{12,8},{16,20},{20,16},{24,28},{28,24},{1,5},{5... | collective-permute-start | bytes 61448 | tf_op jit(solution)/shard_map/ppermute | solution.py:842
  29.0 9.7 %collective-permute-start.11 = (f32[16,320]{1,0:T(8,128)S(1)}, f32[16,320]{1,0:T(8,128)S(1)}, u32[]{:S(2)}, u32[]{:S(2)}) collective-permute-start(f32[16,320]{1,0:T(8,128)S(1)} %get-tuple-element.64.mine_b), channel_id=1, source_target_pairs={{0,28},{4,8},{8,4},{12,16},{16,12},{20,24},{24,20},{28,0},{1,29},{... | collective-permute-start | bytes 61448 | tf_op jit(solution)/shard_map/ppermute | solution.py:841
  32.7 3.7 %collective-permute-start.9 = (f32[8,321]{1,0:T(8,128)S(1)}, f32[8,321]{1,0:T(8,128)S(1)}, u32[]{:S(2)}, u32[]{:S(2)}) collective-permute-start(f32[8,321]{1,0:T(8,128)S(1)} %slice.10), channel_id=1, source_target_pairs={{0,2},{1,3},{2,0},{3,1},{4,6},{5,7},{6,4},{7,5},{8,10},{9,11},{10,... | collective-permute-start | bytes 30824 | tf_op jit(solution)/shard_map/ppermute | solution.py:941
